TPU v7x, 32 devices: a whole 2x2x4 slice. The times are simulated.
32 devices in a mesh: mem: 2 (over y), gx: 4 (over x, core), gy: 4 (over z).
Axes of the slice: x: 2, y: 2, z: 4, core: 2. Of those that a mesh axis runs over, the one named last changes fastest.
Arguments:
- background_samples: float32 [256, 128, 256], P('mem', 'gx', 'gy'), may hold values from -6 to 6
- measured_space_anomalies: float32 [256, 4, 4, 2048], P('mem', 'gx', 'gy'), may hold values from -32 to 32
- innovation_vector: float32 [4, 4, 2, 1024], P('gx', 'gy', 'mem'), may hold values from -6 to 6
- error_spread_squared: float32 [4, 4, 2, 1024], P('gx', 'gy', 'mem'), may hold values from 0.25 to 4
- measured_nearest_anchor: int32 [4, 4, 2, 1024], P('gx', 'gy', 'mem'), may hold values from 0 to 3
- active_measurement_tally: int32 [4, 4, 2], P('gx', 'gy', 'mem'), may hold values from 256 to 1024, as said below
Outputs:
- updated_sample_matrix: float32 [256, 128, 256], P('mem', 'gx', 'gy')
Inputs may be any that keep to these rules, and one draw needn't show every extreme that they name: `active_measurement_tally`: some band has all 1024 slots live and some band only 256.
All inputs are finite; a program needn't handle non-finite values.
Results may differ from a plain program's by a relative error of at most 0.0003.
Values sent between devices are 32-bit elements; how exact they have to be, the bound alone decides.
No kernel may reach another device: no remote copies, remote signals or barrier semaphores. Data moves between devices by JAX's collectives and lax.ppermute only.
A program may use at most 128 MiB of HBM per device.

v0:
```python
import functools

import jax
import jax.numpy as jnp
from jax import lax
from jax.experimental import pallas as pl
from jax.experimental.pallas import tpu as pltpu
from jax.sharding import PartitionSpec as P

CGX = 4
NS_STEPS = 12
GROUPS = ((0, 1, 2, 3),)

F32 = jnp.float32
BF16 = jnp.bfloat16
VMEM_LIMIT = 56 * 1024 * 1024
NT = (((1,), (1,)), ((), ()))


def dot(a, b):
    return jnp.dot(a, b, preferred_element_type=F32)


def dot_nt(a, b):
    return lax.dot_general(a, b, NT, preferred_element_type=F32)


def split2(x):
    high = x.astype(BF16)
    return high, (x - high.astype(F32)).astype(BF16)


def split3(x):
    high = x.astype(BF16)
    rest = x - high.astype(F32)
    mid = rest.astype(BF16)
    return high, mid, (rest - mid.astype(F32)).astype(BF16)


def mm3(a, b):
    return dot(
        jnp.concatenate([a[0], a[0], a[1]], axis=1),
        jnp.concatenate([b[0], b[1], b[0]], axis=0),
    )


def mm5(a, b):
    return dot(
        jnp.concatenate([a[0], a[1], a[2], a[0], a[1]], axis=1),
        jnp.concatenate([b[0], b[0], b[0], b[1], b[1]], axis=0),
    )


def quartic(p, identity):
    ps = split2(p)
    square = mm3(ps, ps)
    inner = 0.0625 * square - 0.5625 * p + 1.6875 * identity
    return mm3(split2(square), split2(inner)) + (2.25 * identity - 2.4375 * p)


def solve_kernel(points, bands, live_ref, own_ref, *refs):
    others = refs[: bands - 1]
    departure_ref, variance_ref, nearest_ref = refs[bands - 1 : bands + 2]
    outs = refs[bands + 2 : 2 * bands + 2]
    y_ref, cov_ref, right_ref, root_ref, inv_ref = refs[2 * bands + 2 :]
    me = lax.axis_index("mem")
    part, slots = own_ref.shape
    members = y_ref.shape[0]
    for shift, ref in enumerate((own_ref,) + tuple(others)):
        owner = lax.rem(me - shift + bands, bands)
        y_ref[pl.ds(pl.multiple_of(owner * part, part), part), :] = ref[...]
    rows = lax.broadcasted_iota(jnp.int32, (members, members), 0)
    columns = lax.broadcasted_iota(jnp.int32, (members, members), 1)
    identity = (rows == columns).astype(F32)
    live = (lax.broadcasted_iota(jnp.int32, (1, slots), 1) < live_ref[0]).astype(F32)
    base = live * lax.rsqrt(variance_ref[...])
    scales = []
    for g, point in enumerate(points):
        distance = (nearest_ref[...] - point).astype(F32)
        weight = jnp.exp(-0.25 * distance * distance) * base
        y0, y1, y2 = split3(y_ref[...] * weight)
        cross = dot_nt(y0, y1) + dot_nt(y0, y2)
        cov = dot_nt(y0, y0) + dot_nt(y1, y1) + (cross + cross.T)
        cov = cov + (members - 1.0) * identity
        d0, d1 = split2(jnp.broadcast_to(weight * departure_ref[...], (8, slots)))
        right = dot_nt(d0, y0) + dot_nt(d0, y1) + dot_nt(d1, y0)
        right_ref[g] = right
        square_sum = jnp.sum(jnp.sum(cov * cov, axis=1, keepdims=True), axis=0, keepdims=True)
        scale = lax.rsqrt(square_sum)
        scales.append(scale)
        root = cov * scale
        u = split2(quartic(root, identity))
        root_ref[g, 0], root_ref[g, 1], root_ref[g, 2] = split3(mm5(split3(root), u))
        inv_ref[g, 0], inv_ref[g, 1] = u

    def step(_, carry):
        for g in range(len(points)):
            root = (root_ref[g, 0], root_ref[g, 1], root_ref[g, 2])
            inv = (inv_ref[g, 0], inv_ref[g, 1])
            u = split2(quartic(mm3(inv, root), identity))
            root_ref[g, 0], root_ref[g, 1], root_ref[g, 2] = split3(mm5(root, u))
            inv_ref[g, 0], inv_ref[g, 1] = split2(mm3(u, inv))
        return carry

    lax.fori_loop(0, NS_STEPS // 2 - 2, step, 0)
    for g in range(len(points)):
        root = (root_ref[g, 0], root_ref[g, 1])
        inv = (inv_ref[g, 0], inv_ref[g, 1])
        u = split2(quartic(mm3(inv, root), identity))
        last = mm3(u, inv)
        right = right_ref[g, 0:1, :]
        half = jnp.sum(last * right, axis=1, keepdims=True)
        mean_weights = jnp.sum(last * half, axis=0, keepdims=True) * scales[g]
        cov_ref[...] = last * jnp.sqrt((members - 1.0) * scales[g]) + mean_weights
        for shift, out in enumerate(outs):
            target = lax.rem(me + shift, bands)
            out[g] = cov_ref[pl.ds(pl.multiple_of(target * part, part), part), :]


def solve(points, live, own, others, departure, variance, nearest):
    bands = 1 + len(others)
    part, slots = own.shape
    members = part * bands
    count = len(points)
    vmem = pl.BlockSpec(memory_space=pltpu.VMEM)
    return pl.pallas_call(
        functools.partial(solve_kernel, points, bands),
        out_shape=[jax.ShapeDtypeStruct((count, part, members), F32)] * bands,
        in_specs=[pl.BlockSpec(memory_space=pltpu.SMEM)] + [vmem] * (bands + 3),
        out_specs=[vmem] * bands,
        scratch_shapes=[
            pltpu.VMEM((members, slots), F32),
            pltpu.VMEM((members, members), F32),
            pltpu.VMEM((count, 8, members), F32),
            pltpu.VMEM((count, 3, members, members), BF16),
            pltpu.VMEM((count, 2, members, members), BF16),
        ],
        compiler_params=pltpu.CompilerParams(vmem_limit_bytes=VMEM_LIMIT),
        cost_estimate=pl.CostEstimate(
            flops=2 * count * members * members * (4 * slots + 91 * members),
            bytes_accessed=4 * members * (slots + count * members),
            transcendentals=0,
        ),
        name="solve",
    )(live, own, *others, departure, variance, nearest)


def update_kernel(groups, bands, tiles_y, blocks, *refs):
    refs = list(refs)

    def take(n):
        taken, refs[:n] = refs[:n], []
        return taken

    cells = take(blocks)
    rows = [take(bands) for _ in groups]
    ends = [take(bands) for _ in groups]
    row_sides = take(2)
    end_sides = take(2)
    (out,) = take(1)
    x_ref, mean_ref, t_ref = refs
    me = lax.axis_index("mem")
    tile_y = lax.axis_index("gy")
    width, height, _ = out.shape
    part = out.shape[2]
    members = x_ref.shape[3]
    spacing = width // CGX
    depth = height // bands

    def put(slot, column, value):
        t_ref[slot, column, 0], t_ref[slot, column, 1] = split2(value)

    for g, points in enumerate(groups):
        for i, point in enumerate(points):
            for shift in range(bands):
                band = lax.rem(me - shift + bands, bands)
                value = rows[g][shift][i]
                put(band + 1, point + 1, value)

                @pl.when((tile_y == 0) & (band == 0))
                def _(value=value, point=point):
                    put(0, point + 1, value)

                @pl.when((tile_y == tiles_y - 1) & (band == bands - 1))
                def _(value=value, point=point):
                    put(bands + 1, point + 1, value)

                @pl.when((tile_y > 0) & (me == (shift - 1) % bands))
                def _(g=g, i=i, shift=shift, point=point):
                    put(0, point + 1, ends[g][shift][i])

                @pl.when((tile_y < tiles_y - 1) & (me == shift))
                def _(g=g, i=i, shift=shift, point=point):
                    put(bands + 1, point + 1, ends[g][shift][i])

    for side, column in enumerate((0, CGX + 1)):
        for shift in range(bands):
            band = lax.rem(me - shift + bands, bands)
            value = row_sides[side][shift]
            put(band + 1, column, value)

            @pl.when((tile_y == 0) & (band == 0))
            def _(value=value, column=column):
                put(0, column, value)

            @pl.when((tile_y == tiles_y - 1) & (band == bands - 1))
            def _(value=value, column=column):
                put(bands + 1, column, value)

            @pl.when((tile_y > 0) & (me == (shift - 1) % bands))
            def _(side=side, shift=shift, column=column):
                put(0, column, end_sides[side][shift])

            @pl.when((tile_y < tiles_y - 1) & (me == shift))
            def _(side=side, shift=shift, column=column):
                put(bands + 1, column, end_sides[side][shift])

    strip = members // blocks
    total = sum(jnp.sum(ref[...], axis=2, keepdims=True) for ref in cells)
    mean = total * (1.0 / members)
    mean_ref[...] = jnp.broadcast_to(mean, mean_ref.shape)
    for shift, ref in enumerate(cells):
        x0, x1 = split2(ref[...] - mean)
        if blocks == 1:
            x_ref[0], x_ref[1] = x0, x1
        else:
            owner = lax.rem(me - shift + blocks, blocks)
            place = pl.ds(pl.multiple_of(owner * strip, strip), strip)
            x_ref[0, :, :, place] = x0
            x_ref[1, :, :, place] = x1

    for v in range(bands + 1):
        j0, j1 = max(depth * v - depth // 2, 0), min(depth * v + depth // 2, height)
        tall = j1 - j0
        j = lax.broadcasted_iota(jnp.int32, (1, tall, 1), 1).astype(F32) + (
            j0 + 0.5 - (v - 0.5) * depth
        )
        upper = j * (1.0 / depth)
        lower = 1.0 - upper
        for c in range(CGX + 1):
            i0 = max(spacing * c - spacing // 2, 0)
            i1 = min(spacing * c + spacing // 2, width)
            wide = i1 - i0
            x0 = x_ref[0, i0:i1, j0:j1, :].reshape(wide * tall, members)
            x1 = x_ref[1, i0:i1, j0:j1, :].reshape(wide * tall, members)
            left = jnp.concatenate([x0, x0, x1], axis=1)
            i = lax.broadcasted_iota(jnp.int32, (wide, 1, 1), 0).astype(F32) + (
                i0 + 0.5 - (c - 0.5) * spacing
            )
            right_weight = i * (1.0 / spacing)
            result = mean_ref[i0:i1, j0:j1, :part]
            for column, weight in ((c, 1.0 - right_weight), (c + 1, right_weight)):
                t0 = jnp.concatenate([t_ref[v, column, 0], t_ref[v + 1, column, 0]], axis=0)
                t1 = jnp.concatenate([t_ref[v, column, 1], t_ref[v + 1, column, 1]], axis=0)
                product = dot_nt(left, jnp.concatenate([t0, t1, t0], axis=1))
                product = product.reshape(wide, tall, 2 * part)
                result = result + weight * (
                    lower * product[:, :, :part] + upper * product[:, :, part:]
                )
            out[i0:i1, j0:j1, :] = result


def update(groups, tiles_y, cells, rows, ends, row_sides, end_sides, part):
    width, height, strip = cells[0].shape
    bands = len(rows[0])
    members = strip * len(cells)
    vmem = pl.BlockSpec(memory_space=pltpu.VMEM)
    operands = (
        list(cells)
        + [array for group in rows for array in group]
        + [array for group in ends for array in group]
        + list(row_sides)
        + list(end_sides)
    )
    return pl.pallas_call(
        functools.partial(update_kernel, groups, bands, tiles_y, len(cells)),
        out_shape=jax.ShapeDtypeStruct((width, height, part), F32),
        in_specs=[vmem] * len(operands),
        out_specs=vmem,
        scratch_shapes=[
            pltpu.VMEM((2, width, height, members), BF16),
            pltpu.VMEM((width, height, part), F32),
            pltpu.VMEM((bands + 2, CGX + 2, 2, part, members), BF16),
        ],
        compiler_params=pltpu.CompilerParams(vmem_limit_bytes=VMEM_LIMIT),
        cost_estimate=pl.CostEstimate(
            flops=24 * width * height * part * members,
            bytes_accessed=4 * width * height * (members + part),
            transcendentals=0,
        ),
        name="update",
    )(*operands)


def shifted(array, axis, by):
    size = lax.axis_size(axis)
    return lax.ppermute(array, axis, [(i, (i + by) % size) for i in range(size)])


def to_next_tile(array, shift):
    bands = lax.axis_size("mem")
    tiles = lax.axis_size("gy")
    last, first = (shift - 1) % bands, shift
    pairs = [(last * tiles + y, last * tiles + y + 1) for y in range(tiles - 1)]
    pairs += [(first * tiles + y, first * tiles + y - 1) for y in range(1, tiles)]
    return lax.ppermute(array, ("mem", "gy"), pairs)


def per_device(background, anomalies, departure, variance, nearest, tally):
    bands = lax.axis_size("mem")
    me = lax.axis_index("mem")
    part = background.shape[0]
    members = part * bands
    slots = departure.shape[3]
    anomalies = anomalies.reshape(part, bands * slots)
    own = lax.dynamic_slice_in_dim(anomalies, me * slots, slots, axis=1)
    others = []
    for shift in range(1, bands):
        piece = lax.dynamic_slice_in_dim(
            anomalies, lax.rem(me + shift, bands) * slots, slots, axis=1
        )
        others.append(shifted(piece, "mem", shift))
    tile = background.transpose(1, 2, 0)
    cells = [tile] + [shifted(tile, "mem", shift) for shift in range(1, bands)]
    if part % 128:
        order = lax.rem(me - jnp.arange(bands) + bands, bands)
        cells = jnp.take(jnp.stack(cells, axis=2), order, axis=2)
        cells = [cells.reshape(cells.shape[:2] + (members,))]
    rows, ends = [], []
    sides = [None] * CGX
    for points in GROUPS:
        solved = solve(
            points,
            tally.reshape(1),
            own,
            others,
            departure.reshape(1, slots),
            variance.reshape(1, slots),
            nearest.reshape(1, slots),
        )
        row = [solved[0]] + [shifted(solved[s], "mem", s) for s in range(1, bands)]
        end = [to_next_tile(row[s], s) for s in range(bands)]
        rows.append(row)
        ends.append(end)
        for i, point in enumerate(points):
            sides[point] = (
                jnp.stack([array[i] for array in row]),
                jnp.stack([array[i] for array in end]),
            )
    row_sides = [shifted(sides[CGX - 1][0], "gx", 1), shifted(sides[0][0], "gx", -1)]
    end_sides = [shifted(sides[CGX - 1][1], "gx", 1), shifted(sides[0][1], "gx", -1)]
    result = update(
        GROUPS, lax.axis_size("gy"), cells, rows, ends, row_sides, end_sides, part
    )
    return result.transpose(2, 0, 1)


def solution(mesh):
    in_specs = (
        P("mem", "gx", "gy"),
        P("mem", "gx", "gy", None),
        P("gx", "gy", "mem", None),
        P("gx", "gy", "mem", None),
        P("gx", "gy", "mem", None),
        P("gx", "gy", "mem"),
    )
    out_specs = P("mem", "gx", "gy")
    return jax.shard_map(
        per_device, mesh=mesh, in_specs=in_specs, out_specs=out_specs, check_vma=False
    )
```

profile of v0, /device:TPU:0, one launch (start us, length us, event | category | flops | bytes accessed | tf_op | source)
XLA Modules:
  0.0 100.7 jit_solution(4627364981901404759)
XLA Ops:
  0.0 1.9 %constant_dynamic-slice_fusion = (f32[128,1,1,1024]{3,2,1,0:T(1,128)S(1)}, f32[128,1,1,1024]{3,2,1,0:T(1,128)S(1)}) fusion(f32[128,1,1,2048]{3,2,1,0:T(1,128)} %param.7, s32[]{:T(128)S(6)} %select_n.7, s32[]{:T(128)S(6)} %select_n.6), kind=kLoop, calls=%fused_computation.6 | loop fusion | bytes 2097160 | tf_op jit(solution)/shard_map/dynamic_slice | solution.py:319
  1.9 0.1 copy.11
  2.0 3.1 %collective-permute-start.1 = (f32[128,1024]{1,0:T(8,128)S(1)}, f32[128,1024]{1,0:T(8,128)S(1)}, u32[]{:S(2)}, u32[]{:S(2)}) collective-permute-start(f32[128,1024]{1,0:T(8,128)S(1)} %bitcast.16), channel_id=1, source_target_pairs={{0,16},{16,0},{1,17},{17,1},{2,18},{18,2},{3,19},{19,3},{4,20},{20... | collective-permute-start | bytes 1572872 | tf_op jit(solution)/shard_map/ppermute | solution.py:297
  5.7 0.9 copy.12
  6.6 10.4 %collective-permute-done.1.refs_0_ = f32[128,1024]{1,0:T(8,128)S(1)} collective-permute-done((f32[128,1024]{1,0:T(8,128)S(1)}, f32[128,1024]{1,0:T(8,128)S(1)}, u32[]{:S(2)}, u32[]{:S(2)}) %collective-permute-start.1) | collective-permute-done | bytes 524320 | tf_op jit(solution)/shard_map/ppermute | solution.py:297
  17.0 0.8 copy-done.9
  17.8 36.9 %solve.1 = (f32[4,128,256]{2,1,0:T(8,128)}, f32[4,128,256]{2,1,0:T(8,128)}) custom-call(s32[1]{0:T(128)} %bitcast.12.live_ref, f32[128,1024]{1,0:T(8,128)} %bitcast.15, f32[128,1024]{1,0:T(8,128)} %copy-done.9, f32[1,1024]{1,0:T(1,128)} %bitcast.17, f32[1,1024]{1,0:T(1,128)} %bitcast.18, s32[1,1024]{1,0:T(1,128)} %bitcast.19), custom_call_target="tpu_custom_call" | custom-call | flops 14361296896 | bytes 2097152 | tf_op jit(solution)/shard_map/solve/pallas_call | solution.py:126
  54.8 1.7 %collective-permute-start.2 = (f32[4,128,256]{2,1,0:T(8,128)}, f32[4,128,256]{2,1,0:T(8,128)S(1)}, u32[]{:S(2)}, u32[]{:S(2)}) collective-permute-start(f32[4,128,256]{2,1,0:T(8,128)} %get-tuple-element.8), channel_id=1, source_target_pairs={{0,16},{16,0},{1,17},{17,1},{2,18},{18,2},{3,19},{19,3},{4,20},{20... | collective-permute-start | bytes 1572872 | tf_op jit(solution)/shard_map/ppermute | solution.py:297
  56.5 0.0 copy-done.3
  56.5 0.3 collective-permute-start
  56.8 1.3 %collective-permute-start.3 = (f32[4,128,256]{2,1,0:T(8,128)}, f32[4,128,256]{2,1,0:T(8,128)S(1)}, u32[]{:S(2)}, u32[]{:S(2)}) collective-permute-start(f32[4,128,256]{2,1,0:T(8,128)} %get-tuple-element.7.refs_2_), channel_id=1, source_target_pairs={{16,17},{17,18},{18,19},{1,0},{2,1},{3,2},{20,21},{21,22},{22,23},... | collective-permute-start | bytes 1572872 | tf_op jit(solution)/shard_map/ppermute | solution.py:306
  58.1 1.0 fusion.2
  59.1 10.7 %collective-permute-done.2.refs_3_ = f32[4,128,256]{2,1,0:T(8,128)S(1)} collective-permute-done((f32[4,128,256]{2,1,0:T(8,128)}, f32[4,128,256]{2,1,0:T(8,128)S(1)}, u32[]{:S(2)}, u32[]{:S(2)}) %collective-permute-start.2) | collective-permute-done | bytes 524320 | tf_op jit(solution)/shard_map/ppermute | solution.py:297
  69.8 3.7 %collective-permute-start.4 = (f32[4,128,256]{2,1,0:T(8,128)S(1)}, f32[4,128,256]{2,1,0:T(8,128)S(1)}, u32[]{:S(2)}, u32[]{:S(2)}) collective-permute-start(f32[4,128,256]{2,1,0:T(8,128)S(1)} %collective-permute-done.2.refs_3_), channel_id=1, source_target_pairs={{0,1},{1,2},{2,3},{17,16},{18,17},{19,18},{4,5},{5,6},{6,7},{21,20... | collective-permute-start | bytes 1572872 | tf_op jit(solution)/shard_map/ppermute | solution.py:306
  73.6 0.1 collective-permute-start.5
  73.7 1.8 %collective-permute-start.6 = (f32[2,128,256]{2,1,0:T(8,128)S(1)}, f32[2,128,256]{2,1,0:T(8,128)S(1)}, u32[]{:S(2)}, u32[]{:S(2)}) collective-permute-start(f32[2,128,256]{2,1,0:T(8,128)S(1)} %pad_maximum_fusion.1), channel_id=1, source_target_pairs={{0,12},{4,0},{8,4},{12,8},{1,13},{5,1},{9,5},{13,9},{2,14},{6,2},{... | collective-permute-start | bytes 786440 | tf_op jit(solution)/shard_map/ppermute | solution.py:297
  75.4 0.0 collective-permute-done.3.refs_4_
  75.5 5.5 %collective-permute-done.4.refs_5_ = f32[4,128,256]{2,1,0:T(8,128)S(1)} collective-permute-done((f32[4,128,256]{2,1,0:T(8,128)S(1)}, f32[4,128,256]{2,1,0:T(8,128)S(1)}, u32[]{:S(2)}, u32[]{:S(2)}) %collective-permute-start.4) | collective-permute-done | bytes 524320 | tf_op jit(solution)/shard_map/ppermute | solution.py:306
  81.0 0.7 copy-done.2
  81.7 0.0 collective-permute-start.7
  81.7 1.8 %collective-permute-start.8 = (f32[2,128,256]{2,1,0:T(8,128)S(1)}, f32[2,128,256]{2,1,0:T(8,128)S(1)}, u32[]{:S(2)}, u32[]{:S(2)}) collective-permute-start(f32[2,128,256]{2,1,0:T(8,128)S(1)} %pad_maximum_fusion.3), channel_id=1, source_target_pairs={{0,12},{4,0},{8,4},{12,8},{1,13},{5,1},{9,5},{13,9},{2,14},{6,2},{... | collective-permute-start | bytes 786440 | tf_op jit(solution)/shard_map/ppermute | solution.py:297
  83.5 7.0 %collective-permute-done.refs_1_ = f32[32,64,128]{2,1,0:T(8,128)S(1)} collective-permute-done((f32[32,64,128]{2,1,0:T(8,128)S(1)}, f32[32,64,128]{2,1,0:T(8,128)S(1)}, u32[]{:S(2)}, u32[]{:S(2)}) %collective-permute-start) | collective-permute-done | bytes 1048608 | tf_op jit(solution)/shard_map/ppermute | solution.py:297
  90.5 0.0 collective-permute-done.5.refs_6_
  90.5 0.0 collective-permute-done.6.refs_7_
  90.6 0.0 collective-permute-done.7.refs_8_
  90.6 0.0 collective-permute-done.8.refs_9_
  90.6 0.9 copy-done.4
  91.5 0.1 copy-done.5
  91.6 0.1 copy-done.6
  91.7 0.1 copy-done.7
  91.8 0.7 copy-done.8
  92.5 8.2 %update.1 = f32[32,64,128]{2,1,0:T(8,128)} custom-call(f32[32,64,128]{2,1,0:T(8,128)} %bitcast.13, f32[32,64,128]{2,1,0:T(8,128)} %copy-done.4, f32[4,128,256]{2,1,0:T(8,128)} %get-tuple-element.7.refs_2_, f32[4,128,256]{2,1,0:T(8,128)} %copy-done, f32[4,128,256]{2,1,0:T(8,128)} %copy-done.1, f32[4,128,256]{2,1,0:T(8,128)} %copy-done.2, ...), custom_call_target="tpu_custom_call" | custom-call | flops 1610612736 | bytes 3145728 | tf_op jit(solution)/shard_map/update/pallas_call | solution.py:275
  (19 shorter events, 0.2 us)
Async XLA Ops:
  2.0 15.0 %collective-permute-start.1 = (f32[128,1024]{1,0:T(8,128)S(1)}, f32[128,1024]{1,0:T(8,128)S(1)}, u32[]{:S(2)}, u32[]{:S(2)}) collective-permute-start(f32[128,1024]{1,0:T(8,128)S(1)} %bitcast.16), channel_id=1, source_target_pairs={{0,16},{16,0},{1,17},{17,1},{2,18},{18,2},{3,19},{19,3},{4,20},{20... | collective-permute-start | bytes 1572872 | tf_op jit(solution)/shard_map/ppermute | solution.py:297
  17.0 0.8 copy-start.9
  17.8 38.7 %copy-start.3 = (f32[128,32,64]{0,2,1:T(8,128)S(1)}, f32[128,32,64]{0,2,1:T(8,128)}, u32[]{:S(2)}) copy-start(f32[128,32,64]{0,2,1:T(8,128)} %param.6) | copy-start | bytes 3145732
  54.8 15.0 %collective-permute-start.2 = (f32[4,128,256]{2,1,0:T(8,128)}, f32[4,128,256]{2,1,0:T(8,128)S(1)}, u32[]{:S(2)}, u32[]{:S(2)}) collective-permute-start(f32[4,128,256]{2,1,0:T(8,128)} %get-tuple-element.8), channel_id=1, source_target_pairs={{0,16},{16,0},{1,17},{17,1},{2,18},{18,2},{3,19},{19,3},{4,20},{20... | collective-permute-start | bytes 1572872 | tf_op jit(solution)/shard_map/ppermute | solution.py:297
  56.5 34.0 %collective-permute-start = (f32[32,64,128]{2,1,0:T(8,128)S(1)}, f32[32,64,128]{2,1,0:T(8,128)S(1)}, u32[]{:S(2)}, u32[]{:S(2)}) collective-permute-start(f32[32,64,128]{2,1,0:T(8,128)S(1)} %bitcast.14), channel_id=1, source_target_pairs={{0,16},{16,0},{1,17},{17,1},{2,18},{18,2},{3,19},{19,3},{4,20},{20... | collective-permute-start | bytes 3145736 | tf_op jit(solution)/shard_map/ppermute | solution.py:297
  56.8 18.6 %collective-permute-start.3 = (f32[4,128,256]{2,1,0:T(8,128)}, f32[4,128,256]{2,1,0:T(8,128)S(1)}, u32[]{:S(2)}, u32[]{:S(2)}) collective-permute-start(f32[4,128,256]{2,1,0:T(8,128)} %get-tuple-element.7.refs_2_), channel_id=1, source_target_pairs={{16,17},{17,18},{18,19},{1,0},{2,1},{3,2},{20,21},{21,22},{22,23},... | collective-permute-start | bytes 1572872 | tf_op jit(solution)/shard_map/ppermute | solution.py:306
  69.8 3.8 %copy-start = (f32[4,128,256]{2,1,0:T(8,128)}, f32[4,128,256]{2,1,0:T(8,128)S(1)}, u32[]{:S(2)}) copy-start(f32[4,128,256]{2,1,0:T(8,128)S(1)} %collective-permute-done.2.refs_3_) | copy-start | bytes 1572868
  69.8 11.2 %collective-permute-start.4 = (f32[4,128,256]{2,1,0:T(8,128)S(1)}, f32[4,128,256]{2,1,0:T(8,128)S(1)}, u32[]{:S(2)}, u32[]{:S(2)}) collective-permute-start(f32[4,128,256]{2,1,0:T(8,128)S(1)} %collective-permute-done.2.refs_3_), channel_id=1, source_target_pairs={{0,1},{1,2},{2,3},{17,16},{18,17},{19,18},{4,5},{5,6},{6,7},{21,20... | collective-permute-start | bytes 1572872 | tf_op jit(solution)/shard_map/ppermute | solution.py:306
  73.6 17.0 %collective-permute-start.5 = (f32[2,128,256]{2,1,0:T(8,128)S(1)}, f32[2,128,256]{2,1,0:T(8,128)S(1)}, u32[]{:S(2)}, u32[]{:S(2)}) collective-permute-start(f32[2,128,256]{2,1,0:T(8,128)S(1)} %pad_maximum_fusion), channel_id=1, source_target_pairs={{0,4},{4,8},{8,12},{12,0},{1,5},{5,9},{9,13},{13,1},{2,6},{6,10},{... | collective-permute-start | bytes 786440 | tf_op jit(solution)/shard_map/ppermute | solution.py:297
  73.7 16.9 %collective-permute-start.6 = (f32[2,128,256]{2,1,0:T(8,128)S(1)}, f32[2,128,256]{2,1,0:T(8,128)S(1)}, u32[]{:S(2)}, u32[]{:S(2)}) collective-permute-start(f32[2,128,256]{2,1,0:T(8,128)S(1)} %pad_maximum_fusion.1), channel_id=1, source_target_pairs={{0,12},{4,0},{8,4},{12,8},{1,13},{5,1},{9,5},{13,9},{2,14},{6,2},{... | collective-permute-start | bytes 786440 | tf_op jit(solution)/shard_map/ppermute | solution.py:297
  75.4 5.5 %copy-start.1 = (f32[4,128,256]{2,1,0:T(8,128)}, f32[4,128,256]{2,1,0:T(8,128)S(1)}, u32[]{:S(2)}) copy-start(f32[4,128,256]{2,1,0:T(8,128)S(1)} %collective-permute-done.3.refs_4_) | copy-start | bytes 1572868
  80.9 0.8 copy-start.2
  81.7 8.8 %collective-permute-start.7 = (f32[2,128,256]{2,1,0:T(8,128)S(1)}, f32[2,128,256]{2,1,0:T(8,128)S(1)}, u32[]{:S(2)}, u32[]{:S(2)}) collective-permute-start(f32[2,128,256]{2,1,0:T(8,128)S(1)} %pad_maximum_fusion.2), channel_id=1, source_target_pairs={{0,4},{4,8},{8,12},{12,0},{1,5},{5,9},{9,13},{13,1},{2,6},{6,10},{... | collective-permute-start | bytes 786440 | tf_op jit(solution)/shard_map/ppermute | solution.py:297
  81.7 8.8 %collective-permute-start.8 = (f32[2,128,256]{2,1,0:T(8,128)S(1)}, f32[2,128,256]{2,1,0:T(8,128)S(1)}, u32[]{:S(2)}, u32[]{:S(2)}) collective-permute-start(f32[2,128,256]{2,1,0:T(8,128)S(1)} %pad_maximum_fusion.3), channel_id=1, source_target_pairs={{0,12},{4,0},{8,4},{12,8},{1,13},{5,1},{9,5},{13,9},{2,14},{6,2},{... | collective-permute-start | bytes 786440 | tf_op jit(solution)/shard_map/ppermute | solution.py:297
  90.5 1.0 copy-start.4
  90.5 1.1 %copy-start.5 = (f32[2,128,256]{2,1,0:T(8,128)}, f32[2,128,256]{2,1,0:T(8,128)S(1)}, u32[]{:S(2)}) copy-start(f32[2,128,256]{2,1,0:T(8,128)S(1)} %collective-permute-done.5.refs_6_) | copy-start | bytes 786436
  90.5 1.1 %copy-start.6 = (f32[2,128,256]{2,1,0:T(8,128)}, f32[2,128,256]{2,1,0:T(8,128)S(1)}, u32[]{:S(2)}) copy-start(f32[2,128,256]{2,1,0:T(8,128)S(1)} %collective-permute-done.6.refs_7_) | copy-start | bytes 786436
  90.6 1.2 %copy-start.7 = (f32[2,128,256]{2,1,0:T(8,128)}, f32[2,128,256]{2,1,0:T(8,128)S(1)}, u32[]{:S(2)}) copy-start(f32[2,128,256]{2,1,0:T(8,128)S(1)} %collective-permute-done.7.refs_8_) | copy-start | bytes 786436
  91.8 0.7 copy-start.8
where the time goes:
time: 101 us
  Pallas kernels  45.1 us (45%)
  waiting for transfers between devices  33.5 us (33%)
  starting transfers between devices  13.7 us (14%)
  local copies, waits for them, and re-layouts  7.39 us (7%)
    pallas_call x1, Pallas kernels, solve(): pl.pallas_call(functools.partial(solve_kernel, points, bands), out_shape=...  36.9 us
    ppermute x7, waiting for transfers between devices, shifted(): lax.ppermute(array, axis, [(i, (i + by) % size) for i in range(size)])  28.1 us
    ppermute x7, starting transfers between devices, shifted(): lax.ppermute(array, axis, [(i, (i + by) % size) for i in range(size)])  8.72 us
    pallas_call x1, Pallas kernels, update(): pl.pallas_call(functools.partial(update_kernel, groups, bands, tiles_y, l...  8.21 us
    ppermute x2, waiting for transfers between devices, to_next_tile(): return lax.ppermute(array, ('mem', 'gy'), pairs)  5.46 us
    ppermute x2, starting transfers between devices, to_next_tile(): return lax.ppermute(array, ('mem', 'gy'), pairs)  5 us
    unnamed x22, local copies, waits for them, and re-layouts  4.43 us
  transfers between devices with their start and end apart: 9, of which 4 were waited for; matrix products, arithmetic and copies ran while one was open for 2% of the time, Pallas kernels for 0%

commit v1 on v0

v1 whole, which is shorter than its diff:
```python
import functools

import jax
import jax.numpy as jnp
from jax import lax
from jax.experimental import pallas as pl
from jax.experimental.pallas import tpu as pltpu
from jax.sharding import PartitionSpec as P


CGX = 4
NS_STEPS = 12
SIDES = (0, CGX - 1)
POINTS = SIDES + tuple(range(1, CGX - 1))

F32 = jnp.float32
BF16 = jnp.bfloat16
MIB = 1024 * 1024
NT = (((1,), (1,)), ((), ()))


def dot(a, b):
    return jnp.dot(a, b, preferred_element_type=F32)


def dot_nt(a, b):
    return lax.dot_general(a, b, NT, preferred_element_type=F32)


def split2(x):
    high = x.astype(BF16)
    return high, (x - high.astype(F32)).astype(BF16)


def split3(x):
    high = x.astype(BF16)
    rest = x - high.astype(F32)
    mid = rest.astype(BF16)
    return high, mid, (rest - mid.astype(F32)).astype(BF16)


def mm3(a, b):
    return dot(
        jnp.concatenate([a[0], a[0], a[1]], axis=1),
        jnp.concatenate([b[0], b[1], b[0]], axis=0),
    )


def mm5(a, b):
    return dot(
        jnp.concatenate([a[0], a[1], a[2], a[0], a[1]], axis=1),
        jnp.concatenate([b[0], b[0], b[0], b[1], b[1]], axis=0),
    )


def quartics(ps, identity):
    pieces = [split2(p) for p in ps]
    squares = [mm3(piece, piece) for piece in pieces]
    results = []
    for p, square in zip(ps, squares):
        inner = 0.0625 * square - 0.5625 * p + 1.6875 * identity
        results.append((split2(square), split2(inner)))
    results = [mm3(*result) for result in results]
    return [
        split2(result + (2.25 * identity - 2.4375 * p)) for p, result in zip(ps, results)
    ]


def solve_kernel(points, bands, live_ref, own_ref, *refs):
    others = refs[: bands - 1]
    departure_ref, variance_ref, nearest_ref = refs[bands - 1 : bands + 2]
    outs = refs[bands + 2 : 3 * bands + 1]
    y_ref, cov_ref, right_ref, root_ref, inv_ref = refs[3 * bands + 1 :]
    me = lax.axis_index("mem")
    part, slots = own_ref.shape
    members = y_ref.shape[0]
    for shift, ref in enumerate((own_ref,) + tuple(others)):
        owner = lax.rem(me - shift + bands, bands)
        y_ref[pl.ds(pl.multiple_of(owner * part, part), part), :] = ref[...]
    rows = lax.broadcasted_iota(jnp.int32, (members, members), 0)
    columns = lax.broadcasted_iota(jnp.int32, (members, members), 1)
    identity = (rows == columns).astype(F32)
    live = (lax.broadcasted_iota(jnp.int32, (1, slots), 1) < live_ref[0]).astype(F32)
    base = live * lax.rsqrt(variance_ref[...])
    scales, roots = [], []
    for g, point in enumerate(points):
        distance = (nearest_ref[...] - point).astype(F32)
        weight = jnp.exp(-0.25 * distance * distance) * base
        y = split2(y_ref[...] * weight)
        cross = dot_nt(y[0], y[1])
        cov = dot_nt(y[0], y[0]) + dot_nt(y[1], y[1]) + (cross + cross.T)
        cov = cov + (members - 1.0) * identity
        d0, d1 = split2(jnp.broadcast_to(weight * departure_ref[...], (8, slots)))
        right_ref[g] = dot_nt(d0, y[0]) + dot_nt(d0, y[1]) + dot_nt(d1, y[0])
        square_sum = jnp.sum(jnp.sum(cov * cov, axis=1, keepdims=True), axis=0, keepdims=True)
        scale = lax.rsqrt(square_sum)
        scales.append(scale)
        roots.append(cov * scale)
    count = len(points)
    us = quartics(roots, identity)
    for g in range(count):
        for i, piece in enumerate(split3(mm5(split3(roots[g]), us[g]))):
            root_ref[g, i] = piece
        inv_ref[g, 0], inv_ref[g, 1] = us[g]

    def step(_, carry):
        ps = []
        for g in range(count):
            ps.append(mm3((inv_ref[g, 0], inv_ref[g, 1]), (root_ref[g, 0], root_ref[g, 1])))
        us = quartics(ps, identity)
        new = [mm5((root_ref[g, 0], root_ref[g, 1], root_ref[g, 2]), us[g]) for g in range(count)]
        for g in range(count):
            for i, piece in enumerate(split3(new[g])):
                root_ref[g, i] = piece
        new = [mm3(us[g], (inv_ref[g, 0], inv_ref[g, 1])) for g in range(count)]
        for g in range(count):
            inv_ref[g, 0], inv_ref[g, 1] = split2(new[g])
        return carry

    lax.fori_loop(0, NS_STEPS // 2 - 2, step, 0)
    ps = []
    for g in range(count):
        ps.append(mm3((inv_ref[g, 0], inv_ref[g, 1]), (root_ref[g, 0], root_ref[g, 1])))
    us = quartics(ps, identity)
    lasts = [mm3(us[g], (inv_ref[g, 0], inv_ref[g, 1])) for g in range(count)]
    for g in range(count):
        last = lasts[g]
        right = right_ref[g, 0:1, :]
        half = jnp.sum(last * right, axis=1, keepdims=True)
        mean_weights = jnp.sum(last * half, axis=0, keepdims=True) * scales[g]
        cov_ref[...] = last * jnp.sqrt((members - 1.0) * scales[g]) + mean_weights
        for shift in range(bands):
            target = lax.rem(me + shift, bands)
            rows = cov_ref[pl.ds(pl.multiple_of(target * part, part), part), :]
            if shift == 0:
                outs[0][g] = rows
            elif g < 2:
                outs[2 * shift - 1][g] = rows
            else:
                outs[2 * shift][g - 2] = rows


def solve(points, live, own, others, departure, variance, nearest):
    bands = 1 + len(others)
    part, slots = own.shape
    members = part * bands
    count = len(points)
    vmem = pl.BlockSpec(memory_space=pltpu.VMEM)
    return pl.pallas_call(
        functools.partial(solve_kernel, points, bands),
        out_shape=[jax.ShapeDtypeStruct((count, part, members), F32)]
        + [
            jax.ShapeDtypeStruct((n, part, members), F32)
            for _ in others
            for n in (2, count - 2)
        ],
        in_specs=[pl.BlockSpec(memory_space=pltpu.SMEM)] + [vmem] * (bands + 3),
        out_specs=[vmem] * (2 * bands - 1),
        scratch_shapes=[
            pltpu.VMEM((members, slots), F32),
            pltpu.VMEM((members, members), F32),
            pltpu.VMEM((count, 8, members), F32),
            pltpu.VMEM((count, 3, members, members), BF16),
            pltpu.VMEM((count, 2, members, members), BF16),
        ],
        compiler_params=pltpu.CompilerParams(vmem_limit_bytes=32 * MIB),
        cost_estimate=pl.CostEstimate(
            flops=2 * count * members * members * (4 * slots + 91 * members),
            bytes_accessed=4 * members * (slots + count * members),
            transcendentals=0,
        ),
        name="solve",
    )(live, own, *others, departure, variance, nearest)


def prepare_kernel(blocks, *refs):
    cells, (x_ref, mean_ref) = refs[:blocks], refs[blocks:]
    me = lax.axis_index("mem")
    members = x_ref.shape[3]
    strip = members // blocks
    total = sum(jnp.sum(ref[...], axis=2, keepdims=True) for ref in cells)
    mean = total * (1.0 / members)
    mean_ref[...] = jnp.broadcast_to(mean, mean_ref.shape)
    for shift, ref in enumerate(cells):
        x0, x1 = split2(ref[...] - mean)
        if blocks == 1:
            x_ref[0], x_ref[1] = x0, x1
        else:
            owner = lax.rem(me - shift + blocks, blocks)
            place = pl.ds(pl.multiple_of(owner * strip, strip), strip)
            x_ref[0, :, :, place] = x0
            x_ref[1, :, :, place] = x1


def prepare(cells, part):
    width, height, strip = cells[0].shape
    members = strip * len(cells)
    vmem = pl.BlockSpec(memory_space=pltpu.VMEM)
    return pl.pallas_call(
        functools.partial(prepare_kernel, len(cells)),
        out_shape=[
            jax.ShapeDtypeStruct((2, width, height, members), BF16),
            jax.ShapeDtypeStruct((width, height, part), F32),
        ],
        in_specs=[vmem] * len(cells),
        out_specs=[vmem] * 2,
        compiler_params=pltpu.CompilerParams(
            vmem_limit_bytes=16 * width * height * members + 8 * MIB
        ),
        cost_estimate=pl.CostEstimate(
            flops=8 * width * height * members,
            bytes_accessed=8 * width * height * members,
            transcendentals=0,
        ),
        name="prepare",
    )(*cells)


def add_terms(x_ref, t_ref, before_ref, out_ref, bands, mine):
    width, height, part = out_ref.shape
    members = x_ref.shape[3]
    spacing = width // CGX
    depth = height // bands
    for v in range(bands + 1):
        j0, j1 = max(depth * v - depth // 2, 0), min(depth * v + depth // 2, height)
        tall = j1 - j0
        j = lax.broadcasted_iota(jnp.int32, (1, tall, 1), 1).astype(F32) + (
            j0 + 0.5 - (v - 0.5) * depth
        )
        upper = j * (1.0 / depth)
        along_y = (1.0 - upper, upper)
        for c in range(CGX + 1):
            i0 = max(spacing * c - spacing // 2, 0)
            i1 = min(spacing * c + spacing // 2, width)
            wide = i1 - i0
            slots = [(v + a, c + b) for a in (0, 1) for b in (0, 1) if (v + a, c + b) in mine]
            if not slots:
                if before_ref is not out_ref:
                    out_ref[i0:i1, j0:j1, :] = before_ref[i0:i1, j0:j1, :]
                continue
            x0 = x_ref[0, i0:i1, j0:j1, :].reshape(wide * tall, members)
            x1 = x_ref[1, i0:i1, j0:j1, :].reshape(wide * tall, members)
            left = jnp.concatenate([x0, x0, x1], axis=1)
            i = lax.broadcasted_iota(jnp.int32, (wide, 1, 1), 0).astype(F32) + (
                i0 + 0.5 - (c - 0.5) * spacing
            )
            right = i * (1.0 / spacing)
            along_x = (1.0 - right, right)
            t0 = jnp.concatenate([t_ref[mine[slot], 0] for slot in slots], axis=0)
            t1 = jnp.concatenate([t_ref[mine[slot], 1] for slot in slots], axis=0)
            product = dot_nt(left, jnp.concatenate([t0, t1, t0], axis=1))
            product = product.reshape(wide, tall, len(slots) * part)
            result = before_ref[i0:i1, j0:j1, :]
            for n, (row, column) in enumerate(slots):
                weight = along_x[column - c] * along_y[row - v]
                result = result + weight * product[:, :, n * part : (n + 1) * part]
            out_ref[i0:i1, j0:j1, :] = result


def inner_slots(bands):
    names = [(row, column) for row in range(1, bands + 1) for column in range(1, CGX + 1)]
    return {name: n for n, name in enumerate(names)}


def outer_slots(bands):
    names = [(row, column) for row in (0, bands + 1) for column in range(CGX + 2)]
    names += [(row, column) for row in range(1, bands + 1) for column in (0, CGX + 1)]
    return {name: n for n, name in enumerate(names)}


def inner_kernel(bands, *refs):
    x_ref, mean_ref = refs[:2]
    rows = refs[2 : 2 * bands + 1]
    out_ref, t_ref = refs[2 * bands + 1 :]
    me = lax.axis_index("mem")
    for shift in range(bands):
        band = lax.rem(me - shift + bands, bands)
        for n, point in enumerate(POINTS):
            if shift == 0:
                value = rows[0][n]
            elif n < 2:
                value = rows[2 * shift - 1][n]
            else:
                value = rows[2 * shift][n - 2]
            t0, t1 = split2(value)
            t_ref[band * CGX + point, 0] = t0
            t_ref[band * CGX + point, 1] = t1
    add_terms(x_ref, t_ref, mean_ref, out_ref, bands, inner_slots(bands))


def outer_kernel(bands, tiles_y, *refs):
    refs = list(refs)

    def take(n):
        taken, refs[:n] = refs[:n], []
        return taken

    x_ref, before_ref = take(2)
    (own,) = take(1)
    ends_side = take(bands - 1)
    ends_mid = take(bands - 1)
    other_side = take(bands - 1)
    other_mid = take(bands - 1)
    (own_end,) = take(1)
    row_sides = take(2)
    end_sides = take(2)
    out_ref, t_ref = refs
    me = lax.axis_index("mem")
    tile_y = lax.axis_index("gy")
    slots = outer_slots(bands)
    south, north = slots[0, 0], slots[bands + 1, 0]

    def put(slot, value):
        t0, t1 = split2(value)
        t_ref[slot, 0] = t0
        t_ref[slot, 1] = t1

    def put_ends(shift, column, tile_value, end_value):
        band = lax.rem(me - shift + bands, bands)

        @pl.when((tile_y == 0) & (band == 0))
        def _():
            put(south + column, tile_value())

        @pl.when((tile_y == tiles_y - 1) & (band == bands - 1))
        def _():
            put(north + column, tile_value())

        @pl.when((tile_y > 0) & (me == (shift - 1) % bands))
        def _():
            put(south + column, end_value())

        @pl.when((tile_y < tiles_y - 1) & (me == shift))
        def _():
            put(north + column, end_value())

    for shift in range(bands):
        band = lax.rem(me - shift + bands, bands)
        for n, point in enumerate(POINTS):
            if shift == 0:
                here, there, k = own, own_end, n
            elif n < 2:
                here, there, k = other_side[shift - 1], ends_side[shift - 1], n
            else:
                here, there, k = other_mid[shift - 1], ends_mid[shift - 1], n - 2
            put_ends(
                shift,
                point + 1,
                lambda here=here, k=k: here[k],
                lambda there=there, k=k: there[k],
            )
        for side, column in enumerate((0, CGX + 1)):
            put(slots[1, 0] + 2 * band + side, row_sides[side][shift])
            put_ends(
                shift,
                column,
                lambda side=side: row_sides[side][shift],
                lambda side=side: end_sides[side][shift],
            )
    add_terms(x_ref, t_ref, before_ref, out_ref, bands, slots)


def apply_terms(kernel, x, before, operands, slots, flops):
    _, width, height, members = x.shape
    part = before.shape[2]
    vmem = pl.BlockSpec(memory_space=pltpu.VMEM)
    size = sum(array.size for array in operands)
    return pl.pallas_call(
        kernel,
        out_shape=jax.ShapeDtypeStruct((width, height, part), F32),
        in_specs=[vmem] * (2 + len(operands)),
        out_specs=vmem,
        scratch_shapes=[pltpu.VMEM((len(slots), 2, part, members), BF16)],
        compiler_params=pltpu.CompilerParams(
            vmem_limit_bytes=min(4 * (x.size + 2 * before.size + 2 * size) + 8 * MIB, 60 * MIB)
        ),
        cost_estimate=pl.CostEstimate(
            flops=flops, bytes_accessed=4 * (x.size + before.size), transcendentals=0
        ),
    )(x, before, *operands)


def shifted(array, axis, by):
    size = lax.axis_size(axis)
    return lax.ppermute(array, axis, [(i, (i + by) % size) for i in range(size)])


def to_next_tile(array, shift):
    bands = lax.axis_size("mem")
    tiles = lax.axis_size("gy")
    last, first = (shift - 1) % bands, shift
    pairs = [(last * tiles + y, last * tiles + y + 1) for y in range(tiles - 1)]
    pairs += [(first * tiles + y, first * tiles + y - 1) for y in range(1, tiles)]
    return lax.ppermute(array, ("mem", "gy"), pairs)


def analysis(background, anomalies, departure, variance, nearest, tally):
    bands = lax.axis_size("mem")
    tiles_y = lax.axis_size("gy")
    me = lax.axis_index("mem")
    part = background.shape[0]
    members = part * bands
    slots = departure.shape[3]
    anomalies = anomalies.reshape(part, bands * slots)
    others = []
    for shift in range(1, bands):
        piece = lax.dynamic_slice_in_dim(
            anomalies, lax.rem(me + shift, bands) * slots, slots, axis=1
        )
        others.append(shifted(piece, "mem", shift))
    own = lax.dynamic_slice_in_dim(anomalies, me * slots, slots, axis=1)
    tile = background.transpose(1, 2, 0)
    cells = [tile]
    for shift in range(1, bands):
        cells.append(shifted(tile, "mem", shift))
    if part % 128:
        order = lax.rem(me - jnp.arange(bands) + bands, bands)
        cells = jnp.take(jnp.stack(cells, axis=2), order, axis=2)
        cells = [cells.reshape(cells.shape[:2] + (members,))]
    solved = solve(
        POINTS,
        tally.reshape(1),
        own,
        others,
        departure.reshape(1, slots),
        variance.reshape(1, slots),
        nearest.reshape(1, slots),
    )
    row = solved[0]
    other_side = [shifted(solved[2 * s - 1], "mem", s) for s in range(1, bands)]
    own_end = to_next_tile(row, 0)
    other_mid = [shifted(solved[2 * s], "mem", s) for s in range(1, bands)]
    ends_side = [to_next_tile(other_side[s - 1], s) for s in range(1, bands)]
    row_sides = [
        shifted(jnp.stack([row[n]] + [array[n] for array in other_side]), "gx", by)
        for n, by in ((1, 1), (0, -1))
    ]
    ends_mid = [to_next_tile(other_mid[s - 1], s) for s in range(1, bands)]
    end_sides = [
        shifted(jnp.stack([own_end[n]] + [array[n] for array in ends_side]), "gx", by)
        for n, by in ((1, 1), (0, -1))
    ]
    x, mean = prepare(cells, part)
    operands = [row]
    for side, mid in zip(other_side, other_mid):
        operands += [side, mid]
    work = 6 * mean.size * members
    result = apply_terms(
        functools.partial(inner_kernel, bands),
        x,
        mean,
        operands,
        inner_slots(bands),
        3 * work,
    )
    result = apply_terms(
        functools.partial(outer_kernel, bands, tiles_y),
        x,
        result,
        [row]
        + ends_side
        + ends_mid
        + other_side
        + other_mid
        + [own_end]
        + row_sides
        + end_sides,
        outer_slots(bands),
        work,
    )
    return result.transpose(2, 0, 1)


def solution(mesh):
    in_specs = (
        P("mem", "gx", "gy"),
        P("mem", "gx", "gy", None),
        P("gx", "gy", "mem", None),
        P("gx", "gy", "mem", None),
        P("gx", "gy", "mem", None),
        P("gx", "gy", "mem"),
    )
    out_specs = P("mem", "gx", "gy")
    return jax.shard_map(
        analysis, mesh=mesh, in_specs=in_specs, out_specs=out_specs, check_vma=False
    )
```

time: 101 us -> 86.5 us (0.86)
  Pallas kernels: 45.1 us -> 24 us
  waiting for transfers between devices: 33.5 us -> 39.9 us
  starting transfers between devices: 13.7 us -> 19.3 us
  local copies, waits for them, and re-layouts: 7.39 us -> 2.24 us
    pallas_call x1, Pallas kernels: 36.9 us -> 18 us  [solve(): pl.pallas_call(functools.partial(solve_kernel, points, bands), out_shape=...]
    ppermute x7 -> x8, waiting for transfers between devices: 28.1 us -> 38.5 us  [shifted(): lax.ppermute(array, axis, [(i, (i + by) % size) for i in range(size)])]
    unnamed x22 -> x10, local copies, waits for them, and re-layouts: 4.43 us -> 0.21 us
    ppermute x2 -> x3, waiting for transfers between devices: 5.46 us -> 1.43 us  [to_next_tile(): return lax.ppermute(array, ('mem', 'gy'), pairs)]
    ppermute x2 -> x3, starting transfers between devices: 5 us -> 8.42 us  [to_next_tile(): return lax.ppermute(array, ('mem', 'gy'), pairs)]
    pallas_call x1 -> x3, Pallas kernels: 8.21 us -> 6.08 us  [the longest x2 5.07 us: apply_terms(): pl.pallas_call(kernel, out_shape=jax.ShapeDtypeStruct((width, height, par...]
    ppermute x7 -> x8, starting transfers between devices: 8.72 us -> 10.8 us  [shifted(): lax.ppermute(array, axis, [(i, (i + by) % size) for i in range(size)])]
  transfers between devices with their start and end apart: 9 -> 11, of which waited for: 4 -> 6; matrix products, arithmetic and copies ran while one was open for 2% -> 0% of each run, Pallas kernels for 0% -> 3%
where the time goes in v1:
time: 86.5 us; the launch traced here: 86.4 us
  waiting for transfers between devices  39.9 us (46%)
  Pallas kernels  24 us (28%)
  starting transfers between devices  19.3 us (22%)
  local copies, waits for them, and re-layouts  2.24 us (3%)
    ppermute x8, waiting for transfers between devices, shifted(): lax.ppermute(array, axis, [(i, (i + by) % size) for i in range(size)])  38.5 us
    pallas_call x1, Pallas kernels, solve(): pl.pallas_call(functools.partial(solve_kernel, points, bands), out_shape=...  18 us
    ppermute x8, starting transfers between devices, shifted(): lax.ppermute(array, axis, [(i, (i + by) % size) for i in range(size)])  10.8 us
    ppermute x3, starting transfers between devices, to_next_tile(): return lax.ppermute(array, ('mem', 'gy'), pairs)  8.42 us
    pallas_call x2, Pallas kernels, apply_terms(): pl.pallas_call(kernel, out_shape=jax.ShapeDtypeStruct((width, height, par...  5.07 us
    dynamic_slice x1, local copies, waits for them, and re-layouts, analysis(): lax.dynamic_slice_in_dim(anomalies, lax.rem(me + shift, bands) * slots, s...  1.96 us
  transfers between devices with their start and end apart: 11, of which 6 were waited for; matrix products, arithmetic and copies ran while one was open for 0% of the time, Pallas kernels for 3%

profile of v1, /device:TPU:0, one launch (start us, length us, event | category | flops | bytes accessed | tf_op | source)
XLA Modules:
  0.0 86.4 jit_solution(2951620402251240601)
XLA Ops:
  0.0 2.0 %constant_dynamic-slice_fusion = (f32[128,1,1,1024]{3,2,1,0:T(1,128)S(1)}, f32[128,1,1,1024]{3,2,1,0:T(1,128)S(1)}) fusion(f32[128,1,1,2048]{3,2,1,0:T(1,128)} %param.7, s32[]{:T(128)S(6)} %select_n.7, s32[]{:T(128)S(6)} %select_n.6), kind=kLoop, calls=%fused_computation.6 | loop fusion | bytes 2097160 | tf_op jit(solution)/shard_map/dynamic_slice | solution.py:407
  2.0 0.1 copy.11
  2.1 3.1 %collective-permute-start.1 = (f32[128,1024]{1,0:T(8,128)S(1)}, f32[128,1024]{1,0:T(8,128)S(1)}, u32[]{:S(2)}, u32[]{:S(2)}) collective-permute-start(f32[128,1024]{1,0:T(8,128)S(1)} %bitcast.19), channel_id=1, source_target_pairs={{0,16},{16,0},{1,17},{17,1},{2,18},{18,2},{3,19},{19,3},{4,20},{20... | collective-permute-start | bytes 1572872 | tf_op jit(solution)/shard_map/ppermute | solution.py:385
  5.1 0.1 copy.12
  5.9 11.2 %collective-permute-done.1.refs_0_ = f32[128,1024]{1,0:T(8,128)S(1)} collective-permute-done((f32[128,1024]{1,0:T(8,128)S(1)}, f32[128,1024]{1,0:T(8,128)S(1)}, u32[]{:S(2)}, u32[]{:S(2)}) %collective-permute-start.1) | collective-permute-done | bytes 524320 | tf_op jit(solution)/shard_map/ppermute | solution.py:385
  17.1 0.0 copy-done.1
  17.1 0.0 copy-done.2
  17.1 0.0 copy-start
  17.1 18.0 %solve.1 = (f32[4,128,256]{2,1,0:T(8,128)S(1)}, f32[2,128,256]{2,1,0:T(8,128)S(1)}, f32[2,128,256]{2,1,0:T(8,128)S(1)}) custom-call(s32[1]{0:T(128)} %bitcast.12.live_ref, f32[128,1024]{1,0:T(8,128)S(1)} %bitcast.15, f32[128,1024]{1,0:T(8,128)S(1)} %collective-permute-done.1.refs_0_, f32[1,1024]{1,0:T(1,128)S(1)} %bitcast.16, f32[1,1024]{1,0:T(1,128)S(1)} %bitcast.17, ...), custom_call_target="tpu_custom_call" | custom-call | flops 14361296896 | bytes 2097152 | tf_op jit(solution)/shard_map/solve/pallas_call | solution.py:149
  35.1 1.8 %collective-permute-start.2 = (f32[2,128,256]{2,1,0:T(8,128)S(1)}, f32[2,128,256]{2,1,0:T(8,128)S(1)}, u32[]{:S(2)}, u32[]{:S(2)}) collective-permute-start(f32[2,128,256]{2,1,0:T(8,128)S(1)} %get-tuple-element.13), channel_id=1, source_target_pairs={{0,16},{16,0},{1,17},{17,1},{2,18},{18,2},{3,19},{19,3},{4,20},{20... | collective-permute-start | bytes 786440 | tf_op jit(solution)/shard_map/ppermute | solution.py:385
  36.9 0.3 collective-permute-start
  37.2 1.3 %collective-permute-start.6 = (f32[4,128,256]{2,1,0:T(8,128)S(1)}, f32[4,128,256]{2,1,0:T(8,128)S(1)}, u32[]{:S(2)}, u32[]{:S(2)}) collective-permute-start(f32[4,128,256]{2,1,0:T(8,128)S(1)} %get-tuple-element.12.refs_2_), channel_id=1, source_target_pairs={{16,17},{17,18},{18,19},{1,0},{2,1},{3,2},{20,21},{21,22},{22,23},... | collective-permute-start | bytes 1572872 | tf_op jit(solution)/shard_map/ppermute | solution.py:394
  38.4 4.0 %collective-permute-start.3 = (f32[2,128,256]{2,1,0:T(8,128)S(1)}, f32[2,128,256]{2,1,0:T(8,128)S(1)}, u32[]{:S(2)}, u32[]{:S(2)}) collective-permute-start(f32[2,128,256]{2,1,0:T(8,128)S(1)} %get-tuple-element.14), channel_id=1, source_target_pairs={{0,16},{16,0},{1,17},{17,1},{2,18},{18,2},{3,19},{19,3},{4,20},{20... | collective-permute-start | bytes 786440 | tf_op jit(solution)/shard_map/ppermute | solution.py:385
  42.5 1.8 %collective-permute-done.2.refs_3_.refs_5_ = f32[2,128,256]{2,1,0:T(8,128)S(1)} collective-permute-done((f32[2,128,256]{2,1,0:T(8,128)S(1)}, f32[2,128,256]{2,1,0:T(8,128)S(1)}, u32[]{:S(2)}, u32[]{:S(2)}) %collective-permute-start.2) | collective-permute-done | bytes 262176 | tf_op jit(solution)/shard_map/ppermute | solution.py:385
  44.3 3.7 %collective-permute-start.4 = (f32[2,128,256]{2,1,0:T(8,128)S(1)}, f32[2,128,256]{2,1,0:T(8,128)S(1)}, u32[]{:S(2)}, u32[]{:S(2)}) collective-permute-start(f32[2,128,256]{2,1,0:T(8,128)S(1)} %collective-permute-done.2.refs_3_.refs_5_), channel_id=1, source_target_pairs={{0,1},{1,2},{2,3},{17,16},{18,17},{19,18},{4,5},{5,6},{6,7},{21,20... | collective-permute-start | bytes 786440 | tf_op jit(solution)/shard_map/ppermute | solution.py:394
  48.1 0.1 collective-permute-start.7
  48.2 22.5 %collective-permute-done.3.refs_4_.refs_6_ = f32[2,128,256]{2,1,0:T(8,128)S(1)} collective-permute-done((f32[2,128,256]{2,1,0:T(8,128)S(1)}, f32[2,128,256]{2,1,0:T(8,128)S(1)}, u32[]{:S(2)}, u32[]{:S(2)}) %collective-permute-start.3) | collective-permute-done | bytes 262176 | tf_op jit(solution)/shard_map/ppermute | solution.py:385
  70.7 0.0 collective-permute-start.8
  70.7 0.0 collective-permute-done.4.refs_3_
  70.7 3.4 %collective-permute-start.5 = (f32[2,128,256]{2,1,0:T(8,128)S(1)}, f32[2,128,256]{2,1,0:T(8,128)S(1)}, u32[]{:S(2)}, u32[]{:S(2)}) collective-permute-start(f32[2,128,256]{2,1,0:T(8,128)S(1)} %collective-permute-done.3.refs_4_.refs_6_), channel_id=1, source_target_pairs={{0,1},{1,2},{2,3},{17,16},{18,17},{19,18},{4,5},{5,6},{6,7},{21,20... | collective-permute-start | bytes 786440 | tf_op jit(solution)/shard_map/ppermute | solution.py:394
  74.2 0.0 collective-permute-done.6.refs_7_
  74.2 1.4 %collective-permute-start.10 = (f32[2,128,256]{2,1,0:T(8,128)S(1)}, f32[2,128,256]{2,1,0:T(8,128)S(1)}, u32[]{:S(2)}, u32[]{:S(2)}) collective-permute-start(f32[2,128,256]{2,1,0:T(8,128)S(1)} %pad_maximum_fusion.3), channel_id=1, source_target_pairs={{0,12},{4,0},{8,4},{12,8},{1,13},{5,1},{9,5},{13,9},{2,14},{6,2},{... | collective-permute-start | bytes 786440 | tf_op jit(solution)/shard_map/ppermute | solution.py:385
  75.6 0.0 collective-permute-done.refs_1_
  75.6 0.2 collective-permute-start.9
  75.9 1.0 %prepare.1 = (bf16[2,32,64,256]{3,2,1,0:T(8,128)(2,1)S(1)}, f32[32,64,128]{2,1,0:T(8,128)S(1)}) custom-call(f32[32,64,128]{2,1,0:T(8,128)S(1)} %bitcast.14, f32[32,64,128]{2,1,0:T(8,128)S(1)} %collective-permute-done.refs_1_), custom_call_target="tpu_custom_call" | custom-call | flops 4194304 | bytes 4194304 | tf_op jit(solution)/shard_map/prepare/pallas_call | solution.py:199
  76.9 2.0 %shard_map.64.refs_1_ = f32[32,64,128]{2,1,0:T(8,128)S(1)} custom-call(bf16[2,32,64,256]{3,2,1,0:T(8,128)(2,1)S(1)} %get-tuple-element.10.refs_0_, f32[32,64,128]{2,1,0:T(8,128)S(1)} %get-tuple-element.11.refs_1_, f32[4,128,256]{2,1,0:T(8,128)S(1)} %get-tuple-element.12.refs_2_, f32[2,128,256]{2,1,0:T(8,128)S(1)} %collective-permute-done.2.refs_3_.refs_5_, ...), custom_call_target="tpu_custom_call" | custom-call | flops 1207959552 | bytes 5242880 | tf_op jit(solution)/shard_map/pallas_call | solution.py:368
  78.9 0.0 collective-permute-done.7.refs_8_
  78.9 0.0 collective-permute-done.8.refs_9_
  78.9 1.4 %collective-permute-done.5.refs_4_ = f32[2,128,256]{2,1,0:T(8,128)S(1)} collective-permute-done((f32[2,128,256]{2,1,0:T(8,128)S(1)}, f32[2,128,256]{2,1,0:T(8,128)S(1)}, u32[]{:S(2)}, u32[]{:S(2)}) %collective-permute-start.5) | collective-permute-done | bytes 262176 | tf_op jit(solution)/shard_map/ppermute | solution.py:394
  80.3 1.7 %collective-permute-done.10.refs_11_ = f32[2,128,256]{2,1,0:T(8,128)S(1)} collective-permute-done((f32[2,128,256]{2,1,0:T(8,128)S(1)}, f32[2,128,256]{2,1,0:T(8,128)S(1)}, u32[]{:S(2)}, u32[]{:S(2)}) %collective-permute-start.10) | collective-permute-done | bytes 262176 | tf_op jit(solution)/shard_map/ppermute | solution.py:385
  82.1 1.2 %collective-permute-done.9.refs_10_ = f32[2,128,256]{2,1,0:T(8,128)S(1)} collective-permute-done((f32[2,128,256]{2,1,0:T(8,128)S(1)}, f32[2,128,256]{2,1,0:T(8,128)S(1)}, u32[]{:S(2)}, u32[]{:S(2)}) %collective-permute-start.9) | collective-permute-done | bytes 262176 | tf_op jit(solution)/shard_map/ppermute | solution.py:385
  83.3 3.1 %shard_map.65 = f32[32,64,128]{2,1,0:T(8,128)} custom-call(bf16[2,32,64,256]{3,2,1,0:T(8,128)(2,1)S(1)} %get-tuple-element.10.refs_0_, f32[32,64,128]{2,1,0:T(8,128)S(1)} %shard_map.64.refs_1_, f32[4,128,256]{2,1,0:T(8,128)S(1)} %get-tuple-element.12.refs_2_, f32[2,128,256]{2,1,0:T(8,128)S(1)} %collective-permute-done.4.refs_3_, ...), custom_call_target="tpu_custom_call" | custom-call | flops 402653184 | bytes 5242880 | tf_op jit(solution)/shard_map/pallas_call | solution.py:368
  (13 shorter events, 0.2 us)
Async XLA Ops:
  0.0 17.1 %copy-start.1 = (f32[1,1,1,1024]{3,2,1,0:T(1,128)S(1)}, f32[1,1,1,1024]{3,2,1,0:T(1,128)}, u32[]{:S(2)}) copy-start(f32[1,1,1,1024]{3,2,1,0:T(1,128)} %param.8) | copy-start | bytes 12292
  0.0 17.1 %copy-start.2 = (f32[1,1,1,1024]{3,2,1,0:T(1,128)S(1)}, f32[1,1,1,1024]{3,2,1,0:T(1,128)}, u32[]{:S(2)}) copy-start(f32[1,1,1,1024]{3,2,1,0:T(1,128)} %param.9) | copy-start | bytes 12292
  0.0 17.1 %copy-start.3 = (s32[1,1,1,1024]{3,2,1,0:T(1,128)S(1)}, s32[1,1,1,1024]{3,2,1,0:T(1,128)}, u32[]{:S(2)}) copy-start(s32[1,1,1,1024]{3,2,1,0:T(1,128)} %param.10) | copy-start | bytes 12292
  2.1 15.0 %collective-permute-start.1 = (f32[128,1024]{1,0:T(8,128)S(1)}, f32[128,1024]{1,0:T(8,128)S(1)}, u32[]{:S(2)}, u32[]{:S(2)}) collective-permute-start(f32[128,1024]{1,0:T(8,128)S(1)} %bitcast.19), channel_id=1, source_target_pairs={{0,16},{16,0},{1,17},{17,1},{2,18},{18,2},{3,19},{19,3},{4,20},{20... | collective-permute-start | bytes 1572872 | tf_op jit(solution)/shard_map/ppermute | solution.py:385
  17.1 19.8 %copy-start = (f32[128,32,64]{0,2,1:T(8,128)S(1)}, f32[128,32,64]{0,2,1:T(8,128)}, u32[]{:S(2)}) copy-start(f32[128,32,64]{0,2,1:T(8,128)} %param.6) | copy-start | bytes 3145732
  35.1 9.2 %collective-permute-start.2 = (f32[2,128,256]{2,1,0:T(8,128)S(1)}, f32[2,128,256]{2,1,0:T(8,128)S(1)}, u32[]{:S(2)}, u32[]{:S(2)}) collective-permute-start(f32[2,128,256]{2,1,0:T(8,128)S(1)} %get-tuple-element.13), channel_id=1, source_target_pairs={{0,16},{16,0},{1,17},{17,1},{2,18},{18,2},{3,19},{19,3},{4,20},{20... | collective-permute-start | bytes 786440 | tf_op jit(solution)/shard_map/ppermute | solution.py:385
  36.9 38.7 %collective-permute-start = (f32[32,64,128]{2,1,0:T(8,128)S(1)}, f32[32,64,128]{2,1,0:T(8,128)S(1)}, u32[]{:S(2)}, u32[]{:S(2)}) collective-permute-start(f32[32,64,128]{2,1,0:T(8,128)S(1)} %bitcast.13), channel_id=1, source_target_pairs={{0,16},{16,0},{1,17},{17,1},{2,18},{18,2},{3,19},{19,3},{4,20},{20... | collective-permute-start | bytes 3145736 | tf_op jit(solution)/shard_map/ppermute | solution.py:385
  37.2 37.0 %collective-permute-start.6 = (f32[4,128,256]{2,1,0:T(8,128)S(1)}, f32[4,128,256]{2,1,0:T(8,128)S(1)}, u32[]{:S(2)}, u32[]{:S(2)}) collective-permute-start(f32[4,128,256]{2,1,0:T(8,128)S(1)} %get-tuple-element.12.refs_2_), channel_id=1, source_target_pairs={{16,17},{17,18},{18,19},{1,0},{2,1},{3,2},{20,21},{21,22},{22,23},... | collective-permute-start | bytes 1572872 | tf_op jit(solution)/shard_map/ppermute | solution.py:394
  38.4 32.2 %collective-permute-start.3 = (f32[2,128,256]{2,1,0:T(8,128)S(1)}, f32[2,128,256]{2,1,0:T(8,128)S(1)}, u32[]{:S(2)}, u32[]{:S(2)}) collective-permute-start(f32[2,128,256]{2,1,0:T(8,128)S(1)} %get-tuple-element.14), channel_id=1, source_target_pairs={{0,16},{16,0},{1,17},{17,1},{2,18},{18,2},{3,19},{19,3},{4,20},{20... | collective-permute-start | bytes 786440 | tf_op jit(solution)/shard_map/ppermute | solution.py:385
  44.3 26.4 %collective-permute-start.4 = (f32[2,128,256]{2,1,0:T(8,128)S(1)}, f32[2,128,256]{2,1,0:T(8,128)S(1)}, u32[]{:S(2)}, u32[]{:S(2)}) collective-permute-start(f32[2,128,256]{2,1,0:T(8,128)S(1)} %collective-permute-done.2.refs_3_.refs_5_), channel_id=1, source_target_pairs={{0,1},{1,2},{2,3},{17,16},{18,17},{19,18},{4,5},{5,6},{6,7},{21,20... | collective-permute-start | bytes 786440 | tf_op jit(solution)/shard_map/ppermute | solution.py:394
  48.1 30.8 %collective-permute-start.7 = (f32[2,128,256]{2,1,0:T(8,128)S(1)}, f32[2,128,256]{2,1,0:T(8,128)S(1)}, u32[]{:S(2)}, u32[]{:S(2)}) collective-permute-start(f32[2,128,256]{2,1,0:T(8,128)S(1)} %pad_maximum_fusion), channel_id=1, source_target_pairs={{0,4},{4,8},{8,12},{12,0},{1,5},{5,9},{9,13},{13,1},{2,6},{6,10},{... | collective-permute-start | bytes 786440 | tf_op jit(solution)/shard_map/ppermute | solution.py:385
  70.7 8.2 %collective-permute-start.8 = (f32[2,128,256]{2,1,0:T(8,128)S(1)}, f32[2,128,256]{2,1,0:T(8,128)S(1)}, u32[]{:S(2)}, u32[]{:S(2)}) collective-permute-start(f32[2,128,256]{2,1,0:T(8,128)S(1)} %pad_maximum_fusion.1), channel_id=1, source_target_pairs={{0,12},{4,0},{8,4},{12,8},{1,13},{5,1},{9,5},{13,9},{2,14},{6,2},{... | collective-permute-start | bytes 786440 | tf_op jit(solution)/shard_map/ppermute | solution.py:385
  70.7 9.6 %collective-permute-start.5 = (f32[2,128,256]{2,1,0:T(8,128)S(1)}, f32[2,128,256]{2,1,0:T(8,128)S(1)}, u32[]{:S(2)}, u32[]{:S(2)}) collective-permute-start(f32[2,128,256]{2,1,0:T(8,128)S(1)} %collective-permute-done.3.refs_4_.refs_6_), channel_id=1, source_target_pairs={{0,1},{1,2},{2,3},{17,16},{18,17},{19,18},{4,5},{5,6},{6,7},{21,20... | collective-permute-start | bytes 786440 | tf_op jit(solution)/shard_map/ppermute | solution.py:394
  74.2 7.8 %collective-permute-start.10 = (f32[2,128,256]{2,1,0:T(8,128)S(1)}, f32[2,128,256]{2,1,0:T(8,128)S(1)}, u32[]{:S(2)}, u32[]{:S(2)}) collective-permute-start(f32[2,128,256]{2,1,0:T(8,128)S(1)} %pad_maximum_fusion.3), channel_id=1, source_target_pairs={{0,12},{4,0},{8,4},{12,8},{1,13},{5,1},{9,5},{13,9},{2,14},{6,2},{... | collective-permute-start | bytes 786440 | tf_op jit(solution)/shard_map/ppermute | solution.py:385
  75.6 7.7 %collective-permute-start.9 = (f32[2,128,256]{2,1,0:T(8,128)S(1)}, f32[2,128,256]{2,1,0:T(8,128)S(1)}, u32[]{:S(2)}, u32[]{:S(2)}) collective-permute-start(f32[2,128,256]{2,1,0:T(8,128)S(1)} %pad_maximum_fusion.2), channel_id=1, source_target_pairs={{0,4},{4,8},{8,12},{12,0},{1,5},{5,9},{9,13},{13,1},{2,6},{6,10},{... | collective-permute-start | bytes 786440 | tf_op jit(solution)/shard_map/ppermute | solution.py:385

commit v2 on v1

--- a/solution.py
+++ b/solution.py
@@ -53,16 +53,19 @@
     )
 
 
-def quartics(ps, identity):
-    pieces = [split2(p) for p in ps]
-    squares = [mm3(piece, piece) for piece in pieces]
-    results = []
-    for p, square in zip(ps, squares):
-        inner = 0.0625 * square - 0.5625 * p + 1.6875 * identity
-        results.append((split2(square), split2(inner)))
-    results = [mm3(*result) for result in results]
+def mm1(a, b):
+    return dot(a[0], b[0])
+
+
+def quartics(ps, identity, square_mm, inner_mm):
+    squares = [square_mm(piece, piece) for piece in [split2(p) for p in ps]]
+    inner = [
+        inner_mm(split2(square), split2(0.0625 * square - 0.5625 * p))
+        for p, square in zip(ps, squares)
+    ]
     return [
-        split2(result + (2.25 * identity - 2.4375 * p)) for p, result in zip(ps, results)
+        split2(product + (1.6875 * square + (2.25 * identity - 2.4375 * p)))
+        for p, square, product in zip(ps, squares, inner)
     ]
 
 
@@ -97,32 +100,45 @@
         scales.append(scale)
         roots.append(cov * scale)
     count = len(points)
-    us = quartics(roots, identity)
+    us = quartics(roots, identity, mm1, mm1)
     for g in range(count):
         for i, piece in enumerate(split3(mm5(split3(roots[g]), us[g]))):
             root_ref[g, i] = piece
         inv_ref[g, 0], inv_ref[g, 1] = us[g]
 
-    def step(_, carry):
-        ps = []
+    def products():
+        return [
+            mm3((inv_ref[g, 0], inv_ref[g, 1]), (root_ref[g, 0], root_ref[g, 1]))
+            for g in range(count)
+        ]
+
+    def inverses(us):
+        return [mm3(us[g], (inv_ref[g, 0], inv_ref[g, 1])) for g in range(count)]
+
+    def step(square_mm, full):
+        us = quartics(products(), identity, square_mm, mm1)
+        if full:
+            new = [
+                mm5((root_ref[g, 0], root_ref[g, 1], root_ref[g, 2]), us[g])
+                for g in range(count)
+            ]
+        else:
+            new = [mm3((root_ref[g, 0], root_ref[g, 1]), us[g]) for g in range(count)]
         for g in range(count):
-            ps.append(mm3((inv_ref[g, 0], inv_ref[g, 1]), (root_ref[g, 0], root_ref[g, 1])))
-        us = quartics(ps, identity)
-        new = [mm5((root_ref[g, 0], root_ref[g, 1], root_ref[g, 2]), us[g]) for g in range(count)]
-        for g in range(count):
-            for i, piece in enumerate(split3(new[g])):
+            pieces = split3(new[g]) if full else split2(new[g])
+            for i, piece in enumerate(pieces):
                 root_ref[g, i] = piece
-        new = [mm3(us[g], (inv_ref[g, 0], inv_ref[g, 1])) for g in range(count)]
+        new = inverses(us)
         for g in range(count):
             inv_ref[g, 0], inv_ref[g, 1] = split2(new[g])
+
+    def early(_, carry):
+        step(mm1, True)
         return carry
 
-    lax.fori_loop(0, NS_STEPS // 2 - 2, step, 0)
-    ps = []
-    for g in range(count):
-        ps.append(mm3((inv_ref[g, 0], inv_ref[g, 1]), (root_ref[g, 0], root_ref[g, 1])))
-    us = quartics(ps, identity)
-    lasts = [mm3(us[g], (inv_ref[g, 0], inv_ref[g, 1])) for g in range(count)]
+    lax.fori_loop(0, NS_STEPS // 2 - 3, early, 0)
+    step(mm3, False)
+    lasts = inverses(quartics(products(), identity, mm3, mm3))
     for g in range(count):
         last = lasts[g]
         right = right_ref[g, 0:1, :]
@@ -165,7 +181,7 @@
         ],
         compiler_params=pltpu.CompilerParams(vmem_limit_bytes=32 * MIB),
         cost_estimate=pl.CostEstimate(
-            flops=2 * count * members * members * (4 * slots + 91 * members),
+            flops=2 * count * members * members * (3 * slots + 71 * members),
             bytes_accessed=4 * members * (slots + count * members),
             transcendentals=0,
         ),
@@ -174,25 +190,28 @@
 
 
 def prepare_kernel(blocks, *refs):
-    cells, (x_ref, mean_ref) = refs[:blocks], refs[blocks:]
     me = lax.axis_index("mem")
+    cells, edges = refs[:blocks], refs[blocks : 2 * blocks]
+    x_ref, mean_ref, edge_ref = refs[2 * blocks :]
     members = x_ref.shape[3]
     strip = members // blocks
-    total = sum(jnp.sum(ref[...], axis=2, keepdims=True) for ref in cells)
-    mean = total * (1.0 / members)
-    mean_ref[...] = jnp.broadcast_to(mean, mean_ref.shape)
-    for shift, ref in enumerate(cells):
-        x0, x1 = split2(ref[...] - mean)
-        if blocks == 1:
-            x_ref[0], x_ref[1] = x0, x1
-        else:
-            owner = lax.rem(me - shift + blocks, blocks)
-            place = pl.ds(pl.multiple_of(owner * strip, strip), strip)
-            x_ref[0, :, :, place] = x0
-            x_ref[1, :, :, place] = x1
-
-
-def prepare(cells, part):
+    for pieces, to_ref in ((cells, x_ref), (edges, edge_ref)):
+        total = sum(jnp.sum(ref[...], axis=2, keepdims=True) for ref in pieces)
+        mean = total * (1.0 / members)
+        if to_ref is x_ref:
+            mean_ref[...] = jnp.broadcast_to(mean, mean_ref.shape)
+        for shift, ref in enumerate(pieces):
+            x0, x1 = split2(ref[...] - mean)
+            if blocks == 1:
+                to_ref[0], to_ref[1] = x0, x1
+            else:
+                owner = lax.rem(me - shift + blocks, blocks)
+                place = pl.ds(pl.multiple_of(owner * strip, strip), strip)
+                to_ref[0, :, :, place] = x0
+                to_ref[1, :, :, place] = x1
+
+
+def prepare(cells, edges, part):
     width, height, strip = cells[0].shape
     members = strip * len(cells)
     vmem = pl.BlockSpec(memory_space=pltpu.VMEM)
@@ -201,9 +220,10 @@
         out_shape=[
             jax.ShapeDtypeStruct((2, width, height, members), BF16),
             jax.ShapeDtypeStruct((width, height, part), F32),
+            jax.ShapeDtypeStruct((2,) + edges[0].shape[:2] + (members,), BF16),
         ],
-        in_specs=[vmem] * len(cells),
-        out_specs=[vmem] * 2,
+        in_specs=[vmem] * (2 * len(cells)),
+        out_specs=[vmem] * 3,
         compiler_params=pltpu.CompilerParams(
             vmem_limit_bytes=16 * width * height * members + 8 * MIB
         ),
@@ -213,7 +233,7 @@
             transcendentals=0,
         ),
         name="prepare",
-    )(*cells)
+    )(*cells, *edges)
 
 
 def add_terms(x_ref, t_ref, before_ref, out_ref, bands, mine):
@@ -262,10 +282,43 @@
     return {name: n for n, name in enumerate(names)}
 
 
-def outer_slots(bands):
-    names = [(row, column) for row in (0, bands + 1) for column in range(CGX + 2)]
+def edge_slots(bands):
+    names = [(row, column) for row in (0, bands + 1) for column in (1, CGX)]
     names += [(row, column) for row in range(1, bands + 1) for column in (0, CGX + 1)]
     return {name: n for n, name in enumerate(names)}
+
+
+def last_slots(bands):
+    names = [(row, column) for row in (0, bands + 1) for column in range(2, CGX)]
+    return {name: n for n, name in enumerate(names)}
+
+
+def put(t_ref, slot, value):
+    t0, t1 = split2(value)
+    t_ref[slot, 0] = t0
+    t_ref[slot, 1] = t1
+
+
+def put_ends(t_ref, south, north, bands, tiles_y, shift, tile_value, end_value):
+    me = lax.axis_index("mem")
+    tile_y = lax.axis_index("gy")
+    band = lax.rem(me - shift + bands, bands)
+
+    @pl.when((tile_y == 0) & (band == 0))
+    def _():
+        put(t_ref, south, tile_value())
+
+    @pl.when((tile_y == tiles_y - 1) & (band == bands - 1))
+    def _():
+        put(t_ref, north, tile_value())
+
+    @pl.when((tile_y > 0) & (me == (shift - 1) % bands))
+    def _():
+        put(t_ref, south, end_value())
+
+    @pl.when((tile_y < tiles_y - 1) & (me == shift))
+    def _():
+        put(t_ref, north, end_value())
 
 
 def inner_kernel(bands, *refs):
@@ -288,7 +341,7 @@
     add_terms(x_ref, t_ref, mean_ref, out_ref, bands, inner_slots(bands))
 
 
-def outer_kernel(bands, tiles_y, *refs):
+def edge_kernel(bands, tiles_y, *refs):
     refs = list(refs)
 
     def take(n):
@@ -296,68 +349,121 @@
         return taken
 
     x_ref, before_ref = take(2)
-    (own,) = take(1)
-    ends_side = take(bands - 1)
-    ends_mid = take(bands - 1)
-    other_side = take(bands - 1)
-    other_mid = take(bands - 1)
-    (own_end,) = take(1)
-    row_sides = take(2)
-    end_sides = take(2)
+    rows, ends, sides = take(bands), take(bands), take(2)
     out_ref, t_ref = refs
     me = lax.axis_index("mem")
-    tile_y = lax.axis_index("gy")
-    slots = outer_slots(bands)
-    south, north = slots[0, 0], slots[bands + 1, 0]
-
-    def put(slot, value):
-        t0, t1 = split2(value)
-        t_ref[slot, 0] = t0
-        t_ref[slot, 1] = t1
-
-    def put_ends(shift, column, tile_value, end_value):
-        band = lax.rem(me - shift + bands, bands)
-
-        @pl.when((tile_y == 0) & (band == 0))
-        def _():
-            put(south + column, tile_value())
-
-        @pl.when((tile_y == tiles_y - 1) & (band == bands - 1))
-        def _():
-            put(north + column, tile_value())
-
-        @pl.when((tile_y > 0) & (me == (shift - 1) % bands))
-        def _():
-            put(south + column, end_value())
-
-        @pl.when((tile_y < tiles_y - 1) & (me == shift))
-        def _():
-            put(north + column, end_value())
-
+    slots = edge_slots(bands)
     for shift in range(bands):
         band = lax.rem(me - shift + bands, bands)
-        for n, point in enumerate(POINTS):
-            if shift == 0:
-                here, there, k = own, own_end, n
-            elif n < 2:
-                here, there, k = other_side[shift - 1], ends_side[shift - 1], n
-            else:
-                here, there, k = other_mid[shift - 1], ends_mid[shift - 1], n - 2
+        for n, point in enumerate(SIDES):
             put_ends(
+                t_ref,
+                slots[0, point + 1],
+                slots[bands + 1, point + 1],
+                bands,
+                tiles_y,
                 shift,
-                point + 1,
-                lambda here=here, k=k: here[k],
-                lambda there=there, k=k: there[k],
+                lambda shift=shift, n=n: rows[shift][n],
+                lambda shift=shift, n=n: ends[shift][n],
             )
-        for side, column in enumerate((0, CGX + 1)):
-            put(slots[1, 0] + 2 * band + side, row_sides[side][shift])
+        for side in (0, 1):
+            put(t_ref, slots[1, 0] + 2 * band + side, sides[side][shift])
+    add_terms(x_ref, t_ref, before_ref, out_ref, bands, slots)
+
+
+def corner_kernel(bands, tiles_y, spacing, depth, *refs):
+    edge_ref = refs[0]
+    rows, ends = refs[1 : 1 + bands], refs[1 + bands : 1 + 2 * bands]
+    left_ref, right_ref, t_ref = refs[1 + 2 * bands :]
+    members = edge_ref.shape[3]
+    part = left_ref.shape[2]
+    for shift in range(bands):
+        for n in (0, 1):
             put_ends(
+                t_ref,
+                n,
+                2 + n,
+                bands,
+                tiles_y,
                 shift,
-                column,
-                lambda side=side: row_sides[side][shift],
-                lambda side=side: end_sides[side][shift],
+                lambda shift=shift, n=n: rows[shift][n],
+                lambda shift=shift, n=n: ends[shift][n],
+            )
+    half, tall = spacing // 2, depth // 2
+    i = lax.broadcasted_iota(jnp.int32, (half, 1, 1), 0).astype(F32) + 0.5
+    j = lax.broadcasted_iota(jnp.int32, (1, tall, 1), 1).astype(F32) + 0.5
+    along_x = (i * (1.0 / spacing), 0.5 - i * (1.0 / spacing))
+    along_y = (0.5 - j * (1.0 / depth), j * (1.0 / depth))
+    for n, out_ref in enumerate((left_ref, right_ref)):
+        for end in (0, 1):
+            cells = slice(end * tall, (end + 1) * tall)
+            first = 0 if n else half
+            x0 = edge_ref[0, first : first + half, cells, :].reshape(half * tall, members)
+            x1 = edge_ref[1, first : first + half, cells, :].reshape(half * tall, members)
+            slot = 2 * end + n
+            product = dot_nt(
+                jnp.concatenate([x0, x0, x1], axis=1),
+                jnp.concatenate([t_ref[slot, 0], t_ref[slot, 1], t_ref[slot, 0]], axis=1),
+            )
+            out_ref[:, cells, :] = (
+                along_x[n] * along_y[end] * product.reshape(half, tall, part)
+            )
+
+
+def corners(bands, tiles_y, spacing, depth, edge, rows, ends):
+    part, members = rows[0].shape[1:]
+    vmem = pl.BlockSpec(memory_space=pltpu.VMEM)
+    shape = jax.ShapeDtypeStruct((spacing // 2, depth, part), F32)
+    return pl.pallas_call(
+        functools.partial(corner_kernel, bands, tiles_y, spacing, depth),
+        out_shape=[shape] * 2,
+        in_specs=[vmem] * (1 + 2 * bands),
+        out_specs=[vmem] * 2,
+        scratch_shapes=[pltpu.VMEM((4, 2, part, members), BF16)],
+        compiler_params=pltpu.CompilerParams(vmem_limit_bytes=16 * MIB),
+        cost_estimate=pl.CostEstimate(
+            flops=12 * spacing * depth * part * members,
+            bytes_accessed=16 * part * members,
+            transcendentals=0,
+        ),
+        name="corners",
+    )(edge, *rows, *ends)
+
+
+def last_kernel(bands, tiles_y, *refs):
+    refs = list(refs)
+
+    def take(n):
+        taken, refs[:n] = refs[:n], []
+        return taken
+
+    x_ref, before_ref = take(2)
+    rows, ends, given = take(bands), take(bands), take(2)
+    out_ref, t_ref = refs
+    slots = last_slots(bands)
+    for shift in range(bands):
+        for n in range(CGX - 2):
+            k = 2 + n if shift == 0 else n
+            put_ends(
+                t_ref,
+                slots[0, 2 + n],
+                slots[bands + 1, 2 + n],
+                bands,
+                tiles_y,
+                shift,
+                lambda shift=shift, k=k: rows[shift][k],
+                lambda shift=shift, k=k: ends[shift][k],
             )
     add_terms(x_ref, t_ref, before_ref, out_ref, bands, slots)
+    width, height, _ = out_ref.shape
+    half, depth, _ = given[0].shape
+    for ref, first in zip(given, (0, width - half)):
+        for start, cells in ((0, 0), (depth // 2, height - depth // 2)):
+            place = slice(cells, cells + depth // 2)
+            out_ref[first : first + half, place, :] = (
+                before_ref[first : first + half, place, :]
+                + ref[:, start : start + depth // 2, :]
+            )
 
 
 def apply_terms(kernel, x, before, operands, slots, flops):
@@ -407,16 +513,34 @@
         piece = lax.dynamic_slice_in_dim(
             anomalies, lax.rem(me + shift, bands) * slots, slots, axis=1
         )
-        others.append(shifted(piece, "mem", shift))
+        others.append(piece)
+    anomalies, others = lax.optimization_barrier((anomalies, others))
+    others = [shifted(piece, "mem", s) for s, piece in enumerate(others, 1)]
     own = lax.dynamic_slice_in_dim(anomalies, me * slots, slots, axis=1)
     tile = background.transpose(1, 2, 0)
-    cells = [tile]
-    for shift in range(1, bands):
-        cells.append(shifted(tile, "mem", shift))
-    if part % 128:
-        order = lax.rem(me - jnp.arange(bands) + bands, bands)
-        cells = jnp.take(jnp.stack(cells, axis=2), order, axis=2)
-        cells = [cells.reshape(cells.shape[:2] + (members,))]
+    width, height = tile.shape[:2]
+    spacing, depth = width // CGX, height // bands
+    ends_y = jnp.concatenate([tile[:, : depth // 2], tile[:, height - depth // 2 :]], axis=1)
+    edge = jnp.concatenate(
+        [
+            shifted(ends_y[: spacing // 2], "gx", -1),
+            shifted(ends_y[width - spacing // 2 :], "gx", 1),
+        ],
+        axis=0,
+    )
+
+    def gathered(array):
+        blocks = [array]
+        for shift in range(1, bands):
+            blocks.append(shifted(array, "mem", shift))
+        if part % 128:
+            order = lax.rem(me - jnp.arange(bands) + bands, bands)
+            blocks = jnp.take(jnp.stack(blocks, axis=2), order, axis=2)
+            blocks = [blocks.reshape(blocks.shape[:2] + (members,))]
+        return blocks
+
+    cells = gathered(tile)
+    edges = gathered(edge)
     solved = solve(
         POINTS,
         tally.reshape(1),
@@ -428,19 +552,19 @@
     )
     row = solved[0]
     other_side = [shifted(solved[2 * s - 1], "mem", s) for s in range(1, bands)]
+    other_mid = [shifted(solved[2 * s], "mem", s) for s in range(1, bands)]
     own_end = to_next_tile(row, 0)
-    other_mid = [shifted(solved[2 * s], "mem", s) for s in range(1, bands)]
     ends_side = [to_next_tile(other_side[s - 1], s) for s in range(1, bands)]
     row_sides = [
         shifted(jnp.stack([row[n]] + [array[n] for array in other_side]), "gx", by)
         for n, by in ((1, 1), (0, -1))
     ]
     ends_mid = [to_next_tile(other_mid[s - 1], s) for s in range(1, bands)]
-    end_sides = [
-        shifted(jnp.stack([own_end[n]] + [array[n] for array in ends_side]), "gx", by)
-        for n, by in ((1, 1), (0, -1))
-    ]
-    x, mean = prepare(cells, part)
+    x, mean, edge = prepare(cells, edges, part)
+    left, right = corners(
+        bands, tiles_y, spacing, depth, edge, [row] + other_side, [own_end] + ends_side
+    )
+    given = [shifted(right, "gx", 1), shifted(left, "gx", -1)]
     operands = [row]
     for side, mid in zip(other_side, other_mid):
         operands += [side, mid]
@@ -454,19 +578,20 @@
         3 * work,
     )
     result = apply_terms(
-        functools.partial(outer_kernel, bands, tiles_y),
+        functools.partial(edge_kernel, bands, tiles_y),
         x,
         result,
-        [row]
-        + ends_side
-        + ends_mid
-        + other_side
-        + other_mid
-        + [own_end]
-        + row_sides
-        + end_sides,
-        outer_slots(bands),
+        [row] + other_side + [own_end] + ends_side + row_sides,
+        edge_slots(bands),
         work,
+    )
+    result = apply_terms(
+        functools.partial(last_kernel, bands, tiles_y),
+        x,
+        result,
+        [row] + other_mid + [own_end] + ends_mid + given,
+        last_slots(bands),
+        work // 2,
     )
     return result.transpose(2, 0, 1)
 

time: 86.5 us -> 66.9 us (0.77)
  waiting for transfers between devices: 39.9 us -> 18.3 us
  starting transfers between devices: 19.3 us -> 21.5 us
  Pallas kernels: 24 us -> 22 us
  local copies, waits for them, and re-layouts: 2.24 us -> 4.01 us
    ppermute x8 -> x11, waiting for transfers between devices: 38.5 us -> 18.3 us  [shifted(): lax.ppermute(array, axis, [(i, (i + by) % size) for i in range(size)])]
    unnamed x10 -> x13, local copies, waits for them, and re-layouts: 0.21 us -> 2.81 us
    pallas_call x1, Pallas kernels: 18 us -> 15.5 us  [solve(): pl.pallas_call(functools.partial(solve_kernel, points, bands), out_shape=...]
    dynamic_slice x1, local copies, waits for them, and re-layouts: 1.96 us -> 0.03 us  [analysis(): lax.dynamic_slice_in_dim(anomalies, lax.rem(me + shift, bands) * slots, s...]
    ppermute x8 -> x11, starting transfers between devices: 10.8 us -> 12.3 us  [shifted(): lax.ppermute(array, axis, [(i, (i + by) % size) for i in range(size)])]
    ppermute x3, waiting for transfers between devices: 1.43 us -> 0.01 us  [to_next_tile(): return lax.ppermute(array, ('mem', 'gy'), pairs)]
    dynamic_slice x0 -> x1, local copies, waits for them, and re-layouts: none -> 1.09 us  [analysis(): own = lax.dynamic_slice_in_dim(anomalies, me * slots, slots, axis=1)]
    pallas_call x2 -> x3, Pallas kernels: 5.07 us -> 4.93 us  [apply_terms(): pl.pallas_call(kernel, out_shape=jax.ShapeDtypeStruct((width, height, par...]
  transfers between devices with their start and end apart: 11 -> 14, of which waited for: 6 -> 4; matrix products, arithmetic and copies ran while one was open for 0% -> 2% of each run, Pallas kernels for 3% -> 30%
where the time goes in v2:
time: 66.9 us; the launch traced here: 66.7 us
  Pallas kernels  22 us (33%)
  starting transfers between devices  21.5 us (32%)
  waiting for transfers between devices  18.3 us (27%)
  local copies, waits for them, and re-layouts  4.01 us (6%)
  between operations  0.87 us (1%)
    ppermute x11, waiting for transfers between devices, shifted(): lax.ppermute(array, axis, [(i, (i + by) % size) for i in range(size)])  18.3 us
    pallas_call x1, Pallas kernels, solve(): pl.pallas_call(functools.partial(solve_kernel, points, bands), out_shape=...  15.5 us
    ppermute x11, starting transfers between devices, shifted(): lax.ppermute(array, axis, [(i, (i + by) % size) for i in range(size)])  12.3 us
    ppermute x3, starting transfers between devices, to_next_tile(): return lax.ppermute(array, ('mem', 'gy'), pairs)  9.15 us
    pallas_call x3, Pallas kernels, apply_terms(): pl.pallas_call(kernel, out_shape=jax.ShapeDtypeStruct((width, height, par...  4.93 us
    unnamed x13, local copies, waits for them, and re-layouts  2.81 us
  transfers between devices with their start and end apart: 14, of which 4 were waited for; matrix products, arithmetic and copies ran while one was open for 2% of the time, Pallas kernels for 30%

profile of v2, /device:TPU:0, one launch (start us, length us, event | category | flops | bytes accessed | tf_op | source)
XLA Modules:
  0.0 66.7 jit_solution(17147799913025119092)
XLA Ops:
  0.0 2.7 %copy.11 = f32[128,1,1,2048]{3,0,1,2:T(8,128)} copy(f32[128,1,1,2048]{3,2,1,0:T(1,128)} %param.7) | data formatting | bytes 2097152
  2.7 0.0 copy-start.1
  2.7 0.0 copy-start.2
  2.8 0.0 copy-start.3
  2.8 0.1 copy.12
  2.9 3.1 %collective-permute-start.4 = (f32[128,1024]{1,0:T(8,128)S(1)}, f32[128,1024]{1,0:T(8,128)S(1)}, u32[]{:S(2)}, u32[]{:S(2)}) collective-permute-start(f32[128,1024]{1,0:T(8,128)S(1)} %bitcast.20), channel_id=1, source_target_pairs={{0,16},{16,0},{1,17},{17,1},{2,18},{18,2},{3,19},{19,3},{4,20},{20... | collective-permute-start | bytes 1572872 | tf_op jit(solution)/shard_map/ppermute | solution.py:491
  5.9 0.1 collective-permute-start
  6.1 0.8 %collective-permute-start.1 = (f32[4,32,128]{2,1,0:T(8,128)S(1)}, f32[4,32,128]{2,1,0:T(8,128)S(1)}, u32[]{:S(2)}, u32[]{:S(2)}) collective-permute-start(f32[4,32,128]{2,1,0:T(8,128)S(1)} %get-tuple-element.30), channel_id=1, source_target_pairs={{0,12},{4,0},{8,4},{12,8},{1,13},{5,1},{9,5},{13,9},{2,14},{6,2},{... | collective-permute-start | bytes 196616 | tf_op jit(solution)/shard_map/ppermute | solution.py:491
  6.9 0.0 collective-permute-start.2
  7.6 1.1 %constant_dynamic-slice_fusion.own_ref = f32[128,1024]{1,0:T(8,128)S(1)} fusion(f32[128,2048]{1,0:T(8,128)} %bitcast.19, s32[]{:T(128)S(6)} %select_n.7), kind=kLoop, calls=%fused_computation.8 | loop fusion | bytes 1048580 | tf_op jit(solution)/shard_map/dynamic_slice | solution.py:519
  8.7 0.2 collective-permute-done.1
  8.8 9.9 %collective-permute-done.4.refs_0_ = f32[128,1024]{1,0:T(8,128)S(1)} collective-permute-done((f32[128,1024]{1,0:T(8,128)S(1)}, f32[128,1024]{1,0:T(8,128)S(1)}, u32[]{:S(2)}, u32[]{:S(2)}) %collective-permute-start.4) | collective-permute-done | bytes 524320 | tf_op jit(solution)/shard_map/ppermute | solution.py:491
  18.7 15.5 %solve.1 = (f32[4,128,256]{2,1,0:T(8,128)S(1)}, f32[2,128,256]{2,1,0:T(8,128)S(1)}, f32[2,128,256]{2,1,0:T(8,128)S(1)}) custom-call(s32[1]{0:T(128)} %bitcast.12.live_ref, f32[128,1024]{1,0:T(8,128)S(1)} %constant_dynamic-slice_fusion.own_ref, f32[128,1024]{1,0:T(8,128)S(1)} %collective-permute-done.4.refs_0_, f32[1,1024]{1,0:T(1,128)S(1)} %bitcast.16, ...), custom_call_target="tpu_custom_call" | custom-call | flops 11140071424 | bytes 2097152 | tf_op jit(solution)/shard_map/solve/pallas_call | solution.py:165
  34.2 2.1 %collective-permute-start.5 = (f32[2,128,256]{2,1,0:T(8,128)S(1)}, f32[2,128,256]{2,1,0:T(8,128)S(1)}, u32[]{:S(2)}, u32[]{:S(2)}) collective-permute-start(f32[2,128,256]{2,1,0:T(8,128)S(1)} %get-tuple-element.20), channel_id=1, source_target_pairs={{0,16},{16,0},{1,17},{17,1},{2,18},{18,2},{3,19},{19,3},{4,20},{20... | collective-permute-start | bytes 786440 | tf_op jit(solution)/shard_map/ppermute | solution.py:491
  36.3 0.1 collective-permute-start.3
  36.4 1.3 %collective-permute-start.7 = (f32[4,128,256]{2,1,0:T(8,128)S(1)}, f32[4,128,256]{2,1,0:T(8,128)S(1)}, u32[]{:S(2)}, u32[]{:S(2)}) collective-permute-start(f32[4,128,256]{2,1,0:T(8,128)S(1)} %get-tuple-element.19.refs_2_.refs_1_), channel_id=1, source_target_pairs={{16,17},{17,18},{18,19},{1,0},{2,1},{3,2},{20,21},{21,22},{22,23},... | collective-permute-start | bytes 1572872 | tf_op jit(solution)/shard_map/ppermute | solution.py:500
  37.7 4.3 %collective-permute-start.6 = (f32[2,128,256]{2,1,0:T(8,128)S(1)}, f32[2,128,256]{2,1,0:T(8,128)S(1)}, u32[]{:S(2)}, u32[]{:S(2)}) collective-permute-start(f32[2,128,256]{2,1,0:T(8,128)S(1)} %get-tuple-element.21), channel_id=1, source_target_pairs={{0,16},{16,0},{1,17},{17,1},{2,18},{18,2},{3,19},{19,3},{4,20},{20... | collective-permute-start | bytes 786440 | tf_op jit(solution)/shard_map/ppermute | solution.py:491
  42.0 4.8 %collective-permute-done.5.refs_3_.refs_2_ = f32[2,128,256]{2,1,0:T(8,128)S(1)} collective-permute-done((f32[2,128,256]{2,1,0:T(8,128)S(1)}, f32[2,128,256]{2,1,0:T(8,128)S(1)}, u32[]{:S(2)}, u32[]{:S(2)}) %collective-permute-start.5) | collective-permute-done | bytes 262176 | tf_op jit(solution)/shard_map/ppermute | solution.py:491
  46.8 4.0 %collective-permute-start.8 = (f32[2,128,256]{2,1,0:T(8,128)S(1)}, f32[2,128,256]{2,1,0:T(8,128)S(1)}, u32[]{:S(2)}, u32[]{:S(2)}) collective-permute-start(f32[2,128,256]{2,1,0:T(8,128)S(1)} %collective-permute-done.5.refs_3_.refs_2_), channel_id=1, source_target_pairs={{0,1},{1,2},{2,3},{17,16},{18,17},{19,18},{4,5},{5,6},{6,7},{21,20... | collective-permute-start | bytes 786440 | tf_op jit(solution)/shard_map/ppermute | solution.py:500
  50.9 0.0 collective-permute-done.3.refs_3_
  50.9 0.1 collective-permute-start.10
  50.9 3.4 %collective-permute-done.6.refs_4_.refs_3_ = f32[2,128,256]{2,1,0:T(8,128)S(1)} collective-permute-done((f32[2,128,256]{2,1,0:T(8,128)S(1)}, f32[2,128,256]{2,1,0:T(8,128)S(1)}, u32[]{:S(2)}, u32[]{:S(2)}) %collective-permute-start.6) | collective-permute-done | bytes 262176 | tf_op jit(solution)/shard_map/ppermute | solution.py:491
  54.4 3.9 %collective-permute-start.11 = (f32[2,128,256]{2,1,0:T(8,128)S(1)}, f32[2,128,256]{2,1,0:T(8,128)S(1)}, u32[]{:S(2)}, u32[]{:S(2)}) collective-permute-start(f32[2,128,256]{2,1,0:T(8,128)S(1)} %collective-permute-done.6.refs_4_.refs_3_), channel_id=1, source_target_pairs={{0,1},{1,2},{2,3},{17,16},{18,17},{19,18},{4,5},{5,6},{6,7},{21,20... | collective-permute-start | bytes 786440 | tf_op jit(solution)/shard_map/ppermute | solution.py:500
  58.3 1.0 %prepare.1 = (bf16[2,32,64,256]{3,2,1,0:T(8,128)(2,1)S(1)}, f32[32,64,128]{2,1,0:T(8,128)S(1)}, bf16[2,8,32,256]{3,2,1,0:T(8,128)(2,1)S(1)}) custom-call(f32[32,64,128]{2,1,0:T(8,128)S(1)} %bitcast.15, f32[32,64,128]{2,1,0:T(8,128)S(1)} %collective-permute-done.refs_1_, f32[8,32,128]{2,1,0:T(8,128)S(1)} %constant_dynamic-update-slice_fusion.refs_2_, ...), custom_call_target="tpu_custom_call" | custom-call | flops 4194304 | bytes 4194304 | tf_op jit(solution)/shard_map/prepare/pallas_call | solution.py:218
  59.3 0.0 collective-permute-done.7.refs_4_.refs_3_
  59.3 0.5 corners.1
  59.9 1.4 %collective-permute-start.12 = (f32[4,32,128]{2,1,0:T(8,128)S(1)}, f32[4,32,128]{2,1,0:T(8,128)S(1)}, u32[]{:S(2)}, u32[]{:S(2)}) collective-permute-start(f32[4,32,128]{2,1,0:T(8,128)S(1)} %get-tuple-element.23), channel_id=1, source_target_pairs={{0,4},{4,8},{8,12},{12,0},{1,5},{5,9},{9,13},{13,1},{2,6},{6,10},{... | collective-permute-start | bytes 196616 | tf_op jit(solution)/shard_map/ppermute | solution.py:491
  61.2 0.4 collective-permute-start.13
  61.7 2.0 %shard_map.64.refs_1_ = f32[32,64,128]{2,1,0:T(8,128)S(1)} custom-call(bf16[2,32,64,256]{3,2,1,0:T(8,128)(2,1)S(1)} %get-tuple-element.15.refs_0_, f32[32,64,128]{2,1,0:T(8,128)S(1)} %get-tuple-element.16.refs_1_, f32[4,128,256]{2,1,0:T(8,128)S(1)} %get-tuple-element.19.refs_2_.refs_1_, f32[2,128,256]{2,1,0:T(8,128)S(1)} %collective-permute-done.5.refs_3_.refs_2_, ...), custom_call_target="tpu_custom_call" | custom-call | flops 1207959552 | bytes 5242880 | tf_op jit(solution)/shard_map/pallas_call | solution.py:474
  63.7 0.0 collective-permute-done.10.refs_7_
  63.7 1.3 %shard_map.65.refs_1_ = f32[32,64,128]{2,1,0:T(8,128)S(1)} custom-call(bf16[2,32,64,256]{3,2,1,0:T(8,128)(2,1)S(1)} %get-tuple-element.15.refs_0_, f32[32,64,128]{2,1,0:T(8,128)S(1)} %shard_map.64.refs_1_, f32[4,128,256]{2,1,0:T(8,128)S(1)} %get-tuple-element.19.refs_2_.refs_1_, f32[2,128,256]{2,1,0:T(8,128)S(1)} %collective-permute-done.5.refs_3_.refs_2_, ...), custom_call_target="tpu_custom_call" | custom-call | flops 402653184 | bytes 5242880 | tf_op jit(solution)/shard_map/pallas_call | solution.py:474
  65.0 1.7 %shard_map.66 = f32[32,64,128]{2,1,0:T(8,128)} custom-call(bf16[2,32,64,256]{3,2,1,0:T(8,128)(2,1)S(1)} %get-tuple-element.15.refs_0_, f32[32,64,128]{2,1,0:T(8,128)S(1)} %shard_map.65.refs_1_, f32[4,128,256]{2,1,0:T(8,128)S(1)} %get-tuple-element.19.refs_2_.refs_1_, f32[2,128,256]{2,1,0:T(8,128)S(1)} %collective-permute-done.6.refs_4_.refs_3_, ...), custom_call_target="tpu_custom_call" | custom-call | flops 201326592 | bytes 5242880 | tf_op jit(solution)/shard_map/pallas_call | solution.py:474
  (24 shorter events, 0.2 us)
Async XLA Ops:
  0.0 2.7 %copy-start.4 = (f32[128,1,1,2048]{3,2,1,0:T(1,128)S(1)}, f32[128,1,1,2048]{3,2,1,0:T(1,128)}, u32[]{:S(2)}) copy-start(f32[128,1,1,2048]{3,2,1,0:T(1,128)} %param.7) | copy-start | bytes 3145732
  0.0 5.9 %copy-start = (f32[128,32,64]{0,2,1:T(8,128)S(1)}, f32[128,32,64]{0,2,1:T(8,128)}, u32[]{:S(2)}) copy-start(f32[128,32,64]{0,2,1:T(8,128)} %param.6) | copy-start | bytes 3145732
  2.7 16.0 %copy-start.1 = (f32[1,1,1,1024]{3,2,1,0:T(1,128)S(1)}, f32[1,1,1,1024]{3,2,1,0:T(1,128)}, u32[]{:S(2)}) copy-start(f32[1,1,1,1024]{3,2,1,0:T(1,128)} %param.8) | copy-start | bytes 12292
  2.7 16.0 %copy-start.2 = (f32[1,1,1,1024]{3,2,1,0:T(1,128)S(1)}, f32[1,1,1,1024]{3,2,1,0:T(1,128)}, u32[]{:S(2)}) copy-start(f32[1,1,1,1024]{3,2,1,0:T(1,128)} %param.9) | copy-start | bytes 12292
  2.8 16.0 %copy-start.3 = (s32[1,1,1,1024]{3,2,1,0:T(1,128)S(1)}, s32[1,1,1,1024]{3,2,1,0:T(1,128)}, u32[]{:S(2)}) copy-start(s32[1,1,1,1024]{3,2,1,0:T(1,128)} %param.10) | copy-start | bytes 12292
  2.9 15.8 %collective-permute-start.4 = (f32[128,1024]{1,0:T(8,128)S(1)}, f32[128,1024]{1,0:T(8,128)S(1)}, u32[]{:S(2)}, u32[]{:S(2)}) collective-permute-start(f32[128,1024]{1,0:T(8,128)S(1)} %bitcast.20), channel_id=1, source_target_pairs={{0,16},{16,0},{1,17},{17,1},{2,18},{18,2},{3,19},{19,3},{4,20},{20... | collective-permute-start | bytes 1572872 | tf_op jit(solution)/shard_map/ppermute | solution.py:491
  5.9 48.4 %collective-permute-start = (f32[32,64,128]{2,1,0:T(8,128)S(1)}, f32[32,64,128]{2,1,0:T(8,128)S(1)}, u32[]{:S(2)}, u32[]{:S(2)}) collective-permute-start(f32[32,64,128]{2,1,0:T(8,128)S(1)} %bitcast.13), channel_id=1, source_target_pairs={{0,16},{16,0},{1,17},{17,1},{2,18},{18,2},{3,19},{19,3},{4,20},{20... | collective-permute-start | bytes 3145736 | tf_op jit(solution)/shard_map/ppermute | solution.py:491
  6.1 2.7 %collective-permute-start.1 = (f32[4,32,128]{2,1,0:T(8,128)S(1)}, f32[4,32,128]{2,1,0:T(8,128)S(1)}, u32[]{:S(2)}, u32[]{:S(2)}) collective-permute-start(f32[4,32,128]{2,1,0:T(8,128)S(1)} %get-tuple-element.30), channel_id=1, source_target_pairs={{0,12},{4,0},{8,4},{12,8},{1,13},{5,1},{9,5},{13,9},{2,14},{6,2},{... | collective-permute-start | bytes 196616 | tf_op jit(solution)/shard_map/ppermute | solution.py:491
  6.9 29.4 %collective-permute-start.2 = (f32[4,32,128]{2,1,0:T(8,128)S(1)}, f32[4,32,128]{2,1,0:T(8,128)S(1)}, u32[]{:S(2)}, u32[]{:S(2)}) collective-permute-start(f32[4,32,128]{2,1,0:T(8,128)S(1)} %get-tuple-element.29), channel_id=1, source_target_pairs={{0,4},{4,8},{8,12},{12,0},{1,5},{5,9},{9,13},{13,1},{2,6},{6,10},{... | collective-permute-start | bytes 196616 | tf_op jit(solution)/shard_map/ppermute | solution.py:491
  34.2 12.6 %collective-permute-start.5 = (f32[2,128,256]{2,1,0:T(8,128)S(1)}, f32[2,128,256]{2,1,0:T(8,128)S(1)}, u32[]{:S(2)}, u32[]{:S(2)}) collective-permute-start(f32[2,128,256]{2,1,0:T(8,128)S(1)} %get-tuple-element.20), channel_id=1, source_target_pairs={{0,16},{16,0},{1,17},{17,1},{2,18},{18,2},{3,19},{19,3},{4,20},{20... | collective-permute-start | bytes 786440 | tf_op jit(solution)/shard_map/ppermute | solution.py:491
  36.3 14.5 %collective-permute-start.3 = (f32[8,32,128]{2,1,0:T(8,128)S(1)}, f32[8,32,128]{2,1,0:T(8,128)S(1)}, u32[]{:S(2)}, u32[]{:S(2)}) collective-permute-start(f32[8,32,128]{2,1,0:T(8,128)S(1)} %constant_dynamic-update-slice_fusion.refs_2_), channel_id=1, source_target_pairs={{0,16},{16,0},{1,17},{17,1},{2,18},{18,2},{3,19},{19,3},{4,20},{20... | collective-permute-start | bytes 393224 | tf_op jit(solution)/shard_map/ppermute | solution.py:491
  36.4 22.9 %collective-permute-start.7 = (f32[4,128,256]{2,1,0:T(8,128)S(1)}, f32[4,128,256]{2,1,0:T(8,128)S(1)}, u32[]{:S(2)}, u32[]{:S(2)}) collective-permute-start(f32[4,128,256]{2,1,0:T(8,128)S(1)} %get-tuple-element.19.refs_2_.refs_1_), channel_id=1, source_target_pairs={{16,17},{17,18},{18,19},{1,0},{2,1},{3,2},{20,21},{21,22},{22,23},... | collective-permute-start | bytes 1572872 | tf_op jit(solution)/shard_map/ppermute | solution.py:500
  37.7 16.7 %collective-permute-start.6 = (f32[2,128,256]{2,1,0:T(8,128)S(1)}, f32[2,128,256]{2,1,0:T(8,128)S(1)}, u32[]{:S(2)}, u32[]{:S(2)}) collective-permute-start(f32[2,128,256]{2,1,0:T(8,128)S(1)} %get-tuple-element.21), channel_id=1, source_target_pairs={{0,16},{16,0},{1,17},{17,1},{2,18},{18,2},{3,19},{19,3},{4,20},{20... | collective-permute-start | bytes 786440 | tf_op jit(solution)/shard_map/ppermute | solution.py:491
  46.8 12.5 %collective-permute-start.8 = (f32[2,128,256]{2,1,0:T(8,128)S(1)}, f32[2,128,256]{2,1,0:T(8,128)S(1)}, u32[]{:S(2)}, u32[]{:S(2)}) collective-permute-start(f32[2,128,256]{2,1,0:T(8,128)S(1)} %collective-permute-done.5.refs_3_.refs_2_), channel_id=1, source_target_pairs={{0,1},{1,2},{2,3},{17,16},{18,17},{19,18},{4,5},{5,6},{6,7},{21,20... | collective-permute-start | bytes 786440 | tf_op jit(solution)/shard_map/ppermute | solution.py:500
  50.9 12.8 %collective-permute-start.10 = (f32[2,128,256]{2,1,0:T(8,128)S(1)}, f32[2,128,256]{2,1,0:T(8,128)S(1)}, u32[]{:S(2)}, u32[]{:S(2)}) collective-permute-start(f32[2,128,256]{2,1,0:T(8,128)S(1)} %pad_maximum_fusion.1), channel_id=1, source_target_pairs={{0,12},{4,0},{8,4},{12,8},{1,13},{5,1},{9,5},{13,9},{2,14},{6,2},{... | collective-permute-start | bytes 786440 | tf_op jit(solution)/shard_map/ppermute | solution.py:491
  54.4 9.3 %collective-permute-start.9 = (f32[2,128,256]{2,1,0:T(8,128)S(1)}, f32[2,128,256]{2,1,0:T(8,128)S(1)}, u32[]{:S(2)}, u32[]{:S(2)}) collective-permute-start(f32[2,128,256]{2,1,0:T(8,128)S(1)} %pad_maximum_fusion), channel_id=1, source_target_pairs={{0,4},{4,8},{8,12},{12,0},{1,5},{5,9},{9,13},{13,1},{2,6},{6,10},{... | collective-permute-start | bytes 786440 | tf_op jit(solution)/shard_map/ppermute | solution.py:491
  54.4 10.6 %collective-permute-start.11 = (f32[2,128,256]{2,1,0:T(8,128)S(1)}, f32[2,128,256]{2,1,0:T(8,128)S(1)}, u32[]{:S(2)}, u32[]{:S(2)}) collective-permute-start(f32[2,128,256]{2,1,0:T(8,128)S(1)} %collective-permute-done.6.refs_4_.refs_3_), channel_id=1, source_target_pairs={{0,1},{1,2},{2,3},{17,16},{18,17},{19,18},{4,5},{5,6},{6,7},{21,20... | collective-permute-start | bytes 786440 | tf_op jit(solution)/shard_map/ppermute | solution.py:500
  59.9 5.1 %collective-permute-start.12 = (f32[4,32,128]{2,1,0:T(8,128)S(1)}, f32[4,32,128]{2,1,0:T(8,128)S(1)}, u32[]{:S(2)}, u32[]{:S(2)}) collective-permute-start(f32[4,32,128]{2,1,0:T(8,128)S(1)} %get-tuple-element.23), channel_id=1, source_target_pairs={{0,4},{4,8},{8,12},{12,0},{1,5},{5,9},{9,13},{13,1},{2,6},{6,10},{... | collective-permute-start | bytes 196616 | tf_op jit(solution)/shard_map/ppermute | solution.py:491
  61.2 3.7 %collective-permute-start.13 = (f32[4,32,128]{2,1,0:T(8,128)S(1)}, f32[4,32,128]{2,1,0:T(8,128)S(1)}, u32[]{:S(2)}, u32[]{:S(2)}) collective-permute-start(f32[4,32,128]{2,1,0:T(8,128)S(1)} %get-tuple-element.24), channel_id=1, source_target_pairs={{0,12},{4,0},{8,4},{12,8},{1,13},{5,1},{9,5},{13,9},{2,14},{6,2},{... | collective-permute-start | bytes 196616 | tf_op jit(solution)/shard_map/ppermute | solution.py:491

commit v3 on v2

--- a/solution.py
+++ b/solution.py
@@ -190,28 +190,25 @@
 
 
 def prepare_kernel(blocks, *refs):
+    cells, (x_ref, mean_ref) = refs[:blocks], refs[blocks:]
     me = lax.axis_index("mem")
-    cells, edges = refs[:blocks], refs[blocks : 2 * blocks]
-    x_ref, mean_ref, edge_ref = refs[2 * blocks :]
     members = x_ref.shape[3]
     strip = members // blocks
-    for pieces, to_ref in ((cells, x_ref), (edges, edge_ref)):
-        total = sum(jnp.sum(ref[...], axis=2, keepdims=True) for ref in pieces)
-        mean = total * (1.0 / members)
-        if to_ref is x_ref:
-            mean_ref[...] = jnp.broadcast_to(mean, mean_ref.shape)
-        for shift, ref in enumerate(pieces):
-            x0, x1 = split2(ref[...] - mean)
-            if blocks == 1:
-                to_ref[0], to_ref[1] = x0, x1
-            else:
-                owner = lax.rem(me - shift + blocks, blocks)
-                place = pl.ds(pl.multiple_of(owner * strip, strip), strip)
-                to_ref[0, :, :, place] = x0
-                to_ref[1, :, :, place] = x1
-
-
-def prepare(cells, edges, part):
+    total = sum(jnp.sum(ref[...], axis=2, keepdims=True) for ref in cells)
+    mean = total * (1.0 / members)
+    mean_ref[...] = jnp.broadcast_to(mean, mean_ref.shape)
+    for shift, ref in enumerate(cells):
+        x0, x1 = split2(ref[...] - mean)
+        if blocks == 1:
+            x_ref[0], x_ref[1] = x0, x1
+        else:
+            owner = lax.rem(me - shift + blocks, blocks)
+            place = pl.ds(pl.multiple_of(owner * strip, strip), strip)
+            x_ref[0, :, :, place] = x0
+            x_ref[1, :, :, place] = x1
+
+
+def prepare(cells, part):
     width, height, strip = cells[0].shape
     members = strip * len(cells)
     vmem = pl.BlockSpec(memory_space=pltpu.VMEM)
@@ -220,10 +217,9 @@
         out_shape=[
             jax.ShapeDtypeStruct((2, width, height, members), BF16),
             jax.ShapeDtypeStruct((width, height, part), F32),
-            jax.ShapeDtypeStruct((2,) + edges[0].shape[:2] + (members,), BF16),
         ],
-        in_specs=[vmem] * (2 * len(cells)),
-        out_specs=[vmem] * 3,
+        in_specs=[vmem] * len(cells),
+        out_specs=[vmem] * 2,
         compiler_params=pltpu.CompilerParams(
             vmem_limit_bytes=16 * width * height * members + 8 * MIB
         ),
@@ -232,13 +228,23 @@
             bytes_accessed=8 * width * height * members,
             transcendentals=0,
         ),
-        name="prepare",
-    )(*cells, *edges)
-
-
-def add_terms(x_ref, t_ref, before_ref, out_ref, bands, mine):
-    width, height, part = out_ref.shape
-    members = x_ref.shape[3]
+    )(*cells)
+
+
+def column_intervals(width):
+    spacing = width // CGX
+    edges = [0] + [spacing * c + spacing // 2 for c in range(CGX)] + [width]
+    return list(zip(edges[:-1], edges[1:]))
+
+
+def window(refs, first):
+    return [(ref, first - start) for ref, start in refs if start <= first][-1]
+
+
+def add_terms(geometry, intervals, x_refs, t_ref, before_refs, out_refs, mine):
+    width, height, bands = geometry
+    part = out_refs[0][0].shape[2]
+    members = x_refs[0][0].shape[3]
     spacing = width // CGX
     depth = height // bands
     for v in range(bands + 1):
@@ -249,32 +255,31 @@
         )
         upper = j * (1.0 / depth)
         along_y = (1.0 - upper, upper)
-        for c in range(CGX + 1):
-            i0 = max(spacing * c - spacing // 2, 0)
-            i1 = min(spacing * c + spacing // 2, width)
+        for c in intervals:
+            i0, i1 = column_intervals(width)[c]
             wide = i1 - i0
+            before, b0 = window(before_refs, i0)
+            out, o0 = window(out_refs, i0)
             slots = [(v + a, c + b) for a in (0, 1) for b in (0, 1) if (v + a, c + b) in mine]
-            if not slots:
-                if before_ref is not out_ref:
-                    out_ref[i0:i1, j0:j1, :] = before_ref[i0:i1, j0:j1, :]
-                continue
-            x0 = x_ref[0, i0:i1, j0:j1, :].reshape(wide * tall, members)
-            x1 = x_ref[1, i0:i1, j0:j1, :].reshape(wide * tall, members)
-            left = jnp.concatenate([x0, x0, x1], axis=1)
-            i = lax.broadcasted_iota(jnp.int32, (wide, 1, 1), 0).astype(F32) + (
-                i0 + 0.5 - (c - 0.5) * spacing
-            )
-            right = i * (1.0 / spacing)
-            along_x = (1.0 - right, right)
-            t0 = jnp.concatenate([t_ref[mine[slot], 0] for slot in slots], axis=0)
-            t1 = jnp.concatenate([t_ref[mine[slot], 1] for slot in slots], axis=0)
-            product = dot_nt(left, jnp.concatenate([t0, t1, t0], axis=1))
-            product = product.reshape(wide, tall, len(slots) * part)
-            result = before_ref[i0:i1, j0:j1, :]
-            for n, (row, column) in enumerate(slots):
-                weight = along_x[column - c] * along_y[row - v]
-                result = result + weight * product[:, :, n * part : (n + 1) * part]
-            out_ref[i0:i1, j0:j1, :] = result
+            result = before[b0 : b0 + wide, j0:j1, :]
+            if slots:
+                x, x_first = window(x_refs, i0)
+                x0 = x[0, x_first : x_first + wide, j0:j1, :].reshape(wide * tall, members)
+                x1 = x[1, x_first : x_first + wide, j0:j1, :].reshape(wide * tall, members)
+                left = jnp.concatenate([x0, x0, x1], axis=1)
+                i = lax.broadcasted_iota(jnp.int32, (wide, 1, 1), 0).astype(F32) + (
+                    i0 + 0.5 - (c - 0.5) * spacing
+                )
+                right = i * (1.0 / spacing)
+                along_x = (1.0 - right, right)
+                t0 = jnp.concatenate([t_ref[mine[slot], 0] for slot in slots], axis=0)
+                t1 = jnp.concatenate([t_ref[mine[slot], 1] for slot in slots], axis=0)
+                product = dot_nt(left, jnp.concatenate([t0, t1, t0], axis=1))
+                product = product.reshape(wide, tall, len(slots) * part)
+                for n, (row, column) in enumerate(slots):
+                    weight = along_x[column - c] * along_y[row - v]
+                    result = result + weight * product[:, :, n * part : (n + 1) * part]
+            out[o0 : o0 + wide, j0:j1, :] = result
 
 
 def inner_slots(bands):
@@ -321,7 +326,8 @@
         put(t_ref, north, end_value())
 
 
-def inner_kernel(bands, *refs):
+def inner_kernel(geometry, intervals, first, *refs):
+    bands = geometry[2]
     x_ref, mean_ref = refs[:2]
     rows = refs[2 : 2 * bands + 1]
     out_ref, t_ref = refs[2 * bands + 1 :]
@@ -329,26 +335,37 @@
     for shift in range(bands):
         band = lax.rem(me - shift + bands, bands)
         for n, point in enumerate(POINTS):
+            if point + 1 < intervals[0] or point > intervals[-1]:
+                continue
             if shift == 0:
                 value = rows[0][n]
             elif n < 2:
                 value = rows[2 * shift - 1][n]
             else:
                 value = rows[2 * shift][n - 2]
-            t0, t1 = split2(value)
-            t_ref[band * CGX + point, 0] = t0
-            t_ref[band * CGX + point, 1] = t1
-    add_terms(x_ref, t_ref, mean_ref, out_ref, bands, inner_slots(bands))
-
-
-def edge_kernel(bands, tiles_y, *refs):
+            put(t_ref, band * CGX + point, value)
+    slots = inner_slots(bands)
+    add_terms(
+        geometry,
+        intervals,
+        [(x_ref, first)],
+        t_ref,
+        [(mean_ref, first)],
+        [(out_ref, first)],
+        slots,
+    )
+
+
+def edge_kernel(geometry, firsts, tiles_y, *refs):
     refs = list(refs)
 
     def take(n):
         taken, refs[:n] = refs[:n], []
         return taken
 
-    x_ref, before_ref = take(2)
+    bands = geometry[2]
+    x_refs = list(zip(take(len(firsts)), firsts))
+    before_refs = list(zip(take(len(firsts)), firsts))
     rows, ends, sides = take(bands), take(bands), take(2)
     out_ref, t_ref = refs
     me = lax.axis_index("mem")
@@ -368,7 +385,9 @@
             )
         for side in (0, 1):
             put(t_ref, slots[1, 0] + 2 * band + side, sides[side][shift])
-    add_terms(x_ref, t_ref, before_ref, out_ref, bands, slots)
+    add_terms(
+        geometry, range(CGX + 1), x_refs, t_ref, before_refs, [(out_ref, 0)], slots
+    )
 
 
 def corner_kernel(bands, tiles_y, spacing, depth, *refs):
@@ -430,14 +449,16 @@
     )(edge, *rows, *ends)
 
 
-def last_kernel(bands, tiles_y, *refs):
+def last_kernel(geometry, firsts, tiles_y, *refs):
     refs = list(refs)
 
     def take(n):
         taken, refs[:n] = refs[:n], []
         return taken
 
-    x_ref, before_ref = take(2)
+    width, height, bands = geometry
+    x_refs = list(zip(take(len(firsts)), firsts))
+    (before_ref,) = take(1)
     rows, ends, given = take(bands), take(bands), take(2)
     out_ref, t_ref = refs
     slots = last_slots(bands)
@@ -454,8 +475,15 @@
                 lambda shift=shift, k=k: rows[shift][k],
                 lambda shift=shift, k=k: ends[shift][k],
             )
-    add_terms(x_ref, t_ref, before_ref, out_ref, bands, slots)
-    width, height, _ = out_ref.shape
+    add_terms(
+        geometry,
+        range(CGX + 1),
+        x_refs,
+        t_ref,
+        [(before_ref, 0)],
+        [(out_ref, 0)],
+        slots,
+    )
     half, depth, _ = given[0].shape
     for ref, first in zip(given, (0, width - half)):
         for start, cells in ((0, 0), (depth // 2, height - depth // 2)):
@@ -466,24 +494,25 @@
             )
 
 
-def apply_terms(kernel, x, before, operands, slots, flops):
-    _, width, height, members = x.shape
-    part = before.shape[2]
+def apply_terms(kernel, width, xs, befores, operands, slots, flops):
+    _, _, height, members = xs[0].shape
+    part = befores[0].shape[2]
     vmem = pl.BlockSpec(memory_space=pltpu.VMEM)
-    size = sum(array.size for array in operands)
+    operands = list(xs) + list(befores) + list(operands)
+    size = sum(array.size * array.dtype.itemsize for array in operands)
     return pl.pallas_call(
         kernel,
         out_shape=jax.ShapeDtypeStruct((width, height, part), F32),
-        in_specs=[vmem] * (2 + len(operands)),
+        in_specs=[vmem] * len(operands),
         out_specs=vmem,
         scratch_shapes=[pltpu.VMEM((len(slots), 2, part, members), BF16)],
         compiler_params=pltpu.CompilerParams(
-            vmem_limit_bytes=min(4 * (x.size + 2 * before.size + 2 * size) + 8 * MIB, 60 * MIB)
+            vmem_limit_bytes=min(size + 8 * width * height * part + 16 * MIB, 60 * MIB)
         ),
         cost_estimate=pl.CostEstimate(
-            flops=flops, bytes_accessed=4 * (x.size + before.size), transcendentals=0
+            flops=flops, bytes_accessed=size, transcendentals=0
         ),
-    )(x, before, *operands)
+    )(*operands)
 
 
 def shifted(array, axis, by):
@@ -507,16 +536,14 @@
     part = background.shape[0]
     members = part * bands
     slots = departure.shape[3]
-    anomalies = anomalies.reshape(part, bands * slots)
-    others = []
-    for shift in range(1, bands):
-        piece = lax.dynamic_slice_in_dim(
-            anomalies, lax.rem(me + shift, bands) * slots, slots, axis=1
-        )
-        others.append(piece)
+
+    def of_band(band):
+        return lax.dynamic_slice_in_dim(anomalies, band * slots, slots, axis=3)
+
+    others = [of_band(lax.rem(me + shift, bands)) for shift in range(1, bands)]
     anomalies, others = lax.optimization_barrier((anomalies, others))
-    others = [shifted(piece, "mem", s) for s, piece in enumerate(others, 1)]
-    own = lax.dynamic_slice_in_dim(anomalies, me * slots, slots, axis=1)
+    others = [shifted(piece.reshape(part, slots), "mem", s) for s, piece in enumerate(others, 1)]
+    own = of_band(me).reshape(part, slots)
     tile = background.transpose(1, 2, 0)
     width, height = tile.shape[:2]
     spacing, depth = width // CGX, height // bands
@@ -539,7 +566,8 @@
             blocks = [blocks.reshape(blocks.shape[:2] + (members,))]
         return blocks
 
-    cells = gathered(tile)
+    firsts = (0, column_intervals(width)[CGX - 1][0])
+    cells = [gathered(tile[: firsts[1]]), gathered(tile[firsts[1] :])]
     edges = gathered(edge)
     solved = solve(
         POINTS,
@@ -560,7 +588,9 @@
         for n, by in ((1, 1), (0, -1))
     ]
     ends_mid = [to_next_tile(other_mid[s - 1], s) for s in range(1, bands)]
-    x, mean, edge = prepare(cells, edges, part)
+    geometry = (width, height, bands)
+    edge, _ = prepare(edges, part)
+    x_first, mean_first = prepare(cells[0], part)
     left, right = corners(
         bands, tiles_y, spacing, depth, edge, [row] + other_side, [own_end] + ends_side
     )
@@ -568,27 +598,37 @@
     operands = [row]
     for side, mid in zip(other_side, other_mid):
         operands += [side, mid]
-    work = 6 * mean.size * members
+    work = 6 * width * height * part * members
+
+    def inner(x, mean, intervals, first):
+        return apply_terms(
+            functools.partial(inner_kernel, geometry, intervals, first),
+            x.shape[1],
+            [x],
+            [mean],
+            operands,
+            inner_slots(bands),
+            3 * work * x.shape[1] // width,
+        )
+
+    inner_first = inner(x_first, mean_first, range(CGX - 1), 0)
+    x_second, mean_second = prepare(cells[1], part)
+    inner_second = inner(x_second, mean_second, range(CGX - 1, CGX + 1), firsts[1])
+    xs = [x_first, x_second]
     result = apply_terms(
-        functools.partial(inner_kernel, bands),
-        x,
-        mean,
-        operands,
-        inner_slots(bands),
-        3 * work,
-    )
-    result = apply_terms(
-        functools.partial(edge_kernel, bands, tiles_y),
-        x,
-        result,
+        functools.partial(edge_kernel, geometry, firsts, tiles_y),
+        width,
+        xs,
+        [inner_first, inner_second],
         [row] + other_side + [own_end] + ends_side + row_sides,
         edge_slots(bands),
         work,
     )
     result = apply_terms(
-        functools.partial(last_kernel, bands, tiles_y),
-        x,
-        result,
+        functools.partial(last_kernel, geometry, firsts, tiles_y),
+        width,
+        xs,
+        [result],
         [row] + other_mid + [own_end] + ends_mid + given,
         last_slots(bands),
         work // 2,

time: 66.9 us -> 87.2 us (1.30); the launches traced: 66.7 us -> 86 us
  waiting for transfers between devices: 18.3 us -> 35.8 us
  Pallas kernels: 22 us -> 24.1 us
    ppermute x11 -> x12, waiting for transfers between devices: 18.3 us -> 35.8 us  [shifted(): lax.ppermute(array, axis, [(i, (i + by) % size) for i in range(size)])]
    unnamed x13 -> x12, local copies, waits for them, and re-layouts: 2.81 us -> 0.13 us
    slice x0 -> x2, local copies, waits for them, and re-layouts: none -> 2.24 us  [analysis(): cells = [gathered(tile[:firsts[1]]), gathered(tile[firsts[1]:])]]
    pallas_call x1, Pallas kernels: 15.5 us -> 16.6 us  [solve(): pl.pallas_call(functools.partial(solve_kernel, points, bands), out_shape=...]
    dynamic_slice x2, local copies, waits for them, and re-layouts: 1.12 us -> 0.08 us  [of_band(): return lax.dynamic_slice_in_dim(anomalies, band * slots, slots, axis=3)]
    optimization_barrier x0 -> x1, local copies, waits for them, and re-layouts: none -> 0.89 us  [analysis(): anomalies, others = lax.optimization_barrier((anomalies, others))]
    ppermute x11 -> x12, starting transfers between devices: 12.3 us -> 13.1 us  [shifted(): lax.ppermute(array, axis, [(i, (i + by) % size) for i in range(size)])]
    pallas_call x1 -> x3, Pallas kernels: 1.05 us -> 1.82 us  [prepare(): pl.pallas_call(functools.partial(prepare_kernel, len(cells)), out_shape=[...]
  transfers between devices with their start and end apart: 14 -> 15, of which waited for: 4 -> 4; matrix products, arithmetic and copies ran while one was open for 2% -> 3% of each run, Pallas kernels for 30% -> 26%
where the time goes in v3:
time: 87.2 us; the launch traced here: 86 us
  waiting for transfers between devices  35.8 us (41%)
  Pallas kernels  24.1 us (28%)
  starting transfers between devices  21.8 us (25%)
  local copies, waits for them, and re-layouts  3.42 us (4%)
  between operations  0.94 us (1%)
    ppermute x12, waiting for transfers between devices, shifted(): lax.ppermute(array, axis, [(i, (i + by) % size) for i in range(size)])  35.8 us
    pallas_call x1, Pallas kernels, solve(): pl.pallas_call(functools.partial(solve_kernel, points, bands), out_shape=...  16.6 us
    ppermute x12, starting transfers between devices, shifted(): lax.ppermute(array, axis, [(i, (i + by) % size) for i in range(size)])  13.1 us
    ppermute x3, starting transfers between devices, to_next_tile(): return lax.ppermute(array, ('mem', 'gy'), pairs)  8.64 us
    pallas_call x4, Pallas kernels, apply_terms(): pl.pallas_call(kernel, out_shape=jax.ShapeDtypeStruct((width, height, par...  5.16 us
    slice x2, local copies, waits for them, and re-layouts, analysis(): cells = [gathered(tile[:firsts[1]]), gathered(tile[firsts[1]:])]  2.24 us
    pallas_call x3, Pallas kernels, prepare(): pl.pallas_call(functools.partial(prepare_kernel, len(cells)), out_shape=[...  1.82 us
  transfers between devices with their start and end apart: 15, of which 4 were waited for; matrix products, arithmetic and copies ran while one was open for 3% of the time, Pallas kernels for 26%

profile of v3, /device:TPU:0, one launch (start us, length us, event | category | flops | bytes accessed | tf_op | source)
XLA Modules:
  0.0 86.0 jit_solution(14749504089236567728)
XLA Ops:
  0.0 1.2 %slice.40.refs_0_ = f32[20,64,128]{2,1,0:T(8,128)S(1)} slice(f32[32,64,128]{2,1,0:T(8,128)} %bitcast.15), slice={[0:20], [0:64], [0:128]} | slice | bytes 1310720 | tf_op jit(solution)/shard_map/slice | solution.py:570
  1.2 3.1 %collective-permute-start = (f32[20,64,128]{2,1,0:T(8,128)S(1)}, f32[20,64,128]{2,1,0:T(8,128)S(1)}, u32[]{:S(2)}, u32[]{:S(2)}) collective-permute-start(f32[20,64,128]{2,1,0:T(8,128)S(1)} %slice.40.refs_0_), channel_id=1, source_target_pairs={{0,16},{16,0},{1,17},{17,1},{2,18},{18,2},{3,19},{19,3},{4,20},{20... | collective-permute-start | bytes 1966088 | tf_op jit(solution)/shard_map/ppermute | solution.py:520
  4.3 1.0 %slice.41.refs_0_ = f32[12,64,128]{2,1,0:T(8,128)S(1)} slice(f32[32,64,128]{2,1,0:T(8,128)} %bitcast.16), slice={[20:32], [0:64], [0:128]} | slice | bytes 786432 | tf_op jit(solution)/shard_map/slice | solution.py:570
  5.3 0.1 collective-permute-start.1
  5.5 0.9 %copy.9 = f32[128,1,1,1024]{3,0,2,1:T(8,128)} copy(f32[128,1,1,1024]{3,2,1,0:T(1,128)S(1)} %constant_dynamic-slice_fusion.1) | data formatting | bytes 1048576 | tf_op jit(solution)/shard_map/optimization_barrier | solution.py:544
  6.4 2.0 %collective-permute-start.2 = (f32[128,1024]{1,0:T(8,128)}, f32[128,1024]{1,0:T(8,128)}, u32[]{:S(2)}, u32[]{:S(2)}) collective-permute-start(f32[128,1024]{1,0:T(8,128)} %bitcast.2), channel_id=1, source_target_pairs={{0,16},{16,0},{1,17},{17,1},{2,18},{18,2},{3,19},{19,3},{4,20},{20... | collective-permute-start | bytes 1572872 | tf_op jit(solution)/shard_map/ppermute | solution.py:520
  8.4 0.1 collective-permute-start.10
  8.6 0.4 collective-permute-start.11
  9.7 0.1 copy.11
  9.8 0.7 collective-permute-done.10
  10.5 28.3 %collective-permute-done.2.refs_0_ = f32[128,1024]{1,0:T(8,128)} collective-permute-done((f32[128,1024]{1,0:T(8,128)}, f32[128,1024]{1,0:T(8,128)}, u32[]{:S(2)}, u32[]{:S(2)}) %collective-permute-start.2) | collective-permute-done | bytes 524320 | tf_op jit(solution)/shard_map/ppermute | solution.py:520
  38.8 16.6 %solve.1 = (f32[4,128,256]{2,1,0:T(8,128)S(1)}, f32[2,128,256]{2,1,0:T(8,128)S(1)}, f32[2,128,256]{2,1,0:T(8,128)S(1)}) custom-call(s32[1]{0:T(128)} %bitcast.10.live_ref, f32[128,1024]{1,0:T(8,128)S(1)} %bitcast.11, f32[128,1024]{1,0:T(8,128)} %collective-permute-done.2.refs_0_, f32[1,1024]{1,0:T(1,128)S(1)} %bitcast.12, f32[1,1024]{1,0:T(1,128)S(1)} %bitcast.13, ...), custom_call_target="tpu_custom_call" | custom-call | flops 11140071424 | bytes 2097152 | tf_op jit(solution)/shard_map/solve/pallas_call | solution.py:165
  55.4 1.8 %collective-permute-start.3 = (f32[2,128,256]{2,1,0:T(8,128)S(1)}, f32[2,128,256]{2,1,0:T(8,128)S(1)}, u32[]{:S(2)}, u32[]{:S(2)}) collective-permute-start(f32[2,128,256]{2,1,0:T(8,128)S(1)} %get-tuple-element.23), channel_id=1, source_target_pairs={{0,16},{16,0},{1,17},{17,1},{2,18},{18,2},{3,19},{19,3},{4,20},{20... | collective-permute-start | bytes 786440 | tf_op jit(solution)/shard_map/ppermute | solution.py:520
  57.2 0.4 collective-permute-start.12
  57.5 1.3 %collective-permute-start.5 = (f32[4,128,256]{2,1,0:T(8,128)S(1)}, f32[4,128,256]{2,1,0:T(8,128)S(1)}, u32[]{:S(2)}, u32[]{:S(2)}) collective-permute-start(f32[4,128,256]{2,1,0:T(8,128)S(1)} %get-tuple-element.22.refs_2_.refs_4_.refs_1_.refs_3_), channel_id=1, source_target_pairs={{16,17},{17,18},{18,19},{1,0},{2,1},{3,2},{20,21},{21,22},{22,23},... | collective-permute-start | bytes 1572872 | tf_op jit(solution)/shard_map/ppermute | solution.py:529
  58.8 5.8 %collective-permute-done.3.refs_3_.refs_5_.refs_2_ = f32[2,128,256]{2,1,0:T(8,128)S(1)} collective-permute-done((f32[2,128,256]{2,1,0:T(8,128)S(1)}, f32[2,128,256]{2,1,0:T(8,128)S(1)}, u32[]{:S(2)}, u32[]{:S(2)}) %collective-permute-start.3) | collective-permute-done | bytes 262176 | tf_op jit(solution)/shard_map/ppermute | solution.py:520
  64.6 1.7 %collective-permute-start.4 = (f32[2,128,256]{2,1,0:T(8,128)S(1)}, f32[2,128,256]{2,1,0:T(8,128)S(1)}, u32[]{:S(2)}, u32[]{:S(2)}) collective-permute-start(f32[2,128,256]{2,1,0:T(8,128)S(1)} %get-tuple-element.24), channel_id=1, source_target_pairs={{0,16},{16,0},{1,17},{17,1},{2,18},{18,2},{3,19},{19,3},{4,20},{20... | collective-permute-start | bytes 786440 | tf_op jit(solution)/shard_map/ppermute | solution.py:520
  66.4 1.0 %collective-permute-done.12.refs_1_ = f32[8,32,128]{2,1,0:T(8,128)S(1)} collective-permute-done((f32[8,32,128]{2,1,0:T(8,128)S(1)}, f32[8,32,128]{2,1,0:T(8,128)S(1)}, u32[]{:S(2)}, u32[]{:S(2)}) %collective-permute-start.12) | collective-permute-done | bytes 131104 | tf_op jit(solution)/shard_map/ppermute | solution.py:520
  67.4 3.7 %collective-permute-start.6 = (f32[2,128,256]{2,1,0:T(8,128)S(1)}, f32[2,128,256]{2,1,0:T(8,128)S(1)}, u32[]{:S(2)}, u32[]{:S(2)}) collective-permute-start(f32[2,128,256]{2,1,0:T(8,128)S(1)} %collective-permute-done.3.refs_3_.refs_5_.refs_2_), channel_id=1, source_target_pairs={{0,1},{1,2},{2,3},{17,16},{18,17},{19,18},{4,5},{5,6},{6,7},{21,20... | collective-permute-start | bytes 786440 | tf_op jit(solution)/shard_map/ppermute | solution.py:529
  71.2 0.1 collective-permute-start.7
  71.2 1.7 %collective-permute-start.8 = (f32[2,128,256]{2,1,0:T(8,128)S(1)}, f32[2,128,256]{2,1,0:T(8,128)S(1)}, u32[]{:S(2)}, u32[]{:S(2)}) collective-permute-start(f32[2,128,256]{2,1,0:T(8,128)S(1)} %pad_maximum_fusion.1), channel_id=1, source_target_pairs={{0,12},{4,0},{8,4},{12,8},{1,13},{5,1},{9,5},{13,9},{2,14},{6,2},{... | collective-permute-start | bytes 786440 | tf_op jit(solution)/shard_map/ppermute | solution.py:520
  73.0 3.7 %collective-permute-start.9 = (f32[2,128,256]{2,1,0:T(8,128)S(1)}, f32[2,128,256]{2,1,0:T(8,128)S(1)}, u32[]{:S(2)}, u32[]{:S(2)}) collective-permute-start(f32[2,128,256]{2,1,0:T(8,128)S(1)} %collective-permute-done.4.refs_4_), channel_id=1, source_target_pairs={{0,1},{1,2},{2,3},{17,16},{18,17},{19,18},{4,5},{5,6},{6,7},{21,20... | collective-permute-start | bytes 786440 | tf_op jit(solution)/shard_map/ppermute | solution.py:529
  76.6 0.8 shard_map.69
  77.4 0.4 shard_map.65
  77.8 0.6 shard_map.64
  78.5 1.3 %shard_map.66.refs_2_ = f32[20,64,128]{2,1,0:T(8,128)S(1)} custom-call(bf16[2,20,64,256]{3,2,1,0:T(8,128)(2,1)S(1)} %get-tuple-element.17.refs_0_, f32[20,64,128]{2,1,0:T(8,128)S(1)} %get-tuple-element.19.refs_1_, f32[4,128,256]{2,1,0:T(8,128)S(1)} %get-tuple-element.22.refs_2_.refs_4_.refs_1_.refs_3_, ...), custom_call_target="tpu_custom_call" | custom-call | flops 754974720 | bytes 3014656 | tf_op jit(solution)/shard_map/pallas_call | solution.py:503
  79.8 0.5 corners.1
  80.4 0.1 collective-permute-start.13
  80.4 1.7 %collective-permute-start.14 = (f32[4,32,128]{2,1,0:T(8,128)S(1)}, f32[4,32,128]{2,1,0:T(8,128)S(1)}, u32[]{:S(2)}, u32[]{:S(2)}) collective-permute-start(f32[4,32,128]{2,1,0:T(8,128)S(1)} %get-tuple-element.28), channel_id=1, source_target_pairs={{0,12},{4,0},{8,4},{12,8},{1,13},{5,1},{9,5},{13,9},{2,14},{6,2},{... | collective-permute-start | bytes 196616 | tf_op jit(solution)/shard_map/ppermute | solution.py:520
  82.2 0.9 %shard_map.67.refs_3_ = f32[12,64,128]{2,1,0:T(8,128)S(1)} custom-call(bf16[2,12,64,256]{3,2,1,0:T(8,128)(2,1)S(1)} %get-tuple-element.18.refs_0_.refs_1_, f32[12,64,128]{2,1,0:T(8,128)S(1)} %get-tuple-element.25.refs_1_, f32[4,128,256]{2,1,0:T(8,128)S(1)} %get-tuple-element.22.refs_2_.refs_4_.refs_1_.refs_3_, ...), custom_call_target="tpu_custom_call" | custom-call | flops 452984832 | bytes 2228224 | tf_op jit(solution)/shard_map/pallas_call | solution.py:503
  83.1 1.3 %shard_map.68.refs_2_ = f32[32,64,128]{2,1,0:T(8,128)S(1)} custom-call(bf16[2,20,64,256]{3,2,1,0:T(8,128)(2,1)S(1)} %get-tuple-element.17.refs_0_, bf16[2,12,64,256]{3,2,1,0:T(8,128)(2,1)S(1)} %get-tuple-element.18.refs_0_.refs_1_, f32[20,64,128]{2,1,0:T(8,128)S(1)} %shard_map.66.refs_2_, f32[12,64,128]{2,1,0:T(8,128)S(1)} %shard_map.67.refs_3_, ...), custom_call_target="tpu_custom_call" | custom-call | flops 402653184 | bytes 5242880 | tf_op jit(solution)/shard_map/pallas_call | solution.py:503
  84.4 1.7 %shard_map.70 = f32[32,64,128]{2,1,0:T(8,128)} custom-call(bf16[2,20,64,256]{3,2,1,0:T(8,128)(2,1)S(1)} %get-tuple-element.17.refs_0_, bf16[2,12,64,256]{3,2,1,0:T(8,128)(2,1)S(1)} %get-tuple-element.18.refs_0_.refs_1_, f32[32,64,128]{2,1,0:T(8,128)S(1)} %shard_map.68.refs_2_, f32[4,128,256]{2,1,0:T(8,128)S(1)} %get-tuple-element.22.refs_2_.refs_4_.refs_1_.refs_3_, ...), custom_call_target="tpu_custom_call" | custom-call | flops 201326592 | bytes 4849664 | tf_op jit(solution)/shard_map/pallas_call | solution.py:503
  (31 shorter events, 0.3 us)
Async XLA Ops:
  0.0 5.4 %copy-start = (f32[128,1,1,2048]{3,2,1,0:T(1,128)S(1)}, f32[128,1,1,2048]{3,2,1,0:T(1,128)}, u32[]{:S(2)}) copy-start(f32[128,1,1,2048]{3,2,1,0:T(1,128)} %param.7) | copy-start | bytes 3145732
  1.2 70.0 %collective-permute-start = (f32[20,64,128]{2,1,0:T(8,128)S(1)}, f32[20,64,128]{2,1,0:T(8,128)S(1)}, u32[]{:S(2)}, u32[]{:S(2)}) collective-permute-start(f32[20,64,128]{2,1,0:T(8,128)S(1)} %slice.40.refs_0_), channel_id=1, source_target_pairs={{0,16},{16,0},{1,17},{17,1},{2,18},{18,2},{3,19},{19,3},{4,20},{20... | collective-permute-start | bytes 1966088 | tf_op jit(solution)/shard_map/ppermute | solution.py:520
  5.3 65.8 %collective-permute-start.1 = (f32[12,64,128]{2,1,0:T(8,128)S(1)}, f32[12,64,128]{2,1,0:T(8,128)S(1)}, u32[]{:S(2)}, u32[]{:S(2)}) collective-permute-start(f32[12,64,128]{2,1,0:T(8,128)S(1)} %slice.41.refs_0_), channel_id=1, source_target_pairs={{0,16},{16,0},{1,17},{17,1},{2,18},{18,2},{3,19},{19,3},{4,20},{20... | collective-permute-start | bytes 1179656 | tf_op jit(solution)/shard_map/ppermute | solution.py:520
  5.4 2.9 %copy-start.4 = (f32[128,32,64]{0,2,1:T(8,128)S(1)}, f32[128,32,64]{0,2,1:T(8,128)}, u32[]{:S(2)}) copy-start(f32[128,32,64]{0,2,1:T(8,128)} %param.6) | copy-start | bytes 3145732
  6.4 32.4 %collective-permute-start.2 = (f32[128,1024]{1,0:T(8,128)}, f32[128,1024]{1,0:T(8,128)}, u32[]{:S(2)}, u32[]{:S(2)}) collective-permute-start(f32[128,1024]{1,0:T(8,128)} %bitcast.2), channel_id=1, source_target_pairs={{0,16},{16,0},{1,17},{17,1},{2,18},{18,2},{3,19},{19,3},{4,20},{20... | collective-permute-start | bytes 1572872 | tf_op jit(solution)/shard_map/ppermute | solution.py:520
  8.4 30.4 %copy-start.1 = (f32[1,1,1,1024]{3,2,1,0:T(1,128)S(1)}, f32[1,1,1,1024]{3,2,1,0:T(1,128)}, u32[]{:S(2)}) copy-start(f32[1,1,1,1024]{3,2,1,0:T(1,128)} %param.8) | copy-start | bytes 12292
  8.4 30.4 %copy-start.2 = (f32[1,1,1,1024]{3,2,1,0:T(1,128)S(1)}, f32[1,1,1,1024]{3,2,1,0:T(1,128)}, u32[]{:S(2)}) copy-start(f32[1,1,1,1024]{3,2,1,0:T(1,128)} %param.9) | copy-start | bytes 12292
  8.4 30.4 %copy-start.3 = (s32[1,1,1,1024]{3,2,1,0:T(1,128)S(1)}, s32[1,1,1,1024]{3,2,1,0:T(1,128)}, u32[]{:S(2)}) copy-start(s32[1,1,1,1024]{3,2,1,0:T(1,128)} %param.10) | copy-start | bytes 12292
  8.4 2.0 %collective-permute-start.10 = (f32[4,32,128]{2,1,0:T(8,128)S(1)}, f32[4,32,128]{2,1,0:T(8,128)S(1)}, u32[]{:S(2)}, u32[]{:S(2)}) collective-permute-start(f32[4,32,128]{2,1,0:T(8,128)S(1)} %get-tuple-element.32), channel_id=1, source_target_pairs={{0,12},{4,0},{8,4},{12,8},{1,13},{5,1},{9,5},{13,9},{2,14},{6,2},{... | collective-permute-start | bytes 196616 | tf_op jit(solution)/shard_map/ppermute | solution.py:520
  8.6 48.6 %collective-permute-start.11 = (f32[4,32,128]{2,1,0:T(8,128)S(1)}, f32[4,32,128]{2,1,0:T(8,128)S(1)}, u32[]{:S(2)}, u32[]{:S(2)}) collective-permute-start(f32[4,32,128]{2,1,0:T(8,128)S(1)} %get-tuple-element.31), channel_id=1, source_target_pairs={{0,4},{4,8},{8,12},{12,0},{1,5},{5,9},{9,13},{13,1},{2,6},{6,10},{... | collective-permute-start | bytes 196616 | tf_op jit(solution)/shard_map/ppermute | solution.py:520
  55.4 9.2 %collective-permute-start.3 = (f32[2,128,256]{2,1,0:T(8,128)S(1)}, f32[2,128,256]{2,1,0:T(8,128)S(1)}, u32[]{:S(2)}, u32[]{:S(2)}) collective-permute-start(f32[2,128,256]{2,1,0:T(8,128)S(1)} %get-tuple-element.23), channel_id=1, source_target_pairs={{0,16},{16,0},{1,17},{17,1},{2,18},{18,2},{3,19},{19,3},{4,20},{20... | collective-permute-start | bytes 786440 | tf_op jit(solution)/shard_map/ppermute | solution.py:520
  57.2 10.2 %collective-permute-start.12 = (f32[8,32,128]{2,1,0:T(8,128)S(1)}, f32[8,32,128]{2,1,0:T(8,128)S(1)}, u32[]{:S(2)}, u32[]{:S(2)}) collective-permute-start(f32[8,32,128]{2,1,0:T(8,128)S(1)} %constant_dynamic-update-slice_fusion.refs_0_), channel_id=1, source_target_pairs={{0,16},{16,0},{1,17},{17,1},{2,18},{18,2},{3,19},{19,3},{4,20},{20... | collective-permute-start | bytes 393224 | tf_op jit(solution)/shard_map/ppermute | solution.py:520
  57.5 22.3 %collective-permute-start.5 = (f32[4,128,256]{2,1,0:T(8,128)S(1)}, f32[4,128,256]{2,1,0:T(8,128)S(1)}, u32[]{:S(2)}, u32[]{:S(2)}) collective-permute-start(f32[4,128,256]{2,1,0:T(8,128)S(1)} %get-tuple-element.22.refs_2_.refs_4_.refs_1_.refs_3_), channel_id=1, source_target_pairs={{16,17},{17,18},{18,19},{1,0},{2,1},{3,2},{20,21},{21,22},{22,23},... | collective-permute-start | bytes 1572872 | tf_op jit(solution)/shard_map/ppermute | solution.py:529
  64.6 8.4 %collective-permute-start.4 = (f32[2,128,256]{2,1,0:T(8,128)S(1)}, f32[2,128,256]{2,1,0:T(8,128)S(1)}, u32[]{:S(2)}, u32[]{:S(2)}) collective-permute-start(f32[2,128,256]{2,1,0:T(8,128)S(1)} %get-tuple-element.24), channel_id=1, source_target_pairs={{0,16},{16,0},{1,17},{17,1},{2,18},{18,2},{3,19},{19,3},{4,20},{20... | collective-permute-start | bytes 786440 | tf_op jit(solution)/shard_map/ppermute | solution.py:520
  67.4 12.4 %collective-permute-start.6 = (f32[2,128,256]{2,1,0:T(8,128)S(1)}, f32[2,128,256]{2,1,0:T(8,128)S(1)}, u32[]{:S(2)}, u32[]{:S(2)}) collective-permute-start(f32[2,128,256]{2,1,0:T(8,128)S(1)} %collective-permute-done.3.refs_3_.refs_5_.refs_2_), channel_id=1, source_target_pairs={{0,1},{1,2},{2,3},{17,16},{18,17},{19,18},{4,5},{5,6},{6,7},{21,20... | collective-permute-start | bytes 786440 | tf_op jit(solution)/shard_map/ppermute | solution.py:529
  71.2 11.9 %collective-permute-start.7 = (f32[2,128,256]{2,1,0:T(8,128)S(1)}, f32[2,128,256]{2,1,0:T(8,128)S(1)}, u32[]{:S(2)}, u32[]{:S(2)}) collective-permute-start(f32[2,128,256]{2,1,0:T(8,128)S(1)} %pad_maximum_fusion), channel_id=1, source_target_pairs={{0,4},{4,8},{8,12},{12,0},{1,5},{5,9},{9,13},{13,1},{2,6},{6,10},{... | collective-permute-start | bytes 786440 | tf_op jit(solution)/shard_map/ppermute | solution.py:520
  71.2 11.8 %collective-permute-start.8 = (f32[2,128,256]{2,1,0:T(8,128)S(1)}, f32[2,128,256]{2,1,0:T(8,128)S(1)}, u32[]{:S(2)}, u32[]{:S(2)}) collective-permute-start(f32[2,128,256]{2,1,0:T(8,128)S(1)} %pad_maximum_fusion.1), channel_id=1, source_target_pairs={{0,12},{4,0},{8,4},{12,8},{1,13},{5,1},{9,5},{13,9},{2,14},{6,2},{... | collective-permute-start | bytes 786440 | tf_op jit(solution)/shard_map/ppermute | solution.py:520
  73.0 11.4 %collective-permute-start.9 = (f32[2,128,256]{2,1,0:T(8,128)S(1)}, f32[2,128,256]{2,1,0:T(8,128)S(1)}, u32[]{:S(2)}, u32[]{:S(2)}) collective-permute-start(f32[2,128,256]{2,1,0:T(8,128)S(1)} %collective-permute-done.4.refs_4_), channel_id=1, source_target_pairs={{0,1},{1,2},{2,3},{17,16},{18,17},{19,18},{4,5},{5,6},{6,7},{21,20... | collective-permute-start | bytes 786440 | tf_op jit(solution)/shard_map/ppermute | solution.py:529
  80.4 4.0 %collective-permute-start.13 = (f32[4,32,128]{2,1,0:T(8,128)S(1)}, f32[4,32,128]{2,1,0:T(8,128)S(1)}, u32[]{:S(2)}, u32[]{:S(2)}) collective-permute-start(f32[4,32,128]{2,1,0:T(8,128)S(1)} %get-tuple-element.27), channel_id=1, source_target_pairs={{0,4},{4,8},{8,12},{12,0},{1,5},{5,9},{9,13},{13,1},{2,6},{6,10},{... | collective-permute-start | bytes 196616 | tf_op jit(solution)/shard_map/ppermute | solution.py:520
  80.4 3.9 %collective-permute-start.14 = (f32[4,32,128]{2,1,0:T(8,128)S(1)}, f32[4,32,128]{2,1,0:T(8,128)S(1)}, u32[]{:S(2)}, u32[]{:S(2)}) collective-permute-start(f32[4,32,128]{2,1,0:T(8,128)S(1)} %get-tuple-element.28), channel_id=1, source_target_pairs={{0,12},{4,0},{8,4},{12,8},{1,13},{5,1},{9,5},{13,9},{2,14},{6,2},{... | collective-permute-start | bytes 196616 | tf_op jit(solution)/shard_map/ppermute | solution.py:520

commit v4 on v3

--- a/solution.py
+++ b/solution.py
@@ -287,14 +287,8 @@
     return {name: n for n, name in enumerate(names)}
 
 
-def edge_slots(bands):
-    names = [(row, column) for row in (0, bands + 1) for column in (1, CGX)]
-    names += [(row, column) for row in range(1, bands + 1) for column in (0, CGX + 1)]
-    return {name: n for n, name in enumerate(names)}
-
-
-def last_slots(bands):
-    names = [(row, column) for row in (0, bands + 1) for column in range(2, CGX)]
+def all_slots(bands):
+    names = [(row, column) for row in range(bands + 2) for column in range(CGX + 2)]
     return {name: n for n, name in enumerate(names)}
 
 
@@ -353,40 +347,6 @@
         [(mean_ref, first)],
         [(out_ref, first)],
         slots,
-    )
-
-
-def edge_kernel(geometry, firsts, tiles_y, *refs):
-    refs = list(refs)
-
-    def take(n):
-        taken, refs[:n] = refs[:n], []
-        return taken
-
-    bands = geometry[2]
-    x_refs = list(zip(take(len(firsts)), firsts))
-    before_refs = list(zip(take(len(firsts)), firsts))
-    rows, ends, sides = take(bands), take(bands), take(2)
-    out_ref, t_ref = refs
-    me = lax.axis_index("mem")
-    slots = edge_slots(bands)
-    for shift in range(bands):
-        band = lax.rem(me - shift + bands, bands)
-        for n, point in enumerate(SIDES):
-            put_ends(
-                t_ref,
-                slots[0, point + 1],
-                slots[bands + 1, point + 1],
-                bands,
-                tiles_y,
-                shift,
-                lambda shift=shift, n=n: rows[shift][n],
-                lambda shift=shift, n=n: ends[shift][n],
-            )
-        for side in (0, 1):
-            put(t_ref, slots[1, 0] + 2 * band + side, sides[side][shift])
-    add_terms(
-        geometry, range(CGX + 1), x_refs, t_ref, before_refs, [(out_ref, 0)], slots
     )
 
 
@@ -449,7 +409,7 @@
     )(edge, *rows, *ends)
 
 
-def last_kernel(geometry, firsts, tiles_y, *refs):
+def final_kernel(geometry, firsts, tiles_y, *refs):
     refs = list(refs)
 
     def take(n):
@@ -457,41 +417,50 @@
         return taken
 
     width, height, bands = geometry
-    x_refs = list(zip(take(len(firsts)), firsts))
-    (before_ref,) = take(1)
-    rows, ends, given = take(bands), take(bands), take(2)
+    x_refs = list(zip(take(2), firsts))
+    before_refs = list(zip(take(2), firsts))
+    row, own_end = take(2)
+    other_side, other_mid = take(bands - 1), take(bands - 1)
+    ends_side, ends_mid = take(bands - 1), take(bands - 1)
+    sides, given = take(2), take(2)
     out_ref, t_ref = refs
-    slots = last_slots(bands)
+    me = lax.axis_index("mem")
+    slots = all_slots(bands)
     for shift in range(bands):
-        for n in range(CGX - 2):
-            k = 2 + n if shift == 0 else n
+        band = lax.rem(me - shift + bands, bands)
+        for n, point in enumerate(POINTS):
+            if shift == 0:
+                here, there, k = row, own_end, n
+            elif n < 2:
+                here, there, k = other_side[shift - 1], ends_side[shift - 1], n
+            else:
+                here, there, k = other_mid[shift - 1], ends_mid[shift - 1], n - 2
+            if point + 2 >= CGX:
+                put(t_ref, (band + 1) * (CGX + 2) + point + 1, here[k])
             put_ends(
                 t_ref,
-                slots[0, 2 + n],
-                slots[bands + 1, 2 + n],
+                slots[0, point + 1],
+                slots[bands + 1, point + 1],
                 bands,
                 tiles_y,
                 shift,
-                lambda shift=shift, k=k: rows[shift][k],
-                lambda shift=shift, k=k: ends[shift][k],
+                lambda here=here, k=k: here[k],
+                lambda there=there, k=k: there[k],
             )
-    add_terms(
-        geometry,
-        range(CGX + 1),
-        x_refs,
-        t_ref,
-        [(before_ref, 0)],
-        [(out_ref, 0)],
-        slots,
-    )
+        for side, column in enumerate((0, CGX + 1)):
+            put(t_ref, (band + 1) * (CGX + 2) + column, sides[side][shift])
+    rows, columns = range(1, bands + 1), range(1, CGX + 1)
+    late = {s: n for s, n in slots.items() if (s[0] in rows) != (s[1] in columns)}
+    both = {s: n for s, n in slots.items() if s[0] in rows or s[1] in columns}
+    for intervals, mine in ((range(CGX - 1), late), (range(CGX - 1, CGX + 1), both)):
+        add_terms(
+            geometry, intervals, x_refs, t_ref, before_refs, [(out_ref, 0)], mine
+        )
     half, depth, _ = given[0].shape
     for ref, first in zip(given, (0, width - half)):
         for start, cells in ((0, 0), (depth // 2, height - depth // 2)):
             place = slice(cells, cells + depth // 2)
-            out_ref[first : first + half, place, :] = (
-                before_ref[first : first + half, place, :]
-                + ref[:, start : start + depth // 2, :]
-            )
+            out_ref[first : first + half, place, :] += ref[:, start : start + depth // 2, :]
 
 
 def apply_terms(kernel, width, xs, befores, operands, slots, flops):
@@ -567,7 +536,8 @@
         return blocks
 
     firsts = (0, column_intervals(width)[CGX - 1][0])
-    cells = [gathered(tile[: firsts[1]]), gathered(tile[firsts[1] :])]
+    tally, second = lax.optimization_barrier((tally, tile[firsts[1] :]))
+    cells = [gathered(tile[: firsts[1]]), gathered(second)]
     edges = gathered(edge)
     solved = solve(
         POINTS,
@@ -600,38 +570,30 @@
         operands += [side, mid]
     work = 6 * width * height * part * members
 
-    def inner(x, mean, intervals, first):
-        return apply_terms(
-            functools.partial(inner_kernel, geometry, intervals, first),
-            x.shape[1],
-            [x],
-            [mean],
-            operands,
-            inner_slots(bands),
-            3 * work * x.shape[1] // width,
-        )
-
-    inner_first = inner(x_first, mean_first, range(CGX - 1), 0)
+    inner_first = apply_terms(
+        functools.partial(inner_kernel, geometry, range(CGX - 1), 0),
+        firsts[1],
+        [x_first],
+        [mean_first],
+        operands,
+        inner_slots(bands),
+        work,
+    )
     x_second, mean_second = prepare(cells[1], part)
-    inner_second = inner(x_second, mean_second, range(CGX - 1, CGX + 1), firsts[1])
-    xs = [x_first, x_second]
     result = apply_terms(
-        functools.partial(edge_kernel, geometry, firsts, tiles_y),
+        functools.partial(final_kernel, geometry, firsts, tiles_y),
         width,
-        xs,
-        [inner_first, inner_second],
-        [row] + other_side + [own_end] + ends_side + row_sides,
-        edge_slots(bands),
-        work,
-    )
-    result = apply_terms(
-        functools.partial(last_kernel, geometry, firsts, tiles_y),
-        width,
-        xs,
-        [result],
-        [row] + other_mid + [own_end] + ends_mid + given,
-        last_slots(bands),
-        work // 2,
+        [x_first, x_second],
+        [inner_first, mean_second],
+        [row, own_end]
+        + other_side
+        + other_mid
+        + ends_side
+        + ends_mid
+        + row_sides
+        + given,
+        all_slots(bands),
+        2 * work,
     )
     return result.transpose(2, 0, 1)
 

time: 87.2 us -> 67.2 us (0.77)
  waiting for transfers between devices: 35.8 us -> 14.7 us
  starting transfers between devices: 21.8 us -> 24.3 us
  Pallas kernels: 24.1 us -> 22.9 us
    ppermute x12, waiting for transfers between devices: 35.8 us -> 14.7 us  [shifted(): lax.ppermute(array, axis, [(i, (i + by) % size) for i in range(size)])]
    ppermute x12, starting transfers between devices: 13.1 us -> 15.1 us  [shifted(): lax.ppermute(array, axis, [(i, (i + by) % size) for i in range(size)])]
    unnamed x12, local copies, waits for them, and re-layouts: 0.13 us -> 1.35 us
    slice x2, local copies, waits for them, and re-layouts: 2.24 us -> 1.07 us  [the longest x1 1.02 us: analysis(): tally, second = lax.optimization_barrier((tally, tile[firsts[1]:]))]
    pallas_call x1, Pallas kernels: 16.6 us -> 15.5 us  [solve(): pl.pallas_call(functools.partial(solve_kernel, points, bands), out_shape=...]
    pallas_call x4 -> x2, Pallas kernels: 5.16 us -> 4.86 us  [apply_terms(): pl.pallas_call(kernel, out_shape=jax.ShapeDtypeStruct((width, height, par...]
  transfers between devices with their start and end apart: 15 -> 15, of which waited for: 4 -> 3; matrix products, arithmetic and copies ran while one was open for 3% -> 2% of each run, Pallas kernels for 26% -> 29%
where the time goes in v4:
time: 67.2 us; the launch traced here: 66.3 us
  starting transfers between devices  24.3 us (36%)
  Pallas kernels  22.9 us (34%)
  waiting for transfers between devices  14.7 us (22%)
  local copies, waits for them, and re-layouts  3.47 us (5%)
  between operations  0.92 us (1%)
    pallas_call x1, Pallas kernels, solve(): pl.pallas_call(functools.partial(solve_kernel, points, bands), out_shape=...  15.5 us
    ppermute x12, starting transfers between devices, shifted(): lax.ppermute(array, axis, [(i, (i + by) % size) for i in range(size)])  15.1 us
    ppermute x12, waiting for transfers between devices, shifted(): lax.ppermute(array, axis, [(i, (i + by) % size) for i in range(size)])  14.7 us
    ppermute x3, starting transfers between devices, to_next_tile(): return lax.ppermute(array, ('mem', 'gy'), pairs)  9.25 us
    pallas_call x2, Pallas kernels, apply_terms(): pl.pallas_call(kernel, out_shape=jax.ShapeDtypeStruct((width, height, par...  4.86 us
    pallas_call x3, Pallas kernels, prepare(): pl.pallas_call(functools.partial(prepare_kernel, len(cells)), out_shape=[...  1.81 us
    unnamed x12, local copies, waits for them, and re-layouts  1.35 us
  transfers between devices with their start and end apart: 15, of which 3 were waited for; matrix products, arithmetic and copies ran while one was open for 2% of the time, Pallas kernels for 29%

profile of v4, /device:TPU:0, one launch (start us, length us, event | category | flops | bytes accessed | tf_op | source)
XLA Modules:
  0.0 66.3 jit_solution(17343331277340986669)
XLA Ops:
  0.0 1.2 %copy-done = f32[128,1,1,2048]{3,2,1,0:T(1,128)S(1)} copy-done((f32[128,1,1,2048]{3,2,1,0:T(1,128)S(1)}, f32[128,1,1,2048]{3,2,1,0:T(1,128)}, u32[]{:S(2)}) %copy-start) | copy-done | bytes 1048600
  1.3 0.9 %copy.9 = f32[128,1,1,1024]{3,0,2,1:T(8,128)} copy(f32[128,1,1,1024]{3,2,1,0:T(1,128)S(1)} %constant_dynamic-slice_fusion.1) | data formatting | bytes 1048576 | tf_op jit(solution)/shard_map/optimization_barrier | solution.py:513
  2.2 3.0 %collective-permute-start.2 = (f32[128,1024]{1,0:T(8,128)}, f32[128,1024]{1,0:T(8,128)S(1)}, u32[]{:S(2)}, u32[]{:S(2)}) collective-permute-start(f32[128,1024]{1,0:T(8,128)} %bitcast.2), channel_id=1, source_target_pairs={{0,16},{16,0},{1,17},{17,1},{2,18},{18,2},{3,19},{19,3},{4,20},{20... | collective-permute-start | bytes 1572872 | tf_op jit(solution)/shard_map/ppermute | solution.py:489
  5.2 0.7 %collective-permute-start.10 = (f32[4,32,128]{2,1,0:T(8,128)S(1)}, f32[4,32,128]{2,1,0:T(8,128)S(1)}, u32[]{:S(2)}, u32[]{:S(2)}) collective-permute-start(f32[4,32,128]{2,1,0:T(8,128)S(1)} %get-tuple-element.36), channel_id=1, source_target_pairs={{0,12},{4,0},{8,4},{12,8},{1,13},{5,1},{9,5},{13,9},{2,14},{6,2},{... | collective-permute-start | bytes 196616 | tf_op jit(solution)/shard_map/ppermute | solution.py:489
  5.9 0.1 slice.40.refs_0_
  6.0 0.6 collective-permute-start
  6.6 1.0 %slice.41.refs_0_ = f32[12,64,128]{2,1,0:T(8,128)S(1)} slice(f32[32,64,128]{2,1,0:T(8,128)} %bitcast.15), slice={[20:32], [0:64], [0:128]} | slice | bytes 786432 | tf_op jit(solution)/shard_map/slice | solution.py:539
  7.6 0.0 copy-start.1
  7.6 0.0 copy-start.2
  7.6 0.0 copy-start.3
  8.3 0.1 copy.11
  8.5 9.7 %collective-permute-done.2.refs_0_ = f32[128,1024]{1,0:T(8,128)S(1)} collective-permute-done((f32[128,1024]{1,0:T(8,128)}, f32[128,1024]{1,0:T(8,128)S(1)}, u32[]{:S(2)}, u32[]{:S(2)}) %collective-permute-start.2) | collective-permute-done | bytes 524320 | tf_op jit(solution)/shard_map/ppermute | solution.py:489
  18.1 15.5 %solve.1 = (f32[4,128,256]{2,1,0:T(8,128)S(1)}, f32[2,128,256]{2,1,0:T(8,128)S(1)}, f32[2,128,256]{2,1,0:T(8,128)S(1)}) custom-call(s32[1]{0:T(128)} %bitcast.10.live_ref, f32[128,1024]{1,0:T(8,128)S(1)} %bitcast.11, f32[128,1024]{1,0:T(8,128)S(1)} %collective-permute-done.2.refs_0_, f32[1,1024]{1,0:T(1,128)S(1)} %bitcast.12, f32[1,1024]{1,0:T(1,128)S(1)} %bitcast.13, ...), custom_call_target="tpu_custom_call" | custom-call | flops 11140071424 | bytes 2097152 | tf_op jit(solution)/shard_map/solve/pallas_call | solution.py:165
  33.6 2.1 %collective-permute-start.3 = (f32[2,128,256]{2,1,0:T(8,128)S(1)}, f32[2,128,256]{2,1,0:T(8,128)S(1)}, u32[]{:S(2)}, u32[]{:S(2)}) collective-permute-start(f32[2,128,256]{2,1,0:T(8,128)S(1)} %get-tuple-element.27), channel_id=1, source_target_pairs={{0,16},{16,0},{1,17},{17,1},{2,18},{18,2},{3,19},{19,3},{4,20},{20... | collective-permute-start | bytes 786440 | tf_op jit(solution)/shard_map/ppermute | solution.py:489
  35.7 0.0 collective-permute-done.11
  35.7 0.1 collective-permute-start.12
  35.8 1.3 %collective-permute-start.5 = (f32[4,128,256]{2,1,0:T(8,128)S(1)}, f32[4,128,256]{2,1,0:T(8,128)S(1)}, u32[]{:S(2)}, u32[]{:S(2)}) collective-permute-start(f32[4,128,256]{2,1,0:T(8,128)S(1)} %get-tuple-element.26.refs_2_.refs_1_.refs_4_), channel_id=1, source_target_pairs={{16,17},{17,18},{18,19},{1,0},{2,1},{3,2},{20,21},{21,22},{22,23},... | collective-permute-start | bytes 1572872 | tf_op jit(solution)/shard_map/ppermute | solution.py:498
  37.1 4.3 %collective-permute-start.4 = (f32[2,128,256]{2,1,0:T(8,128)S(1)}, f32[2,128,256]{2,1,0:T(8,128)S(1)}, u32[]{:S(2)}, u32[]{:S(2)}) collective-permute-start(f32[2,128,256]{2,1,0:T(8,128)S(1)} %get-tuple-element.28), channel_id=1, source_target_pairs={{0,16},{16,0},{1,17},{17,1},{2,18},{18,2},{3,19},{19,3},{4,20},{20... | collective-permute-start | bytes 786440 | tf_op jit(solution)/shard_map/ppermute | solution.py:489
  41.4 1.5 %collective-permute-done.3.refs_3_.refs_2_.refs_6_ = f32[2,128,256]{2,1,0:T(8,128)S(1)} collective-permute-done((f32[2,128,256]{2,1,0:T(8,128)S(1)}, f32[2,128,256]{2,1,0:T(8,128)S(1)}, u32[]{:S(2)}, u32[]{:S(2)}) %collective-permute-start.3) | collective-permute-done | bytes 262176 | tf_op jit(solution)/shard_map/ppermute | solution.py:489
  42.9 4.0 %collective-permute-start.6 = (f32[2,128,256]{2,1,0:T(8,128)S(1)}, f32[2,128,256]{2,1,0:T(8,128)S(1)}, u32[]{:S(2)}, u32[]{:S(2)}) collective-permute-start(f32[2,128,256]{2,1,0:T(8,128)S(1)} %collective-permute-done.3.refs_3_.refs_2_.refs_6_), channel_id=1, source_target_pairs={{0,1},{1,2},{2,3},{17,16},{18,17},{19,18},{4,5},{5,6},{6,7},{21,20... | collective-permute-start | bytes 786440 | tf_op jit(solution)/shard_map/ppermute | solution.py:498
  46.9 0.8 %collective-permute-start.1 = (f32[12,64,128]{2,1,0:T(8,128)S(1)}, f32[12,64,128]{2,1,0:T(8,128)S(1)}, u32[]{:S(2)}, u32[]{:S(2)}) collective-permute-start(f32[12,64,128]{2,1,0:T(8,128)S(1)} %slice.41.refs_0_), channel_id=1, source_target_pairs={{0,16},{16,0},{1,17},{17,1},{2,18},{18,2},{3,19},{19,3},{4,20},{20... | collective-permute-start | bytes 1179656 | tf_op jit(solution)/shard_map/ppermute | solution.py:489
  47.8 3.6 %collective-permute-done.4.refs_4_.refs_7_ = f32[2,128,256]{2,1,0:T(8,128)S(1)} collective-permute-done((f32[2,128,256]{2,1,0:T(8,128)S(1)}, f32[2,128,256]{2,1,0:T(8,128)S(1)}, u32[]{:S(2)}, u32[]{:S(2)}) %collective-permute-start.4) | collective-permute-done | bytes 262176 | tf_op jit(solution)/shard_map/ppermute | solution.py:489
  51.3 1.7 %collective-permute-start.9 = (f32[2,128,256]{2,1,0:T(8,128)S(1)}, f32[2,128,256]{2,1,0:T(8,128)S(1)}, u32[]{:S(2)}, u32[]{:S(2)}) collective-permute-start(f32[2,128,256]{2,1,0:T(8,128)S(1)} %pad_maximum_fusion.1), channel_id=1, source_target_pairs={{0,12},{4,0},{8,4},{12,8},{1,13},{5,1},{9,5},{13,9},{2,14},{6,2},{... | collective-permute-start | bytes 786440 | tf_op jit(solution)/shard_map/ppermute | solution.py:489
  53.1 4.0 %collective-permute-start.7 = (f32[2,128,256]{2,1,0:T(8,128)S(1)}, f32[2,128,256]{2,1,0:T(8,128)S(1)}, u32[]{:S(2)}, u32[]{:S(2)}) collective-permute-start(f32[2,128,256]{2,1,0:T(8,128)S(1)} %collective-permute-done.4.refs_4_.refs_7_), channel_id=1, source_target_pairs={{0,1},{1,2},{2,3},{17,16},{18,17},{19,18},{4,5},{5,6},{6,7},{21,20... | collective-permute-start | bytes 786440 | tf_op jit(solution)/shard_map/ppermute | solution.py:498
  57.1 0.8 %shard_map.67 = (bf16[2,8,32,256]{3,2,1,0:T(8,128)(2,1)S(1)}, f32[8,32,128]{2,1,0:T(8,128)}) custom-call(f32[8,32,128]{2,1,0:T(8,128)S(1)} %constant_dynamic-update-slice_fusion.refs_0_, f32[8,32,128]{2,1,0:T(8,128)S(1)} %collective-permute-done.12.refs_1_), custom_call_target="tpu_custom_call" | custom-call | flops 524288 | bytes 524288 | tf_op jit(solution)/shard_map/pallas_call | solution.py:215
  57.9 0.7 %corners.1 = (f32[4,32,128]{2,1,0:T(8,128)S(1)}, f32[4,32,128]{2,1,0:T(8,128)S(1)}) custom-call(bf16[2,8,32,256]{3,2,1,0:T(8,128)(2,1)S(1)} %get-tuple-element.30.refs_0_, f32[4,128,256]{2,1,0:T(8,128)S(1)} %get-tuple-element.26.refs_2_.refs_1_.refs_4_, f32[2,128,256]{2,1,0:T(8,128)S(1)} %collective-permute-done.3.refs_3_.refs_2_.refs_6_, ...), custom_call_target="tpu_custom_call" | custom-call | flops 100663296 | bytes 524288 | tf_op jit(solution)/shard_map/corners/pallas_call | solution.py:396
  58.6 0.1 collective-permute-start.13
  58.6 1.7 %collective-permute-start.14 = (f32[4,32,128]{2,1,0:T(8,128)S(1)}, f32[4,32,128]{2,1,0:T(8,128)S(1)}, u32[]{:S(2)}, u32[]{:S(2)}) collective-permute-start(f32[4,32,128]{2,1,0:T(8,128)S(1)} %get-tuple-element.32), channel_id=1, source_target_pairs={{0,12},{4,0},{8,4},{12,8},{1,13},{5,1},{9,5},{13,9},{2,14},{6,2},{... | collective-permute-start | bytes 196616 | tf_op jit(solution)/shard_map/ppermute | solution.py:489
  60.4 0.4 shard_map.65
  60.8 0.6 shard_map.64
  61.4 1.3 %shard_map.66.refs_2_ = f32[20,64,128]{2,1,0:T(8,128)S(1)} custom-call(bf16[2,20,64,256]{3,2,1,0:T(8,128)(2,1)S(1)} %get-tuple-element.19.refs_0_, f32[20,64,128]{2,1,0:T(8,128)S(1)} %get-tuple-element.22.refs_1_, f32[4,128,256]{2,1,0:T(8,128)S(1)} %get-tuple-element.26.refs_2_.refs_1_.refs_4_, ...), custom_call_target="tpu_custom_call" | custom-call | flops 402653184 | bytes 3014656 | tf_op jit(solution)/shard_map/pallas_call | solution.py:472
  62.8 3.5 %shard_map.68 = f32[32,64,128]{2,1,0:T(8,128)} custom-call(bf16[2,20,64,256]{3,2,1,0:T(8,128)(2,1)S(1)} %get-tuple-element.19.refs_0_, bf16[2,12,64,256]{3,2,1,0:T(8,128)(2,1)S(1)} %get-tuple-element.21.refs_1_, f32[20,64,128]{2,1,0:T(8,128)S(1)} %shard_map.66.refs_2_, f32[12,64,128]{2,1,0:T(8,128)S(1)} %get-tuple-element.29.refs_3_, ...), custom_call_target="tpu_custom_call" | custom-call | flops 805306368 | bytes 5898240 | tf_op jit(solution)/shard_map/pallas_call | solution.py:472
  (29 shorter events, 0.3 us)
Async XLA Ops:
  0.0 1.2 %copy-start = (f32[128,1,1,2048]{3,2,1,0:T(1,128)S(1)}, f32[128,1,1,2048]{3,2,1,0:T(1,128)}, u32[]{:S(2)}) copy-start(f32[128,1,1,2048]{3,2,1,0:T(1,128)} %param.7) | copy-start | bytes 3145732
  0.0 5.1 %copy-start.4 = (f32[128,32,64]{0,2,1:T(8,128)S(1)}, f32[128,32,64]{0,2,1:T(8,128)}, u32[]{:S(2)}) copy-start(f32[128,32,64]{0,2,1:T(8,128)} %param.6) | copy-start | bytes 3145732
  2.2 16.0 %collective-permute-start.2 = (f32[128,1024]{1,0:T(8,128)}, f32[128,1024]{1,0:T(8,128)S(1)}, u32[]{:S(2)}, u32[]{:S(2)}) collective-permute-start(f32[128,1024]{1,0:T(8,128)} %bitcast.2), channel_id=1, source_target_pairs={{0,16},{16,0},{1,17},{17,1},{2,18},{18,2},{3,19},{19,3},{4,20},{20... | collective-permute-start | bytes 1572872 | tf_op jit(solution)/shard_map/ppermute | solution.py:489
  5.2 3.2 %collective-permute-start.10 = (f32[4,32,128]{2,1,0:T(8,128)S(1)}, f32[4,32,128]{2,1,0:T(8,128)S(1)}, u32[]{:S(2)}, u32[]{:S(2)}) collective-permute-start(f32[4,32,128]{2,1,0:T(8,128)S(1)} %get-tuple-element.36), channel_id=1, source_target_pairs={{0,12},{4,0},{8,4},{12,8},{1,13},{5,1},{9,5},{13,9},{2,14},{6,2},{... | collective-permute-start | bytes 196616 | tf_op jit(solution)/shard_map/ppermute | solution.py:489
  5.9 29.8 %collective-permute-start.11 = (f32[4,32,128]{2,1,0:T(8,128)S(1)}, f32[4,32,128]{2,1,0:T(8,128)S(1)}, u32[]{:S(2)}, u32[]{:S(2)}) collective-permute-start(f32[4,32,128]{2,1,0:T(8,128)S(1)} %get-tuple-element.35), channel_id=1, source_target_pairs={{0,4},{4,8},{8,12},{12,0},{1,5},{5,9},{9,13},{13,1},{2,6},{6,10},{... | collective-permute-start | bytes 196616 | tf_op jit(solution)/shard_map/ppermute | solution.py:489
  6.0 52.6 %collective-permute-start = (f32[20,64,128]{2,1,0:T(8,128)S(1)}, f32[20,64,128]{2,1,0:T(8,128)S(1)}, u32[]{:S(2)}, u32[]{:S(2)}) collective-permute-start(f32[20,64,128]{2,1,0:T(8,128)S(1)} %slice.40.refs_0_), channel_id=1, source_target_pairs={{0,16},{16,0},{1,17},{17,1},{2,18},{18,2},{3,19},{19,3},{4,20},{20... | collective-permute-start | bytes 1966088 | tf_op jit(solution)/shard_map/ppermute | solution.py:489
  7.6 10.6 %copy-start.1 = (f32[1,1,1,1024]{3,2,1,0:T(1,128)S(1)}, f32[1,1,1,1024]{3,2,1,0:T(1,128)}, u32[]{:S(2)}) copy-start(f32[1,1,1,1024]{3,2,1,0:T(1,128)} %param.8) | copy-start | bytes 12292
  7.6 10.5 %copy-start.2 = (f32[1,1,1,1024]{3,2,1,0:T(1,128)S(1)}, f32[1,1,1,1024]{3,2,1,0:T(1,128)}, u32[]{:S(2)}) copy-start(f32[1,1,1,1024]{3,2,1,0:T(1,128)} %param.9) | copy-start | bytes 12292
  7.6 10.5 %copy-start.3 = (s32[1,1,1,1024]{3,2,1,0:T(1,128)S(1)}, s32[1,1,1,1024]{3,2,1,0:T(1,128)}, u32[]{:S(2)}) copy-start(s32[1,1,1,1024]{3,2,1,0:T(1,128)} %param.10) | copy-start | bytes 12292
  33.6 9.2 %collective-permute-start.3 = (f32[2,128,256]{2,1,0:T(8,128)S(1)}, f32[2,128,256]{2,1,0:T(8,128)S(1)}, u32[]{:S(2)}, u32[]{:S(2)}) collective-permute-start(f32[2,128,256]{2,1,0:T(8,128)S(1)} %get-tuple-element.27), channel_id=1, source_target_pairs={{0,16},{16,0},{1,17},{17,1},{2,18},{18,2},{3,19},{19,3},{4,20},{20... | collective-permute-start | bytes 786440 | tf_op jit(solution)/shard_map/ppermute | solution.py:489
  35.7 11.2 %collective-permute-start.12 = (f32[8,32,128]{2,1,0:T(8,128)S(1)}, f32[8,32,128]{2,1,0:T(8,128)S(1)}, u32[]{:S(2)}, u32[]{:S(2)}) collective-permute-start(f32[8,32,128]{2,1,0:T(8,128)S(1)} %constant_dynamic-update-slice_fusion.refs_0_), channel_id=1, source_target_pairs={{0,16},{16,0},{1,17},{17,1},{2,18},{18,2},{3,19},{19,3},{4,20},{20... | collective-permute-start | bytes 393224 | tf_op jit(solution)/shard_map/ppermute | solution.py:489
  35.8 17.2 %collective-permute-start.5 = (f32[4,128,256]{2,1,0:T(8,128)S(1)}, f32[4,128,256]{2,1,0:T(8,128)S(1)}, u32[]{:S(2)}, u32[]{:S(2)}) collective-permute-start(f32[4,128,256]{2,1,0:T(8,128)S(1)} %get-tuple-element.26.refs_2_.refs_1_.refs_4_), channel_id=1, source_target_pairs={{16,17},{17,18},{18,19},{1,0},{2,1},{3,2},{20,21},{21,22},{22,23},... | collective-permute-start | bytes 1572872 | tf_op jit(solution)/shard_map/ppermute | solution.py:498
  37.1 14.2 %collective-permute-start.4 = (f32[2,128,256]{2,1,0:T(8,128)S(1)}, f32[2,128,256]{2,1,0:T(8,128)S(1)}, u32[]{:S(2)}, u32[]{:S(2)}) collective-permute-start(f32[2,128,256]{2,1,0:T(8,128)S(1)} %get-tuple-element.28), channel_id=1, source_target_pairs={{0,16},{16,0},{1,17},{17,1},{2,18},{18,2},{3,19},{19,3},{4,20},{20... | collective-permute-start | bytes 786440 | tf_op jit(solution)/shard_map/ppermute | solution.py:489
  42.9 8.4 %collective-permute-start.6 = (f32[2,128,256]{2,1,0:T(8,128)S(1)}, f32[2,128,256]{2,1,0:T(8,128)S(1)}, u32[]{:S(2)}, u32[]{:S(2)}) collective-permute-start(f32[2,128,256]{2,1,0:T(8,128)S(1)} %collective-permute-done.3.refs_3_.refs_2_.refs_6_), channel_id=1, source_target_pairs={{0,1},{1,2},{2,3},{17,16},{18,17},{19,18},{4,5},{5,6},{6,7},{21,20... | collective-permute-start | bytes 786440 | tf_op jit(solution)/shard_map/ppermute | solution.py:498
  46.9 11.6 %collective-permute-start.1 = (f32[12,64,128]{2,1,0:T(8,128)S(1)}, f32[12,64,128]{2,1,0:T(8,128)S(1)}, u32[]{:S(2)}, u32[]{:S(2)}) collective-permute-start(f32[12,64,128]{2,1,0:T(8,128)S(1)} %slice.41.refs_0_), channel_id=1, source_target_pairs={{0,16},{16,0},{1,17},{17,1},{2,18},{18,2},{3,19},{19,3},{4,20},{20... | collective-permute-start | bytes 1179656 | tf_op jit(solution)/shard_map/ppermute | solution.py:489
  51.3 11.4 %collective-permute-start.8 = (f32[2,128,256]{2,1,0:T(8,128)S(1)}, f32[2,128,256]{2,1,0:T(8,128)S(1)}, u32[]{:S(2)}, u32[]{:S(2)}) collective-permute-start(f32[2,128,256]{2,1,0:T(8,128)S(1)} %pad_maximum_fusion), channel_id=1, source_target_pairs={{0,4},{4,8},{8,12},{12,0},{1,5},{5,9},{9,13},{13,1},{2,6},{6,10},{... | collective-permute-start | bytes 786440 | tf_op jit(solution)/shard_map/ppermute | solution.py:489
  51.3 11.4 %collective-permute-start.9 = (f32[2,128,256]{2,1,0:T(8,128)S(1)}, f32[2,128,256]{2,1,0:T(8,128)S(1)}, u32[]{:S(2)}, u32[]{:S(2)}) collective-permute-start(f32[2,128,256]{2,1,0:T(8,128)S(1)} %pad_maximum_fusion.1), channel_id=1, source_target_pairs={{0,12},{4,0},{8,4},{12,8},{1,13},{5,1},{9,5},{13,9},{2,14},{6,2},{... | collective-permute-start | bytes 786440 | tf_op jit(solution)/shard_map/ppermute | solution.py:489
  53.1 9.7 %collective-permute-start.7 = (f32[2,128,256]{2,1,0:T(8,128)S(1)}, f32[2,128,256]{2,1,0:T(8,128)S(1)}, u32[]{:S(2)}, u32[]{:S(2)}) collective-permute-start(f32[2,128,256]{2,1,0:T(8,128)S(1)} %collective-permute-done.4.refs_4_.refs_7_), channel_id=1, source_target_pairs={{0,1},{1,2},{2,3},{17,16},{18,17},{19,18},{4,5},{5,6},{6,7},{21,20... | collective-permute-start | bytes 786440 | tf_op jit(solution)/shard_map/ppermute | solution.py:498
  58.6 4.2 %collective-permute-start.13 = (f32[4,32,128]{2,1,0:T(8,128)S(1)}, f32[4,32,128]{2,1,0:T(8,128)S(1)}, u32[]{:S(2)}, u32[]{:S(2)}) collective-permute-start(f32[4,32,128]{2,1,0:T(8,128)S(1)} %get-tuple-element.31), channel_id=1, source_target_pairs={{0,4},{4,8},{8,12},{12,0},{1,5},{5,9},{9,13},{13,1},{2,6},{6,10},{... | collective-permute-start | bytes 196616 | tf_op jit(solution)/shard_map/ppermute | solution.py:489
  58.6 4.1 %collective-permute-start.14 = (f32[4,32,128]{2,1,0:T(8,128)S(1)}, f32[4,32,128]{2,1,0:T(8,128)S(1)}, u32[]{:S(2)}, u32[]{:S(2)}) collective-permute-start(f32[4,32,128]{2,1,0:T(8,128)S(1)} %get-tuple-element.32), channel_id=1, source_target_pairs={{0,12},{4,0},{8,4},{12,8},{1,13},{5,1},{9,5},{13,9},{2,14},{6,2},{... | collective-permute-start | bytes 196616 | tf_op jit(solution)/shard_map/ppermute | solution.py:489

commit v5 on v3

--- a/solution.py
+++ b/solution.py
@@ -73,7 +73,7 @@
     others = refs[: bands - 1]
     departure_ref, variance_ref, nearest_ref = refs[bands - 1 : bands + 2]
     outs = refs[bands + 2 : 3 * bands + 1]
-    y_ref, cov_ref, right_ref, root_ref, inv_ref = refs[3 * bands + 1 :]
+    y_ref, z_ref, cov_ref, right_ref, root_ref, inv_ref = refs[3 * bands + 1 :]
     me = lax.axis_index("mem")
     part, slots = own_ref.shape
     members = y_ref.shape[0]
@@ -85,21 +85,36 @@
     identity = (rows == columns).astype(F32)
     live = (lax.broadcasted_iota(jnp.int32, (1, slots), 1) < live_ref[0]).astype(F32)
     base = live * lax.rsqrt(variance_ref[...])
-    scales, roots = [], []
-    for g, point in enumerate(points):
-        distance = (nearest_ref[...] - point).astype(F32)
+    scales, roots, sums = [], [], []
+    count = len(points)
+
+    def split(g):
+        distance = (nearest_ref[...] - points[g]).astype(F32)
         weight = jnp.exp(-0.25 * distance * distance) * base
-        y = split2(y_ref[...] * weight)
-        cross = dot_nt(y[0], y[1])
-        cov = dot_nt(y[0], y[0]) + dot_nt(y[1], y[1]) + (cross + cross.T)
+        y0, y1 = split2(y_ref[...] * weight)
+        d0, d1 = split2(weight * departure_ref[...])
+        z_ref[g, :members], z_ref[g, members : 2 * members] = y0, y1
+        z_ref[g, 2 * members :] = jnp.concatenate(
+            [jnp.broadcast_to(d0, (16, slots)), jnp.broadcast_to(d1, (16, slots))], axis=0
+        )
+
+    split(0)
+    for g in range(count):
+        first = dot_nt(z_ref[g], z_ref[g, :members])
+        if g + 1 < count:
+            split(g + 1)
+        second = dot_nt(z_ref[g, members : 2 * members + 16], z_ref[g, members : 2 * members])
+        sums.append((first, second))
+    for first, second in sums:
+        cross = first[members : 2 * members]
+        cov = first[:members] + second[:members] + (cross + cross.T)
         cov = cov + (members - 1.0) * identity
-        d0, d1 = split2(jnp.broadcast_to(weight * departure_ref[...], (8, slots)))
-        right_ref[g] = dot_nt(d0, y[0]) + dot_nt(d0, y[1]) + dot_nt(d1, y[0])
+        right = first[2 * members :]
+        right_ref[len(roots)] = right[:8] + right[16:24] + second[members : members + 8]
         square_sum = jnp.sum(jnp.sum(cov * cov, axis=1, keepdims=True), axis=0, keepdims=True)
         scale = lax.rsqrt(square_sum)
         scales.append(scale)
         roots.append(cov * scale)
-    count = len(points)
     us = quartics(roots, identity, mm1, mm1)
     for g in range(count):
         for i, piece in enumerate(split3(mm5(split3(roots[g]), us[g]))):
@@ -174,6 +189,7 @@
         out_specs=[vmem] * (2 * bands - 1),
         scratch_shapes=[
             pltpu.VMEM((members, slots), F32),
+            pltpu.VMEM((count, 2 * members + 32, slots), BF16),
             pltpu.VMEM((members, members), F32),
             pltpu.VMEM((count, 8, members), F32),
             pltpu.VMEM((count, 3, members, members), BF16),
@@ -241,13 +257,13 @@
     return [(ref, first - start) for ref, start in refs if start <= first][-1]
 
 
-def add_terms(geometry, intervals, x_refs, t_ref, before_refs, out_refs, mine):
+def add_terms(geometry, intervals, x_refs, t_ref, before_refs, out_refs, mine, bands_y=None):
     width, height, bands = geometry
     part = out_refs[0][0].shape[2]
     members = x_refs[0][0].shape[3]
     spacing = width // CGX
     depth = height // bands
-    for v in range(bands + 1):
+    for v in range(bands + 1) if bands_y is None else bands_y:
         j0, j1 = max(depth * v - depth // 2, 0), min(depth * v + depth // 2, height)
         tall = j1 - j0
         j = lax.broadcasted_iota(jnp.int32, (1, tall, 1), 1).astype(F32) + (
@@ -290,6 +306,7 @@
 def edge_slots(bands):
     names = [(row, column) for row in (0, bands + 1) for column in (1, CGX)]
     names += [(row, column) for row in range(1, bands + 1) for column in (0, CGX + 1)]
+    names += [(row, column) for row in range(1, bands + 1) for column in (CGX - 1, CGX)]
     return {name: n for n, name in enumerate(names)}
 
 
@@ -366,7 +383,7 @@
     bands = geometry[2]
     x_refs = list(zip(take(len(firsts)), firsts))
     before_refs = list(zip(take(len(firsts)), firsts))
-    rows, ends, sides = take(bands), take(bands), take(2)
+    rows, ends, mids, sides = take(bands), take(bands), take(bands - 1), take(2)
     out_ref, t_ref = refs
     me = lax.axis_index("mem")
     slots = edge_slots(bands)
@@ -385,9 +402,14 @@
             )
         for side in (0, 1):
             put(t_ref, slots[1, 0] + 2 * band + side, sides[side][shift])
-    add_terms(
-        geometry, range(CGX + 1), x_refs, t_ref, before_refs, [(out_ref, 0)], slots
-    )
+        for n, point in enumerate(POINTS):
+            if (1, point + 1) in slots:
+                value = rows[shift][n] if shift == 0 or n < 2 else mids[shift - 1][n - 2]
+                put(t_ref, slots[1, CGX - 1] + 2 * band + point + 2 - CGX, value)
+    rows_in, columns_in = range(1, bands + 1), range(1, CGX + 1)
+    late = {name: n for name, n in slots.items() if not (name[0] in rows_in and name[1] in columns_in)}
+    for intervals, mine in ((range(CGX - 1), late), (range(CGX - 1, CGX + 1), slots)):
+        add_terms(geometry, intervals, x_refs, t_ref, before_refs, [(out_ref, 0)], mine)
 
 
 def corner_kernel(bands, tiles_y, spacing, depth, *refs):
@@ -460,8 +482,19 @@
     x_refs = list(zip(take(len(firsts)), firsts))
     (before_ref,) = take(1)
     rows, ends, given = take(bands), take(bands), take(2)
-    out_ref, t_ref = refs
+    out_ref, t_ref, result_ref, sems = refs
     slots = last_slots(bands)
+    half, depth, _ = given[0].shape
+    tall = depth // 2
+
+    def leave(from_ref, start, stop, sem):
+        place = slice(start, stop)
+        return pltpu.make_async_copy(
+            from_ref.at[:, place, :], out_ref.at[:, place, :], sems.at[sem]
+        )
+
+    middle = leave(before_ref, tall, height - tall, 0)
+    middle.start()
     for shift in range(bands):
         for n in range(CGX - 2):
             k = 2 + n if shift == 0 else n
@@ -475,26 +508,30 @@
                 lambda shift=shift, k=k: rows[shift][k],
                 lambda shift=shift, k=k: ends[shift][k],
             )
-    add_terms(
-        geometry,
-        range(CGX + 1),
-        x_refs,
-        t_ref,
-        [(before_ref, 0)],
-        [(out_ref, 0)],
-        slots,
-    )
-    half, depth, _ = given[0].shape
-    for ref, first in zip(given, (0, width - half)):
-        for start, cells in ((0, 0), (depth // 2, height - depth // 2)):
-            place = slice(cells, cells + depth // 2)
-            out_ref[first : first + half, place, :] = (
-                before_ref[first : first + half, place, :]
-                + ref[:, start : start + depth // 2, :]
+    copies = [middle]
+    for end, (v, j) in enumerate(((0, 0), (bands, height - tall))):
+        add_terms(
+            geometry,
+            range(CGX + 1),
+            x_refs,
+            t_ref,
+            [(before_ref, 0)],
+            [(result_ref, 0)],
+            slots,
+            (v,),
+        )
+        for ref, first in zip(given, (0, width - half)):
+            result_ref[first : first + half, j : j + tall, :] = (
+                before_ref[first : first + half, j : j + tall, :]
+                + ref[:, end * tall : (end + 1) * tall, :]
             )
-
-
-def apply_terms(kernel, width, xs, befores, operands, slots, flops):
+        copies.append(leave(result_ref, j, j + tall, end + 1))
+        copies[-1].start()
+    for copy in copies:
+        copy.wait()
+
+
+def apply_terms(kernel, width, xs, befores, operands, slots, flops, copies=False):
     _, _, height, members = xs[0].shape
     part = befores[0].shape[2]
     vmem = pl.BlockSpec(memory_space=pltpu.VMEM)
@@ -504,8 +541,9 @@
         kernel,
         out_shape=jax.ShapeDtypeStruct((width, height, part), F32),
         in_specs=[vmem] * len(operands),
-        out_specs=vmem,
-        scratch_shapes=[pltpu.VMEM((len(slots), 2, part, members), BF16)],
+        out_specs=pl.BlockSpec(memory_space=pl.ANY) if copies else vmem,
+        scratch_shapes=[pltpu.VMEM((len(slots), 2, part, members), BF16)]
+        + [pltpu.VMEM((width, height, part), F32), pltpu.SemaphoreType.DMA((3,))] * copies,
         compiler_params=pltpu.CompilerParams(
             vmem_limit_bytes=min(size + 8 * width * height * part + 16 * MIB, 60 * MIB)
         ),
@@ -567,7 +605,8 @@
         return blocks
 
     firsts = (0, column_intervals(width)[CGX - 1][0])
-    cells = [gathered(tile[: firsts[1]]), gathered(tile[firsts[1] :])]
+    second = tile[firsts[1] :]
+    cells = [gathered(tile[: firsts[1]]), gathered(second)]
     edges = gathered(edge)
     solved = solve(
         POINTS,
@@ -613,14 +652,13 @@
 
     inner_first = inner(x_first, mean_first, range(CGX - 1), 0)
     x_second, mean_second = prepare(cells[1], part)
-    inner_second = inner(x_second, mean_second, range(CGX - 1, CGX + 1), firsts[1])
     xs = [x_first, x_second]
     result = apply_terms(
         functools.partial(edge_kernel, geometry, firsts, tiles_y),
         width,
         xs,
-        [inner_first, inner_second],
-        [row] + other_side + [own_end] + ends_side + row_sides,
+        [inner_first, mean_second],
+        [row] + other_side + [own_end] + ends_side + other_mid + row_sides,
         edge_slots(bands),
         work,
     )
@@ -632,6 +670,7 @@
         [row] + other_mid + [own_end] + ends_mid + given,
         last_slots(bands),
         work // 2,
+        copies=True,
     )
     return result.transpose(2, 0, 1)
 

time: 87.2 us -> 85 us (0.975)
  Pallas kernels: 24.1 us -> 22.5 us
    pallas_call x1, Pallas kernels: 16.6 us -> 15.5 us  [solve(): pl.pallas_call(functools.partial(solve_kernel, points, bands), out_shape=...]
    pallas_call x4 -> x3, Pallas kernels: 5.16 us -> 4.72 us  [apply_terms(): pl.pallas_call(kernel, out_shape=jax.ShapeDtypeStruct((width, height, par...]
  transfers between devices with their start and end apart: 15 -> 15, of which waited for: 4 -> 4; matrix products, arithmetic and copies ran while one was open for 3% -> 3% of each run, Pallas kernels for 26% -> 25%
where the time goes in v5:
time: 85 us; the launch traced here: 84.7 us
  waiting for transfers between devices  35.8 us (42%)
  Pallas kernels  22.5 us (26%)
  starting transfers between devices  21.8 us (26%)
  local copies, waits for them, and re-layouts  3.42 us (4%)
  between operations  1.09 us (1%)
    ppermute x12, waiting for transfers between devices, shifted(): lax.ppermute(array, axis, [(i, (i + by) % size) for i in range(size)])  35.8 us
    pallas_call x1, Pallas kernels, solve(): pl.pallas_call(functools.partial(solve_kernel, points, bands), out_shape=...  15.5 us
    ppermute x12, starting transfers between devices, shifted(): lax.ppermute(array, axis, [(i, (i + by) % size) for i in range(size)])  13.2 us
    ppermute x3, starting transfers between devices, to_next_tile(): return lax.ppermute(array, ('mem', 'gy'), pairs)  8.64 us
    pallas_call x3, Pallas kernels, apply_terms(): pl.pallas_call(kernel, out_shape=jax.ShapeDtypeStruct((width, height, par...  4.72 us
    pallas_call x3, Pallas kernels, prepare(): pl.pallas_call(functools.partial(prepare_kernel, len(cells)), out_shape=[...  1.82 us
  transfers between devices with their start and end apart: 15, of which 4 were waited for; matrix products, arithmetic and copies ran while one was open for 3% of the time, Pallas kernels for 25%

profile of v5, /device:TPU:0, one launch (start us, length us, event | category | flops | bytes accessed | tf_op | source)
XLA Modules:
  0.0 84.7 jit_solution(14630946256631770610)
XLA Ops:
  0.0 1.2 %slice.40.refs_0_ = f32[20,64,128]{2,1,0:T(8,128)S(1)} slice(f32[32,64,128]{2,1,0:T(8,128)} %bitcast.15), slice={[0:20], [0:64], [0:128]} | slice | bytes 1310720 | tf_op jit(solution)/shard_map/slice | solution.py:609
  1.2 3.1 %collective-permute-start = (f32[20,64,128]{2,1,0:T(8,128)S(1)}, f32[20,64,128]{2,1,0:T(8,128)S(1)}, u32[]{:S(2)}, u32[]{:S(2)}) collective-permute-start(f32[20,64,128]{2,1,0:T(8,128)S(1)} %slice.40.refs_0_), channel_id=1, source_target_pairs={{0,16},{16,0},{1,17},{17,1},{2,18},{18,2},{3,19},{19,3},{4,20},{20... | collective-permute-start | bytes 1966088 | tf_op jit(solution)/shard_map/ppermute | solution.py:558
  4.3 1.0 %slice.41.refs_0_ = f32[12,64,128]{2,1,0:T(8,128)S(1)} slice(f32[32,64,128]{2,1,0:T(8,128)} %bitcast.16), slice={[20:32], [0:64], [0:128]} | slice | bytes 786432 | tf_op jit(solution)/shard_map/slice | solution.py:608
  5.3 0.1 collective-permute-start.1
  5.4 0.0 copy-start.4
  5.5 0.9 %copy.9 = f32[128,1,1,1024]{3,0,2,1:T(8,128)} copy(f32[128,1,1,1024]{3,2,1,0:T(1,128)S(1)} %constant_dynamic-slice_fusion.1) | data formatting | bytes 1048576 | tf_op jit(solution)/shard_map/optimization_barrier | solution.py:582
  6.4 2.0 %collective-permute-start.2 = (f32[128,1024]{1,0:T(8,128)}, f32[128,1024]{1,0:T(8,128)}, u32[]{:S(2)}, u32[]{:S(2)}) collective-permute-start(f32[128,1024]{1,0:T(8,128)} %bitcast.2), channel_id=1, source_target_pairs={{0,16},{16,0},{1,17},{17,1},{2,18},{18,2},{3,19},{19,3},{4,20},{20... | collective-permute-start | bytes 1572872 | tf_op jit(solution)/shard_map/ppermute | solution.py:558
  8.4 0.1 collective-permute-start.10
  8.6 0.4 collective-permute-start.11
  9.7 0.1 copy.11
  9.8 0.7 collective-permute-done.10
  10.5 28.3 %collective-permute-done.2.refs_0_ = f32[128,1024]{1,0:T(8,128)} collective-permute-done((f32[128,1024]{1,0:T(8,128)}, f32[128,1024]{1,0:T(8,128)}, u32[]{:S(2)}, u32[]{:S(2)}) %collective-permute-start.2) | collective-permute-done | bytes 524320 | tf_op jit(solution)/shard_map/ppermute | solution.py:558
  38.8 15.5 %solve.1 = (f32[4,128,256]{2,1,0:T(8,128)S(1)}, f32[2,128,256]{2,1,0:T(8,128)S(1)}, f32[2,128,256]{2,1,0:T(8,128)S(1)}) custom-call(s32[1]{0:T(128)} %bitcast.10.live_ref, f32[128,1024]{1,0:T(8,128)S(1)} %bitcast.11, f32[128,1024]{1,0:T(8,128)} %collective-permute-done.2.refs_0_, f32[1,1024]{1,0:T(1,128)S(1)} %bitcast.12, f32[1,1024]{1,0:T(1,128)S(1)} %bitcast.13, ...), custom_call_target="tpu_custom_call" | custom-call | flops 11140071424 | bytes 2097152 | tf_op jit(solution)/shard_map/solve/pallas_call | solution.py:180
  54.3 1.8 %collective-permute-start.3 = (f32[2,128,256]{2,1,0:T(8,128)S(1)}, f32[2,128,256]{2,1,0:T(8,128)S(1)}, u32[]{:S(2)}, u32[]{:S(2)}) collective-permute-start(f32[2,128,256]{2,1,0:T(8,128)S(1)} %get-tuple-element.23), channel_id=1, source_target_pairs={{0,16},{16,0},{1,17},{17,1},{2,18},{18,2},{3,19},{19,3},{4,20},{20... | collective-permute-start | bytes 786440 | tf_op jit(solution)/shard_map/ppermute | solution.py:558
  56.1 0.3 collective-permute-start.12
  56.5 1.3 %collective-permute-start.5 = (f32[4,128,256]{2,1,0:T(8,128)S(1)}, f32[4,128,256]{2,1,0:T(8,128)S(1)}, u32[]{:S(2)}, u32[]{:S(2)}) collective-permute-start(f32[4,128,256]{2,1,0:T(8,128)S(1)} %get-tuple-element.22.refs_2_.refs_4_.refs_1_.refs_3_), channel_id=1, source_target_pairs={{16,17},{17,18},{18,19},{1,0},{2,1},{3,2},{20,21},{21,22},{22,23},... | collective-permute-start | bytes 1572872 | tf_op jit(solution)/shard_map/ppermute | solution.py:567
  57.8 5.8 %collective-permute-done.3.refs_3_.refs_5_.refs_2_ = f32[2,128,256]{2,1,0:T(8,128)S(1)} collective-permute-done((f32[2,128,256]{2,1,0:T(8,128)S(1)}, f32[2,128,256]{2,1,0:T(8,128)S(1)}, u32[]{:S(2)}, u32[]{:S(2)}) %collective-permute-start.3) | collective-permute-done | bytes 262176 | tf_op jit(solution)/shard_map/ppermute | solution.py:558
  63.5 1.8 %collective-permute-start.4 = (f32[2,128,256]{2,1,0:T(8,128)S(1)}, f32[2,128,256]{2,1,0:T(8,128)S(1)}, u32[]{:S(2)}, u32[]{:S(2)}) collective-permute-start(f32[2,128,256]{2,1,0:T(8,128)S(1)} %get-tuple-element.24), channel_id=1, source_target_pairs={{0,16},{16,0},{1,17},{17,1},{2,18},{18,2},{3,19},{19,3},{4,20},{20... | collective-permute-start | bytes 786440 | tf_op jit(solution)/shard_map/ppermute | solution.py:558
  65.3 1.0 %collective-permute-done.12.refs_1_ = f32[8,32,128]{2,1,0:T(8,128)S(1)} collective-permute-done((f32[8,32,128]{2,1,0:T(8,128)S(1)}, f32[8,32,128]{2,1,0:T(8,128)S(1)}, u32[]{:S(2)}, u32[]{:S(2)}) %collective-permute-start.12) | collective-permute-done | bytes 131104 | tf_op jit(solution)/shard_map/ppermute | solution.py:558
  66.3 3.7 %collective-permute-start.6 = (f32[2,128,256]{2,1,0:T(8,128)S(1)}, f32[2,128,256]{2,1,0:T(8,128)S(1)}, u32[]{:S(2)}, u32[]{:S(2)}) collective-permute-start(f32[2,128,256]{2,1,0:T(8,128)S(1)} %collective-permute-done.3.refs_3_.refs_5_.refs_2_), channel_id=1, source_target_pairs={{0,1},{1,2},{2,3},{17,16},{18,17},{19,18},{4,5},{5,6},{6,7},{21,20... | collective-permute-start | bytes 786440 | tf_op jit(solution)/shard_map/ppermute | solution.py:567
  70.1 0.1 collective-permute-start.7
  70.2 1.7 %collective-permute-start.8 = (f32[2,128,256]{2,1,0:T(8,128)S(1)}, f32[2,128,256]{2,1,0:T(8,128)S(1)}, u32[]{:S(2)}, u32[]{:S(2)}) collective-permute-start(f32[2,128,256]{2,1,0:T(8,128)S(1)} %pad_maximum_fusion.1), channel_id=1, source_target_pairs={{0,12},{4,0},{8,4},{12,8},{1,13},{5,1},{9,5},{13,9},{2,14},{6,2},{... | collective-permute-start | bytes 786440 | tf_op jit(solution)/shard_map/ppermute | solution.py:558
  71.9 3.7 %collective-permute-start.9 = (f32[2,128,256]{2,1,0:T(8,128)S(1)}, f32[2,128,256]{2,1,0:T(8,128)S(1)}, u32[]{:S(2)}, u32[]{:S(2)}) collective-permute-start(f32[2,128,256]{2,1,0:T(8,128)S(1)} %collective-permute-done.4.refs_4_.refs_8_), channel_id=1, source_target_pairs={{0,1},{1,2},{2,3},{17,16},{18,17},{19,18},{4,5},{5,6},{6,7},{21,20... | collective-permute-start | bytes 786440 | tf_op jit(solution)/shard_map/ppermute | solution.py:567
  75.6 0.8 shard_map.68
  76.4 0.4 shard_map.65
  76.7 0.6 shard_map.64
  77.4 0.5 corners.1
  77.9 0.1 collective-permute-start.13
  78.0 1.7 %collective-permute-start.14 = (f32[4,32,128]{2,1,0:T(8,128)S(1)}, f32[4,32,128]{2,1,0:T(8,128)S(1)}, u32[]{:S(2)}, u32[]{:S(2)}) collective-permute-start(f32[4,32,128]{2,1,0:T(8,128)S(1)} %get-tuple-element.28), channel_id=1, source_target_pairs={{0,12},{4,0},{8,4},{12,8},{1,13},{5,1},{9,5},{13,9},{2,14},{6,2},{... | collective-permute-start | bytes 196616 | tf_op jit(solution)/shard_map/ppermute | solution.py:558
  79.7 1.3 %shard_map.66.refs_2_ = f32[20,64,128]{2,1,0:T(8,128)S(1)} custom-call(bf16[2,20,64,256]{3,2,1,0:T(8,128)(2,1)S(1)} %get-tuple-element.17.refs_0_, f32[20,64,128]{2,1,0:T(8,128)S(1)} %get-tuple-element.19.refs_1_, f32[4,128,256]{2,1,0:T(8,128)S(1)} %get-tuple-element.22.refs_2_.refs_4_.refs_1_.refs_3_, ...), custom_call_target="tpu_custom_call" | custom-call | flops 754974720 | bytes 3014656 | tf_op jit(solution)/shard_map/pallas_call | solution.py:540
  81.1 1.9 %shard_map.67.refs_2_ = f32[32,64,128]{2,1,0:T(8,128)S(1)} custom-call(bf16[2,20,64,256]{3,2,1,0:T(8,128)(2,1)S(1)} %get-tuple-element.17.refs_0_, bf16[2,12,64,256]{3,2,1,0:T(8,128)(2,1)S(1)} %get-tuple-element.18.refs_1_, f32[20,64,128]{2,1,0:T(8,128)S(1)} %shard_map.66.refs_2_, f32[12,64,128]{2,1,0:T(8,128)S(1)} %get-tuple-element.25.refs_3_, ...), custom_call_target="tpu_custom_call" | custom-call | flops 402653184 | bytes 5505024 | tf_op jit(solution)/shard_map/pallas_call | solution.py:540
  83.1 1.5 %shard_map.69 = f32[32,64,128]{2,1,0:T(8,128)} custom-call(bf16[2,20,64,256]{3,2,1,0:T(8,128)(2,1)S(1)} %get-tuple-element.17.refs_0_, bf16[2,12,64,256]{3,2,1,0:T(8,128)(2,1)S(1)} %get-tuple-element.18.refs_1_, f32[32,64,128]{2,1,0:T(8,128)S(1)} %shard_map.67.refs_2_, f32[4,128,256]{2,1,0:T(8,128)S(1)} %get-tuple-element.22.refs_2_.refs_4_.refs_1_.refs_3_, ...), custom_call_target="tpu_custom_call" | custom-call | flops 201326592 | bytes 4849664 | tf_op jit(solution)/shard_map/pallas_call | solution.py:540
  (30 shorter events, 0.3 us)
Async XLA Ops:
  0.0 5.4 %copy-start = (f32[128,1,1,2048]{3,2,1,0:T(1,128)S(1)}, f32[128,1,1,2048]{3,2,1,0:T(1,128)}, u32[]{:S(2)}) copy-start(f32[128,1,1,2048]{3,2,1,0:T(1,128)} %param.7) | copy-start | bytes 3145732
  1.2 68.9 %collective-permute-start = (f32[20,64,128]{2,1,0:T(8,128)S(1)}, f32[20,64,128]{2,1,0:T(8,128)S(1)}, u32[]{:S(2)}, u32[]{:S(2)}) collective-permute-start(f32[20,64,128]{2,1,0:T(8,128)S(1)} %slice.40.refs_0_), channel_id=1, source_target_pairs={{0,16},{16,0},{1,17},{17,1},{2,18},{18,2},{3,19},{19,3},{4,20},{20... | collective-permute-start | bytes 1966088 | tf_op jit(solution)/shard_map/ppermute | solution.py:558
  5.3 64.8 %collective-permute-start.1 = (f32[12,64,128]{2,1,0:T(8,128)S(1)}, f32[12,64,128]{2,1,0:T(8,128)S(1)}, u32[]{:S(2)}, u32[]{:S(2)}) collective-permute-start(f32[12,64,128]{2,1,0:T(8,128)S(1)} %slice.41.refs_0_), channel_id=1, source_target_pairs={{0,16},{16,0},{1,17},{17,1},{2,18},{18,2},{3,19},{19,3},{4,20},{20... | collective-permute-start | bytes 1179656 | tf_op jit(solution)/shard_map/ppermute | solution.py:558
  5.4 2.9 %copy-start.4 = (f32[128,32,64]{0,2,1:T(8,128)S(1)}, f32[128,32,64]{0,2,1:T(8,128)}, u32[]{:S(2)}) copy-start(f32[128,32,64]{0,2,1:T(8,128)} %param.6) | copy-start | bytes 3145732
  6.4 32.4 %collective-permute-start.2 = (f32[128,1024]{1,0:T(8,128)}, f32[128,1024]{1,0:T(8,128)}, u32[]{:S(2)}, u32[]{:S(2)}) collective-permute-start(f32[128,1024]{1,0:T(8,128)} %bitcast.2), channel_id=1, source_target_pairs={{0,16},{16,0},{1,17},{17,1},{2,18},{18,2},{3,19},{19,3},{4,20},{20... | collective-permute-start | bytes 1572872 | tf_op jit(solution)/shard_map/ppermute | solution.py:558
  8.4 30.4 %copy-start.1 = (f32[1,1,1,1024]{3,2,1,0:T(1,128)S(1)}, f32[1,1,1,1024]{3,2,1,0:T(1,128)}, u32[]{:S(2)}) copy-start(f32[1,1,1,1024]{3,2,1,0:T(1,128)} %param.8) | copy-start | bytes 12292
  8.4 30.4 %copy-start.2 = (f32[1,1,1,1024]{3,2,1,0:T(1,128)S(1)}, f32[1,1,1,1024]{3,2,1,0:T(1,128)}, u32[]{:S(2)}) copy-start(f32[1,1,1,1024]{3,2,1,0:T(1,128)} %param.9) | copy-start | bytes 12292
  8.4 30.4 %copy-start.3 = (s32[1,1,1,1024]{3,2,1,0:T(1,128)S(1)}, s32[1,1,1,1024]{3,2,1,0:T(1,128)}, u32[]{:S(2)}) copy-start(s32[1,1,1,1024]{3,2,1,0:T(1,128)} %param.10) | copy-start | bytes 12292
  8.4 2.0 %collective-permute-start.10 = (f32[4,32,128]{2,1,0:T(8,128)S(1)}, f32[4,32,128]{2,1,0:T(8,128)S(1)}, u32[]{:S(2)}, u32[]{:S(2)}) collective-permute-start(f32[4,32,128]{2,1,0:T(8,128)S(1)} %get-tuple-element.32), channel_id=1, source_target_pairs={{0,12},{4,0},{8,4},{12,8},{1,13},{5,1},{9,5},{13,9},{2,14},{6,2},{... | collective-permute-start | bytes 196616 | tf_op jit(solution)/shard_map/ppermute | solution.py:558
  8.6 47.5 %collective-permute-start.11 = (f32[4,32,128]{2,1,0:T(8,128)S(1)}, f32[4,32,128]{2,1,0:T(8,128)S(1)}, u32[]{:S(2)}, u32[]{:S(2)}) collective-permute-start(f32[4,32,128]{2,1,0:T(8,128)S(1)} %get-tuple-element.31), channel_id=1, source_target_pairs={{0,4},{4,8},{8,12},{12,0},{1,5},{5,9},{9,13},{13,1},{2,6},{6,10},{... | collective-permute-start | bytes 196616 | tf_op jit(solution)/shard_map/ppermute | solution.py:558
  54.3 9.2 %collective-permute-start.3 = (f32[2,128,256]{2,1,0:T(8,128)S(1)}, f32[2,128,256]{2,1,0:T(8,128)S(1)}, u32[]{:S(2)}, u32[]{:S(2)}) collective-permute-start(f32[2,128,256]{2,1,0:T(8,128)S(1)} %get-tuple-element.23), channel_id=1, source_target_pairs={{0,16},{16,0},{1,17},{17,1},{2,18},{18,2},{3,19},{19,3},{4,20},{20... | collective-permute-start | bytes 786440 | tf_op jit(solution)/shard_map/ppermute | solution.py:558
  56.1 10.2 %collective-permute-start.12 = (f32[8,32,128]{2,1,0:T(8,128)S(1)}, f32[8,32,128]{2,1,0:T(8,128)S(1)}, u32[]{:S(2)}, u32[]{:S(2)}) collective-permute-start(f32[8,32,128]{2,1,0:T(8,128)S(1)} %constant_dynamic-update-slice_fusion.refs_0_), channel_id=1, source_target_pairs={{0,16},{16,0},{1,17},{17,1},{2,18},{18,2},{3,19},{19,3},{4,20},{20... | collective-permute-start | bytes 393224 | tf_op jit(solution)/shard_map/ppermute | solution.py:558
  56.5 20.9 %collective-permute-start.5 = (f32[4,128,256]{2,1,0:T(8,128)S(1)}, f32[4,128,256]{2,1,0:T(8,128)S(1)}, u32[]{:S(2)}, u32[]{:S(2)}) collective-permute-start(f32[4,128,256]{2,1,0:T(8,128)S(1)} %get-tuple-element.22.refs_2_.refs_4_.refs_1_.refs_3_), channel_id=1, source_target_pairs={{16,17},{17,18},{18,19},{1,0},{2,1},{3,2},{20,21},{21,22},{22,23},... | collective-permute-start | bytes 1572872 | tf_op jit(solution)/shard_map/ppermute | solution.py:567
  63.5 8.4 %collective-permute-start.4 = (f32[2,128,256]{2,1,0:T(8,128)S(1)}, f32[2,128,256]{2,1,0:T(8,128)S(1)}, u32[]{:S(2)}, u32[]{:S(2)}) collective-permute-start(f32[2,128,256]{2,1,0:T(8,128)S(1)} %get-tuple-element.24), channel_id=1, source_target_pairs={{0,16},{16,0},{1,17},{17,1},{2,18},{18,2},{3,19},{19,3},{4,20},{20... | collective-permute-start | bytes 786440 | tf_op jit(solution)/shard_map/ppermute | solution.py:558
  66.3 11.1 %collective-permute-start.6 = (f32[2,128,256]{2,1,0:T(8,128)S(1)}, f32[2,128,256]{2,1,0:T(8,128)S(1)}, u32[]{:S(2)}, u32[]{:S(2)}) collective-permute-start(f32[2,128,256]{2,1,0:T(8,128)S(1)} %collective-permute-done.3.refs_3_.refs_5_.refs_2_), channel_id=1, source_target_pairs={{0,1},{1,2},{2,3},{17,16},{18,17},{19,18},{4,5},{5,6},{6,7},{21,20... | collective-permute-start | bytes 786440 | tf_op jit(solution)/shard_map/ppermute | solution.py:567
  70.1 11.0 %collective-permute-start.7 = (f32[2,128,256]{2,1,0:T(8,128)S(1)}, f32[2,128,256]{2,1,0:T(8,128)S(1)}, u32[]{:S(2)}, u32[]{:S(2)}) collective-permute-start(f32[2,128,256]{2,1,0:T(8,128)S(1)} %pad_maximum_fusion), channel_id=1, source_target_pairs={{0,4},{4,8},{8,12},{12,0},{1,5},{5,9},{9,13},{13,1},{2,6},{6,10},{... | collective-permute-start | bytes 786440 | tf_op jit(solution)/shard_map/ppermute | solution.py:558
  70.2 10.9 %collective-permute-start.8 = (f32[2,128,256]{2,1,0:T(8,128)S(1)}, f32[2,128,256]{2,1,0:T(8,128)S(1)}, u32[]{:S(2)}, u32[]{:S(2)}) collective-permute-start(f32[2,128,256]{2,1,0:T(8,128)S(1)} %pad_maximum_fusion.1), channel_id=1, source_target_pairs={{0,12},{4,0},{8,4},{12,8},{1,13},{5,1},{9,5},{13,9},{2,14},{6,2},{... | collective-permute-start | bytes 786440 | tf_op jit(solution)/shard_map/ppermute | solution.py:558
  71.9 11.1 %collective-permute-start.9 = (f32[2,128,256]{2,1,0:T(8,128)S(1)}, f32[2,128,256]{2,1,0:T(8,128)S(1)}, u32[]{:S(2)}, u32[]{:S(2)}) collective-permute-start(f32[2,128,256]{2,1,0:T(8,128)S(1)} %collective-permute-done.4.refs_4_.refs_8_), channel_id=1, source_target_pairs={{0,1},{1,2},{2,3},{17,16},{18,17},{19,18},{4,5},{5,6},{6,7},{21,20... | collective-permute-start | bytes 786440 | tf_op jit(solution)/shard_map/ppermute | solution.py:567
  77.9 5.1 %collective-permute-start.13 = (f32[4,32,128]{2,1,0:T(8,128)S(1)}, f32[4,32,128]{2,1,0:T(8,128)S(1)}, u32[]{:S(2)}, u32[]{:S(2)}) collective-permute-start(f32[4,32,128]{2,1,0:T(8,128)S(1)} %get-tuple-element.27), channel_id=1, source_target_pairs={{0,4},{4,8},{8,12},{12,0},{1,5},{5,9},{9,13},{13,1},{2,6},{6,10},{... | collective-permute-start | bytes 196616 | tf_op jit(solution)/shard_map/ppermute | solution.py:558
  78.0 5.1 %collective-permute-start.14 = (f32[4,32,128]{2,1,0:T(8,128)S(1)}, f32[4,32,128]{2,1,0:T(8,128)S(1)}, u32[]{:S(2)}, u32[]{:S(2)}) collective-permute-start(f32[4,32,128]{2,1,0:T(8,128)S(1)} %get-tuple-element.28), channel_id=1, source_target_pairs={{0,12},{4,0},{8,4},{12,8},{1,13},{5,1},{9,5},{13,9},{2,14},{6,2},{... | collective-permute-start | bytes 196616 | tf_op jit(solution)/shard_map/ppermute | solution.py:558

commit v6 on v5

--- a/solution.py
+++ b/solution.py
@@ -40,17 +40,16 @@
 
 
 def mm3(a, b):
-    return dot(
-        jnp.concatenate([a[0], a[0], a[1]], axis=1),
-        jnp.concatenate([b[0], b[1], b[0]], axis=0),
-    )
+    n = a[0].shape[0]
+    both = dot(jnp.concatenate([a[0], a[1]], axis=0), b[0])
+    return both[:n] + (both[n:] + dot(a[0], b[1]))
 
 
 def mm5(a, b):
-    return dot(
-        jnp.concatenate([a[0], a[1], a[2], a[0], a[1]], axis=1),
-        jnp.concatenate([b[0], b[0], b[0], b[1], b[1]], axis=0),
-    )
+    n = a[0].shape[0]
+    three = dot(jnp.concatenate([a[0], a[1], a[2]], axis=0), b[0])
+    two = dot(jnp.concatenate([a[0], a[1]], axis=0), b[1])
+    return three[:n] + ((three[n : 2 * n] + two[:n]) + (three[2 * n :] + two[n:]))
 
 
 def mm1(a, b):

time: 85 us -> 84.9 us (level)
  no operation moved by 1% of the time
where the time goes in v6:
time: 84.9 us; the launch traced here: 84.6 us
  waiting for transfers between devices  35.8 us (42%)
  Pallas kernels  22.7 us (27%)
  starting transfers between devices  21.6 us (25%)
  local copies, waits for them, and re-layouts  3.42 us (4%)
  between operations  1.09 us (1%)
    ppermute x12, waiting for transfers between devices, shifted(): lax.ppermute(array, axis, [(i, (i + by) % size) for i in range(size)])  35.8 us
    pallas_call x1, Pallas kernels, solve(): pl.pallas_call(functools.partial(solve_kernel, points, bands), out_shape=...  15.4 us
    ppermute x12, starting transfers between devices, shifted(): lax.ppermute(array, axis, [(i, (i + by) % size) for i in range(size)])  13.2 us
    ppermute x3, starting transfers between devices, to_next_tile(): return lax.ppermute(array, ('mem', 'gy'), pairs)  8.46 us
    pallas_call x3, Pallas kernels, apply_terms(): pl.pallas_call(kernel, out_shape=jax.ShapeDtypeStruct((width, height, par...  4.71 us
    pallas_call x3, Pallas kernels, prepare(): pl.pallas_call(functools.partial(prepare_kernel, len(cells)), out_shape=[...  1.82 us
  transfers between devices with their start and end apart: 15, of which 4 were waited for; matrix products, arithmetic and copies ran while one was open for 3% of the time, Pallas kernels for 25%

profile of v6, /device:TPU:0, one launch (start us, length us, event | category | flops | bytes accessed | tf_op | source)
XLA Modules:
  0.0 84.6 jit_solution(13364692701676340319)
XLA Ops:
  0.0 1.2 %slice.40.refs_0_ = f32[20,64,128]{2,1,0:T(8,128)S(1)} slice(f32[32,64,128]{2,1,0:T(8,128)} %bitcast.15), slice={[0:20], [0:64], [0:128]} | slice | bytes 1310720 | tf_op jit(solution)/shard_map/slice | solution.py:608
  1.2 3.1 %collective-permute-start = (f32[20,64,128]{2,1,0:T(8,128)S(1)}, f32[20,64,128]{2,1,0:T(8,128)S(1)}, u32[]{:S(2)}, u32[]{:S(2)}) collective-permute-start(f32[20,64,128]{2,1,0:T(8,128)S(1)} %slice.40.refs_0_), channel_id=1, source_target_pairs={{0,16},{16,0},{1,17},{17,1},{2,18},{18,2},{3,19},{19,3},{4,20},{20... | collective-permute-start | bytes 1966088 | tf_op jit(solution)/shard_map/ppermute | solution.py:557
  4.3 1.0 %slice.41.refs_0_ = f32[12,64,128]{2,1,0:T(8,128)S(1)} slice(f32[32,64,128]{2,1,0:T(8,128)} %bitcast.16), slice={[20:32], [0:64], [0:128]} | slice | bytes 786432 | tf_op jit(solution)/shard_map/slice | solution.py:607
  5.3 0.1 collective-permute-start.1
  5.4 0.0 copy-start.4
  5.5 0.9 %copy.9 = f32[128,1,1,1024]{3,0,2,1:T(8,128)} copy(f32[128,1,1,1024]{3,2,1,0:T(1,128)S(1)} %constant_dynamic-slice_fusion.1) | data formatting | bytes 1048576 | tf_op jit(solution)/shard_map/optimization_barrier | solution.py:581
  6.4 2.0 %collective-permute-start.2 = (f32[128,1024]{1,0:T(8,128)}, f32[128,1024]{1,0:T(8,128)}, u32[]{:S(2)}, u32[]{:S(2)}) collective-permute-start(f32[128,1024]{1,0:T(8,128)} %bitcast.2), channel_id=1, source_target_pairs={{0,16},{16,0},{1,17},{17,1},{2,18},{18,2},{3,19},{19,3},{4,20},{20... | collective-permute-start | bytes 1572872 | tf_op jit(solution)/shard_map/ppermute | solution.py:557
  8.4 0.1 collective-permute-start.10
  8.6 0.4 collective-permute-start.11
  9.7 0.1 copy.11
  9.8 0.7 collective-permute-done.10
  10.5 28.3 %collective-permute-done.2.refs_0_ = f32[128,1024]{1,0:T(8,128)} collective-permute-done((f32[128,1024]{1,0:T(8,128)}, f32[128,1024]{1,0:T(8,128)}, u32[]{:S(2)}, u32[]{:S(2)}) %collective-permute-start.2) | collective-permute-done | bytes 524320 | tf_op jit(solution)/shard_map/ppermute | solution.py:557
  38.8 15.4 %solve.1 = (f32[4,128,256]{2,1,0:T(8,128)S(1)}, f32[2,128,256]{2,1,0:T(8,128)S(1)}, f32[2,128,256]{2,1,0:T(8,128)S(1)}) custom-call(s32[1]{0:T(128)} %bitcast.10.live_ref, f32[128,1024]{1,0:T(8,128)S(1)} %bitcast.11, f32[128,1024]{1,0:T(8,128)} %collective-permute-done.2.refs_0_, f32[1,1024]{1,0:T(1,128)S(1)} %bitcast.12, f32[1,1024]{1,0:T(1,128)S(1)} %bitcast.13, ...), custom_call_target="tpu_custom_call" | custom-call | flops 11140071424 | bytes 2097152 | tf_op jit(solution)/shard_map/solve/pallas_call | solution.py:179
  54.2 1.8 %collective-permute-start.3 = (f32[2,128,256]{2,1,0:T(8,128)S(1)}, f32[2,128,256]{2,1,0:T(8,128)S(1)}, u32[]{:S(2)}, u32[]{:S(2)}) collective-permute-start(f32[2,128,256]{2,1,0:T(8,128)S(1)} %get-tuple-element.23), channel_id=1, source_target_pairs={{0,16},{16,0},{1,17},{17,1},{2,18},{18,2},{3,19},{19,3},{4,20},{20... | collective-permute-start | bytes 786440 | tf_op jit(solution)/shard_map/ppermute | solution.py:557
  56.1 0.3 collective-permute-start.12
  56.4 1.3 %collective-permute-start.5 = (f32[4,128,256]{2,1,0:T(8,128)S(1)}, f32[4,128,256]{2,1,0:T(8,128)S(1)}, u32[]{:S(2)}, u32[]{:S(2)}) collective-permute-start(f32[4,128,256]{2,1,0:T(8,128)S(1)} %get-tuple-element.22.refs_2_.refs_4_.refs_1_.refs_3_), channel_id=1, source_target_pairs={{16,17},{17,18},{18,19},{1,0},{2,1},{3,2},{20,21},{21,22},{22,23},... | collective-permute-start | bytes 1572872 | tf_op jit(solution)/shard_map/ppermute | solution.py:566
  57.7 5.8 %collective-permute-done.3.refs_3_.refs_5_.refs_2_ = f32[2,128,256]{2,1,0:T(8,128)S(1)} collective-permute-done((f32[2,128,256]{2,1,0:T(8,128)S(1)}, f32[2,128,256]{2,1,0:T(8,128)S(1)}, u32[]{:S(2)}, u32[]{:S(2)}) %collective-permute-start.3) | collective-permute-done | bytes 262176 | tf_op jit(solution)/shard_map/ppermute | solution.py:557
  63.5 1.8 %collective-permute-start.4 = (f32[2,128,256]{2,1,0:T(8,128)S(1)}, f32[2,128,256]{2,1,0:T(8,128)S(1)}, u32[]{:S(2)}, u32[]{:S(2)}) collective-permute-start(f32[2,128,256]{2,1,0:T(8,128)S(1)} %get-tuple-element.24), channel_id=1, source_target_pairs={{0,16},{16,0},{1,17},{17,1},{2,18},{18,2},{3,19},{19,3},{4,20},{20... | collective-permute-start | bytes 786440 | tf_op jit(solution)/shard_map/ppermute | solution.py:557
  65.3 1.0 %collective-permute-done.12.refs_1_ = f32[8,32,128]{2,1,0:T(8,128)S(1)} collective-permute-done((f32[8,32,128]{2,1,0:T(8,128)S(1)}, f32[8,32,128]{2,1,0:T(8,128)S(1)}, u32[]{:S(2)}, u32[]{:S(2)}) %collective-permute-start.12) | collective-permute-done | bytes 131104 | tf_op jit(solution)/shard_map/ppermute | solution.py:557
  66.3 3.7 %collective-permute-start.6 = (f32[2,128,256]{2,1,0:T(8,128)S(1)}, f32[2,128,256]{2,1,0:T(8,128)S(1)}, u32[]{:S(2)}, u32[]{:S(2)}) collective-permute-start(f32[2,128,256]{2,1,0:T(8,128)S(1)} %collective-permute-done.3.refs_3_.refs_5_.refs_2_), channel_id=1, source_target_pairs={{0,1},{1,2},{2,3},{17,16},{18,17},{19,18},{4,5},{5,6},{6,7},{21,20... | collective-permute-start | bytes 786440 | tf_op jit(solution)/shard_map/ppermute | solution.py:566
  70.0 0.1 collective-permute-start.7
  70.1 1.7 %collective-permute-start.8 = (f32[2,128,256]{2,1,0:T(8,128)S(1)}, f32[2,128,256]{2,1,0:T(8,128)S(1)}, u32[]{:S(2)}, u32[]{:S(2)}) collective-permute-start(f32[2,128,256]{2,1,0:T(8,128)S(1)} %pad_maximum_fusion.1), channel_id=1, source_target_pairs={{0,12},{4,0},{8,4},{12,8},{1,13},{5,1},{9,5},{13,9},{2,14},{6,2},{... | collective-permute-start | bytes 786440 | tf_op jit(solution)/shard_map/ppermute | solution.py:557
  71.8 3.5 %collective-permute-start.9 = (f32[2,128,256]{2,1,0:T(8,128)S(1)}, f32[2,128,256]{2,1,0:T(8,128)S(1)}, u32[]{:S(2)}, u32[]{:S(2)}) collective-permute-start(f32[2,128,256]{2,1,0:T(8,128)S(1)} %collective-permute-done.4.refs_4_.refs_8_), channel_id=1, source_target_pairs={{0,1},{1,2},{2,3},{17,16},{18,17},{19,18},{4,5},{5,6},{6,7},{21,20... | collective-permute-start | bytes 786440 | tf_op jit(solution)/shard_map/ppermute | solution.py:566
  75.3 0.8 shard_map.68
  76.1 0.4 shard_map.65
  76.5 0.6 shard_map.64
  77.2 0.7 corners.1
  77.9 0.1 collective-permute-start.13
  77.9 1.7 %collective-permute-start.14 = (f32[4,32,128]{2,1,0:T(8,128)S(1)}, f32[4,32,128]{2,1,0:T(8,128)S(1)}, u32[]{:S(2)}, u32[]{:S(2)}) collective-permute-start(f32[4,32,128]{2,1,0:T(8,128)S(1)} %get-tuple-element.28), channel_id=1, source_target_pairs={{0,12},{4,0},{8,4},{12,8},{1,13},{5,1},{9,5},{13,9},{2,14},{6,2},{... | collective-permute-start | bytes 196616 | tf_op jit(solution)/shard_map/ppermute | solution.py:557
  79.7 1.3 %shard_map.66.refs_2_ = f32[20,64,128]{2,1,0:T(8,128)S(1)} custom-call(bf16[2,20,64,256]{3,2,1,0:T(8,128)(2,1)S(1)} %get-tuple-element.17.refs_0_, f32[20,64,128]{2,1,0:T(8,128)S(1)} %get-tuple-element.19.refs_1_, f32[4,128,256]{2,1,0:T(8,128)S(1)} %get-tuple-element.22.refs_2_.refs_4_.refs_1_.refs_3_, ...), custom_call_target="tpu_custom_call" | custom-call | flops 754974720 | bytes 3014656 | tf_op jit(solution)/shard_map/pallas_call | solution.py:539
  81.0 1.9 %shard_map.67.refs_2_ = f32[32,64,128]{2,1,0:T(8,128)S(1)} custom-call(bf16[2,20,64,256]{3,2,1,0:T(8,128)(2,1)S(1)} %get-tuple-element.17.refs_0_, bf16[2,12,64,256]{3,2,1,0:T(8,128)(2,1)S(1)} %get-tuple-element.18.refs_1_, f32[20,64,128]{2,1,0:T(8,128)S(1)} %shard_map.66.refs_2_, f32[12,64,128]{2,1,0:T(8,128)S(1)} %get-tuple-element.25.refs_3_, ...), custom_call_target="tpu_custom_call" | custom-call | flops 402653184 | bytes 5505024 | tf_op jit(solution)/shard_map/pallas_call | solution.py:539
  83.0 1.5 %shard_map.69 = f32[32,64,128]{2,1,0:T(8,128)} custom-call(bf16[2,20,64,256]{3,2,1,0:T(8,128)(2,1)S(1)} %get-tuple-element.17.refs_0_, bf16[2,12,64,256]{3,2,1,0:T(8,128)(2,1)S(1)} %get-tuple-element.18.refs_1_, f32[32,64,128]{2,1,0:T(8,128)S(1)} %shard_map.67.refs_2_, f32[4,128,256]{2,1,0:T(8,128)S(1)} %get-tuple-element.22.refs_2_.refs_4_.refs_1_.refs_3_, ...), custom_call_target="tpu_custom_call" | custom-call | flops 201326592 | bytes 4849664 | tf_op jit(solution)/shard_map/pallas_call | solution.py:539
  (30 shorter events, 0.3 us)
Async XLA Ops:
  0.0 5.4 %copy-start = (f32[128,1,1,2048]{3,2,1,0:T(1,128)S(1)}, f32[128,1,1,2048]{3,2,1,0:T(1,128)}, u32[]{:S(2)}) copy-start(f32[128,1,1,2048]{3,2,1,0:T(1,128)} %param.7) | copy-start | bytes 3145732
  1.2 68.9 %collective-permute-start = (f32[20,64,128]{2,1,0:T(8,128)S(1)}, f32[20,64,128]{2,1,0:T(8,128)S(1)}, u32[]{:S(2)}, u32[]{:S(2)}) collective-permute-start(f32[20,64,128]{2,1,0:T(8,128)S(1)} %slice.40.refs_0_), channel_id=1, source_target_pairs={{0,16},{16,0},{1,17},{17,1},{2,18},{18,2},{3,19},{19,3},{4,20},{20... | collective-permute-start | bytes 1966088 | tf_op jit(solution)/shard_map/ppermute | solution.py:557
  5.3 64.7 %collective-permute-start.1 = (f32[12,64,128]{2,1,0:T(8,128)S(1)}, f32[12,64,128]{2,1,0:T(8,128)S(1)}, u32[]{:S(2)}, u32[]{:S(2)}) collective-permute-start(f32[12,64,128]{2,1,0:T(8,128)S(1)} %slice.41.refs_0_), channel_id=1, source_target_pairs={{0,16},{16,0},{1,17},{17,1},{2,18},{18,2},{3,19},{19,3},{4,20},{20... | collective-permute-start | bytes 1179656 | tf_op jit(solution)/shard_map/ppermute | solution.py:557
  5.4 2.9 %copy-start.4 = (f32[128,32,64]{0,2,1:T(8,128)S(1)}, f32[128,32,64]{0,2,1:T(8,128)}, u32[]{:S(2)}) copy-start(f32[128,32,64]{0,2,1:T(8,128)} %param.6) | copy-start | bytes 3145732
  6.4 32.4 %collective-permute-start.2 = (f32[128,1024]{1,0:T(8,128)}, f32[128,1024]{1,0:T(8,128)}, u32[]{:S(2)}, u32[]{:S(2)}) collective-permute-start(f32[128,1024]{1,0:T(8,128)} %bitcast.2), channel_id=1, source_target_pairs={{0,16},{16,0},{1,17},{17,1},{2,18},{18,2},{3,19},{19,3},{4,20},{20... | collective-permute-start | bytes 1572872 | tf_op jit(solution)/shard_map/ppermute | solution.py:557
  8.4 30.4 %copy-start.1 = (f32[1,1,1,1024]{3,2,1,0:T(1,128)S(1)}, f32[1,1,1,1024]{3,2,1,0:T(1,128)}, u32[]{:S(2)}) copy-start(f32[1,1,1,1024]{3,2,1,0:T(1,128)} %param.8) | copy-start | bytes 12292
  8.4 30.4 %copy-start.2 = (f32[1,1,1,1024]{3,2,1,0:T(1,128)S(1)}, f32[1,1,1,1024]{3,2,1,0:T(1,128)}, u32[]{:S(2)}) copy-start(f32[1,1,1,1024]{3,2,1,0:T(1,128)} %param.9) | copy-start | bytes 12292
  8.4 30.4 %copy-start.3 = (s32[1,1,1,1024]{3,2,1,0:T(1,128)S(1)}, s32[1,1,1,1024]{3,2,1,0:T(1,128)}, u32[]{:S(2)}) copy-start(s32[1,1,1,1024]{3,2,1,0:T(1,128)} %param.10) | copy-start | bytes 12292
  8.4 2.0 %collective-permute-start.10 = (f32[4,32,128]{2,1,0:T(8,128)S(1)}, f32[4,32,128]{2,1,0:T(8,128)S(1)}, u32[]{:S(2)}, u32[]{:S(2)}) collective-permute-start(f32[4,32,128]{2,1,0:T(8,128)S(1)} %get-tuple-element.32), channel_id=1, source_target_pairs={{0,12},{4,0},{8,4},{12,8},{1,13},{5,1},{9,5},{13,9},{2,14},{6,2},{... | collective-permute-start | bytes 196616 | tf_op jit(solution)/shard_map/ppermute | solution.py:557
  8.6 47.5 %collective-permute-start.11 = (f32[4,32,128]{2,1,0:T(8,128)S(1)}, f32[4,32,128]{2,1,0:T(8,128)S(1)}, u32[]{:S(2)}, u32[]{:S(2)}) collective-permute-start(f32[4,32,128]{2,1,0:T(8,128)S(1)} %get-tuple-element.31), channel_id=1, source_target_pairs={{0,4},{4,8},{8,12},{12,0},{1,5},{5,9},{9,13},{13,1},{2,6},{6,10},{... | collective-permute-start | bytes 196616 | tf_op jit(solution)/shard_map/ppermute | solution.py:557
  54.2 9.2 %collective-permute-start.3 = (f32[2,128,256]{2,1,0:T(8,128)S(1)}, f32[2,128,256]{2,1,0:T(8,128)S(1)}, u32[]{:S(2)}, u32[]{:S(2)}) collective-permute-start(f32[2,128,256]{2,1,0:T(8,128)S(1)} %get-tuple-element.23), channel_id=1, source_target_pairs={{0,16},{16,0},{1,17},{17,1},{2,18},{18,2},{3,19},{19,3},{4,20},{20... | collective-permute-start | bytes 786440 | tf_op jit(solution)/shard_map/ppermute | solution.py:557
  56.1 10.2 %collective-permute-start.12 = (f32[8,32,128]{2,1,0:T(8,128)S(1)}, f32[8,32,128]{2,1,0:T(8,128)S(1)}, u32[]{:S(2)}, u32[]{:S(2)}) collective-permute-start(f32[8,32,128]{2,1,0:T(8,128)S(1)} %constant_dynamic-update-slice_fusion.refs_0_), channel_id=1, source_target_pairs={{0,16},{16,0},{1,17},{17,1},{2,18},{18,2},{3,19},{19,3},{4,20},{20... | collective-permute-start | bytes 393224 | tf_op jit(solution)/shard_map/ppermute | solution.py:557
  56.4 20.8 %collective-permute-start.5 = (f32[4,128,256]{2,1,0:T(8,128)S(1)}, f32[4,128,256]{2,1,0:T(8,128)S(1)}, u32[]{:S(2)}, u32[]{:S(2)}) collective-permute-start(f32[4,128,256]{2,1,0:T(8,128)S(1)} %get-tuple-element.22.refs_2_.refs_4_.refs_1_.refs_3_), channel_id=1, source_target_pairs={{16,17},{17,18},{18,19},{1,0},{2,1},{3,2},{20,21},{21,22},{22,23},... | collective-permute-start | bytes 1572872 | tf_op jit(solution)/shard_map/ppermute | solution.py:566
  63.5 8.4 %collective-permute-start.4 = (f32[2,128,256]{2,1,0:T(8,128)S(1)}, f32[2,128,256]{2,1,0:T(8,128)S(1)}, u32[]{:S(2)}, u32[]{:S(2)}) collective-permute-start(f32[2,128,256]{2,1,0:T(8,128)S(1)} %get-tuple-element.24), channel_id=1, source_target_pairs={{0,16},{16,0},{1,17},{17,1},{2,18},{18,2},{3,19},{19,3},{4,20},{20... | collective-permute-start | bytes 786440 | tf_op jit(solution)/shard_map/ppermute | solution.py:557
  66.3 10.9 %collective-permute-start.6 = (f32[2,128,256]{2,1,0:T(8,128)S(1)}, f32[2,128,256]{2,1,0:T(8,128)S(1)}, u32[]{:S(2)}, u32[]{:S(2)}) collective-permute-start(f32[2,128,256]{2,1,0:T(8,128)S(1)} %collective-permute-done.3.refs_3_.refs_5_.refs_2_), channel_id=1, source_target_pairs={{0,1},{1,2},{2,3},{17,16},{18,17},{19,18},{4,5},{5,6},{6,7},{21,20... | collective-permute-start | bytes 786440 | tf_op jit(solution)/shard_map/ppermute | solution.py:566
  70.0 11.0 %collective-permute-start.7 = (f32[2,128,256]{2,1,0:T(8,128)S(1)}, f32[2,128,256]{2,1,0:T(8,128)S(1)}, u32[]{:S(2)}, u32[]{:S(2)}) collective-permute-start(f32[2,128,256]{2,1,0:T(8,128)S(1)} %pad_maximum_fusion), channel_id=1, source_target_pairs={{0,4},{4,8},{8,12},{12,0},{1,5},{5,9},{9,13},{13,1},{2,6},{6,10},{... | collective-permute-start | bytes 786440 | tf_op jit(solution)/shard_map/ppermute | solution.py:557
  70.1 10.9 %collective-permute-start.8 = (f32[2,128,256]{2,1,0:T(8,128)S(1)}, f32[2,128,256]{2,1,0:T(8,128)S(1)}, u32[]{:S(2)}, u32[]{:S(2)}) collective-permute-start(f32[2,128,256]{2,1,0:T(8,128)S(1)} %pad_maximum_fusion.1), channel_id=1, source_target_pairs={{0,12},{4,0},{8,4},{12,8},{1,13},{5,1},{9,5},{13,9},{2,14},{6,2},{... | collective-permute-start | bytes 786440 | tf_op jit(solution)/shard_map/ppermute | solution.py:557
  71.8 11.1 %collective-permute-start.9 = (f32[2,128,256]{2,1,0:T(8,128)S(1)}, f32[2,128,256]{2,1,0:T(8,128)S(1)}, u32[]{:S(2)}, u32[]{:S(2)}) collective-permute-start(f32[2,128,256]{2,1,0:T(8,128)S(1)} %collective-permute-done.4.refs_4_.refs_8_), channel_id=1, source_target_pairs={{0,1},{1,2},{2,3},{17,16},{18,17},{19,18},{4,5},{5,6},{6,7},{21,20... | collective-permute-start | bytes 786440 | tf_op jit(solution)/shard_map/ppermute | solution.py:566
  77.9 5.1 %collective-permute-start.13 = (f32[4,32,128]{2,1,0:T(8,128)S(1)}, f32[4,32,128]{2,1,0:T(8,128)S(1)}, u32[]{:S(2)}, u32[]{:S(2)}) collective-permute-start(f32[4,32,128]{2,1,0:T(8,128)S(1)} %get-tuple-element.27), channel_id=1, source_target_pairs={{0,4},{4,8},{8,12},{12,0},{1,5},{5,9},{9,13},{13,1},{2,6},{6,10},{... | collective-permute-start | bytes 196616 | tf_op jit(solution)/shard_map/ppermute | solution.py:557
  77.9 5.0 %collective-permute-start.14 = (f32[4,32,128]{2,1,0:T(8,128)S(1)}, f32[4,32,128]{2,1,0:T(8,128)S(1)}, u32[]{:S(2)}, u32[]{:S(2)}) collective-permute-start(f32[4,32,128]{2,1,0:T(8,128)S(1)} %get-tuple-element.28), channel_id=1, source_target_pairs={{0,12},{4,0},{8,4},{12,8},{1,13},{5,1},{9,5},{13,9},{2,14},{6,2},{... | collective-permute-start | bytes 196616 | tf_op jit(solution)/shard_map/ppermute | solution.py:557
